TPU v7x, 32 devices: a whole 2x2x4 slice. The times are simulated.
32 devices in a mesh: mesh: 8 (over z, y), harm: 4 (over x, core).
Axes of the slice: x: 2, y: 2, z: 4, core: 2. Of those that a mesh axis runs over, the one named last changes fastest.
Arguments:
- displacement: float32 [32, 3, 16, 32, 256], P('harm', None, 'mesh'), may hold values from -3 to 3
- direction: float32 [32, 3, 16, 32, 256], P('harm', None, 'mesh'), may hold values from -6 to 6
- forcing: float32 [32, 3, 16, 32, 256], P('harm', None, 'mesh'), may hold values from -6 to 6
- stiffness: float32 [16, 32, 256], P('mesh'), may hold values from 0.5 to 3
- lumped_mass: float32 [16, 32, 256], P('mesh'), may hold values from 0.5 to 2
- face_cells: int32 [8192], P('mesh'), may hold values from 0 to 16383, as said below
- send_rows: int32 [8192], P('mesh'), may hold values from 0 to 1024, as said below
- pair_rows: int32 [2, 2048], P(None, 'mesh'), may hold values from 0 to 1023, as said below
- status: int32 [64, 2048], P('harm', 'mesh'), may hold values 0 or 1
- crack_gap: float32 [2048], P('mesh'), may hold values from -1 to 1
Outputs:
- residual: float32 [32, 3, 16, 32, 256], P('harm', None, 'mesh')
- jacobian_product: float32 [32, 3, 16, 32, 256], P('harm', None, 'mesh')
Inputs may be any that keep to these rules, and one draw needn't show every extreme that they name: `face_cells`: each sector's 1024 entries are distinct cells of its block. `send_rows`: the crack crosses a contiguous arc of 4 sectors that passes over the cycle's seam (it holds sectors 8 - 1 and 0). Each sector of the arc sends every one of its 1024 face rows in exactly one slot, so each owner gets exactly 128 rows from each sector of the arc; the other sectors' slots all hold 1024, meaning empty. `pair_rows`: each owner's 2 * 256 entries are exactly the slots it receives from the sectors of the arc, each once.
All inputs are finite; a program needn't handle non-finite values. No bound on the sum of `status` on one device may be relied on, other than what follows from the above.
Results may differ from a plain program's by a relative error of at most 0.00005.
Values sent between devices are 32-bit elements; how exact they have to be, the bound alone decides.
No kernel may reach another device: no remote copies, remote signals or barrier semaphores. Data moves between devices by JAX's collectives and lax.ppermute only.
A program may use at most 192 MiB of HBM per device.

v0:
```python
import math

import jax
import jax.numpy as jnp
import numpy as np
from jax import lax
from jax.experimental import pallas as pl
from jax.experimental.pallas import tpu as pltpu
from jax.sharding import PartitionSpec as P

HARM = 16
TIME = 64
LANES = 128

damping_ratio = 0.3
normal_penalty = 2.0
shear_penalty = 1.0

CHUNKS = ((0, 1), (1, 4), (4, 7), (7, 8))
VMEM = 56 * 1024 * 1024


def split2(value):
    high = value.astype(jnp.bfloat16)
    low = (value - high.astype(jnp.float32)).astype(jnp.bfloat16)
    return high, low


def split3(value):
    high = value.astype(jnp.bfloat16)
    rest = value - high.astype(jnp.float32)
    mid = rest.astype(jnp.bfloat16)
    low = (rest - mid.astype(jnp.float32)).astype(jnp.bfloat16)
    return high, mid, low


def slot_cells(cells_ref, send_ref):
    rows = cells_ref.shape[0]
    send = send_ref[...]
    high = send // LANES
    low = send % LANES
    found = jnp.zeros_like(send)
    for row in range(rows):
        table = jnp.broadcast_to(cells_ref[row : row + 1, :], send.shape)
        picked = jnp.take_along_axis(table, low, axis=1)
        found = jnp.where(high == row, picked, found)
    return jnp.concatenate([found[row : row + 1, :] for row in range(rows)], axis=1)


def one_hot_rows(index_row, count, kind):
    shape = (count, index_row.shape[1])
    hit = lax.broadcasted_iota(jnp.int32, shape, 0) == index_row
    return jnp.where(hit, 1.0, 0.0).astype(kind)


def gather_kernel(cells_ref, send_ref, x_ref, y_ref, out_ref, cell_ref, low_ref):
    comp = pl.program_id(0)
    coefs, _, rows, axial = x_ref.shape
    slots = cell_ref.shape[1]

    @pl.when(comp == 0)
    def _():
        cell = slot_cells(cells_ref, send_ref)
        cell_ref[...] = cell
        hot = one_hot_rows(cell % axial, axial, jnp.bfloat16)
        low_ref[0:axial, :] = hot
        low_ref[axial : 2 * axial, :] = hot

    row_of = cell_ref[...] // axial
    mask = lax.broadcasted_iota(jnp.int32, (rows, slots), 0) == row_of
    for field, ref in enumerate((x_ref, y_ref)):
        flat = ref[...].reshape(coefs * rows, axial)
        high, low = split2(flat)
        picked = jnp.dot(
            jnp.concatenate([high, low], axis=1),
            low_ref[...],
            preferred_element_type=jnp.float32,
        ).reshape(coefs, rows, slots)
        values = jnp.sum(jnp.where(mask[None], picked, 0.0), axis=1)
        block = field * 3 + comp
        if len(out_ref.shape) == 4:
            cap = out_ref.shape[3]
            for owner in range(out_ref.shape[0]):
                out_ref[owner, block] = values[:, owner * cap : (owner + 1) * cap]
        else:
            out_ref[block] = values


def pair_table(pairs_ref, slots):
    count = pairs_ref.shape[1]
    place = lax.broadcasted_iota(jnp.int32, (slots, count), 0)
    side_a = jnp.where(place == pairs_ref[0:1, :], 1.0, 0.0)
    side_b = jnp.where(place == pairs_ref[1:2, :], 1.0, 0.0)
    return (side_a - side_b).astype(jnp.bfloat16)


def by_slot(ref, block):
    if len(ref.shape) == 3:
        return ref[block]
    return jnp.concatenate([ref[owner, block] for owner in range(ref.shape[0])], axis=1)


def opening_kernel(pairs_ref, status_ref, arrived_ref, out_ref):
    arrived = jnp.concatenate([by_slot(arrived_ref, block) for block in range(6)], axis=0)
    values, slots = arrived.shape
    table = pair_table(pairs_ref, slots)
    total = None
    for part in split3(arrived):
        term = jnp.dot(part, table, preferred_element_type=jnp.float32)
        total = term if total is None else total + term
    out_ref[0:values, :] = total
    out_ref[values:, :] = status_ref[...].astype(jnp.float32)


def force_kernel(place_ref, pairs_ref, gap_ref, table_ref, back_ref, all_ref, out_ref):
    harm_count, total_rows, pairs = all_ref.shape
    coefs = table_ref.shape[1] // harm_count
    values = 6 * coefs
    back = back_ref[place_ref[0]]
    closed = jnp.concatenate([all_ref[g, values:total_rows, :] for g in range(harm_count)], axis=0)
    coef_rows = []
    for block in range(6):
        spread = jnp.concatenate(
            [all_ref[g, block * coefs : (block + 1) * coefs, :] for g in range(harm_count)], axis=0
        )
        opening = jnp.dot(
            table_ref[...], spread, precision=lax.Precision.HIGHEST, preferred_element_type=jnp.float32
        )
        if block == 0:
            opening = opening + gap_ref[...]
        kappa = normal_penalty if block % 3 == 0 else shear_penalty
        force = closed * kappa * opening
        coef_rows.append(
            jnp.dot(back, force, precision=lax.Precision.HIGHEST, preferred_element_type=jnp.float32)
        )
    coef_force = jnp.concatenate(coef_rows, axis=0)
    direct = len(out_ref.shape) == 4
    slots = out_ref.shape[0] * out_ref.shape[3] if direct else out_ref.shape[2]
    table = pair_table(pairs_ref, slots)
    total = None
    for part in split3(coef_force):
        term = lax.dot_general(
            part, table, (((1,), (1,)), ((), ())), preferred_element_type=jnp.float32
        )
        total = term if total is None else total + term
    for block in range(6):
        part = total[block * coefs : (block + 1) * coefs]
        if direct:
            cap = out_ref.shape[3]
            for owner in range(out_ref.shape[0]):
                out_ref[owner, block] = part[:, owner * cap : (owner + 1) * cap]
        else:
            out_ref[block] = part


def local_kernel(place_ref, stiff_ref, mass_ref, x_ref, y_ref, forcing_ref, res_ref, jac_ref):
    _, comps, rows, axial = x_ref.shape
    layer = rows // 2
    harmonic = place_ref[0] * pl.num_programs(0) + pl.program_id(0) + 1
    frequency = harmonic.astype(jnp.float32) * (1.5 / HARM)
    mass = mass_ref[...]
    diagonal = 6.0 + stiff_ref[...] - (frequency * frequency) * mass
    turn = (frequency * damping_ratio) * mass
    row = lax.broadcasted_iota(jnp.int32, (rows, axial), 0) % layer
    column = lax.broadcasted_iota(jnp.int32, (rows, axial), 1)
    for ref, out_ref, forced in ((x_ref, res_ref, True), (y_ref, jac_ref, False)):
        for comp in range(comps):
            cosine = ref[0, comp]
            sine = ref[1, comp]
            for part, value, turned in ((0, cosine, sine), (1, sine, -cosine)):
                near = jnp.where(row == 0, 0.0, jnp.roll(value, 1, axis=0))
                near = near + jnp.where(row == layer - 1, 0.0, jnp.roll(value, -1, axis=0))
                near = near + jnp.where(column == 0, 0.0, pltpu.roll(value, 1, axis=1))
                near = near + jnp.where(column == axial - 1, 0.0, pltpu.roll(value, axial - 1, axis=1))
                near = near + jnp.concatenate([value[layer:], value[:layer]], axis=0)
                result = diagonal * value + turn * turned - near
                if forced:
                    result = result - forcing_ref[part, comp]
                out_ref[part, comp] = result


def scatter_kernel(cells_ref, send_ref, back_ref, *refs, spans):
    count = len(spans)
    halos = refs[: 4 * count]
    res_in, jac_in, res_ref, jac_ref, cell_ref, low_ref = refs[4 * count :]
    comp = pl.program_id(0)
    coefs, _, rows, axial = res_ref.shape
    slots = cell_ref.shape[1]
    layer = rows // 2

    @pl.when(comp == 0)
    def _():
        cell = slot_cells(cells_ref, send_ref)
        cell_ref[...] = cell
        low_ref[...] = one_hot_rows(cell % axial, axial, jnp.bfloat16)

    row_of = cell_ref[...] // axial
    mask = lax.broadcasted_iota(jnp.int32, (rows, slots), 0) == row_of
    for field, (in_ref, out_ref) in enumerate(((res_in, res_ref), (jac_in, jac_ref))):
        force = by_slot(back_ref, field * 3 + comp)
        total = None
        for part in split2(force):
            wide = part.astype(jnp.float32)
            spread = jnp.where(mask[None], wide[:, None, :], 0.0).astype(jnp.bfloat16)
            term = lax.dot_general(
                spread.reshape(coefs * rows, slots),
                low_ref[...],
                (((1,), (1,)), ((), ())),
                preferred_element_type=jnp.float32,
            )
            total = term if total is None else total + term
        total = in_ref[...].reshape(coefs, rows, axial) + total.reshape(coefs, rows, axial)
        out_ref[...] = total.reshape(coefs, 1, rows, axial)
        for index, (first, last) in enumerate(spans):
            below, above = halos[4 * index + 2 * field : 4 * index + 2 * field + 2]
            out_ref[first:last, 0, 0:layer, :] = total[first:last, 0:layer] - below[:, 0]
            out_ref[first:last, 0, layer:rows, :] = total[first:last, layer:rows] - above[:, 0]


def tail_kernel(res_in, jac_in, *refs):
    res_ref, jac_ref = refs[-2:]
    layer = res_ref.shape[2] // 2
    for field, (in_ref, out_ref) in enumerate(((res_in, res_ref), (jac_in, jac_ref))):
        below, above = refs[2 * field : 2 * field + 2]
        out_ref[:, :, 0:layer, :] = in_ref[:, :, 0:layer, :] - below[...]
        out_ref[:, :, layer:, :] = in_ref[:, :, layer:, :] - above[...]


def transform_table(time_count, coef_count):
    sample = np.arange(time_count)[:, None]
    coef = np.arange(coef_count)[None, :]
    angles = ((coef // 2 + 1) * sample % time_count) * (2.0 * math.pi / time_count)
    return np.where(coef % 2 == 0, np.cos(angles), np.sin(angles)).astype(np.float32)


def params(*semantics):
    return pltpu.CompilerParams(vmem_limit_bytes=VMEM, dimension_semantics=semantics or None)


def on_device(
    displacement,
    direction,
    forcing,
    stiffness,
    lumped_mass,
    face_cells,
    send_rows,
    pair_rows,
    status,
    crack_gap,
):
    coefs, comps, layers, radial, axial = displacement.shape
    rows = layers * radial
    slots = face_cells.shape[0]
    pairs = pair_rows.shape[1]
    owners = lax.axis_size("mesh")
    cap = slots // owners
    direct = cap % LANES == 0
    harm_count = lax.axis_size("harm")
    harm_index = lax.axis_index("harm")
    coef_total = coefs * harm_count
    place = jnp.reshape(harm_index, (1,)).astype(jnp.int32)
    f32 = jnp.float32
    values = 2 * comps * coefs
    wire = (owners, 6, coefs, cap) if direct else (6, coefs, slots)

    forward = [(i, (i + 1) % owners) for i in range(owners)]
    backward = [(target, source) for source, target in forward]

    def halo(first, last):
        pieces = []
        for field in (displacement, direction):
            part = field[first:last]
            pieces.append(lax.ppermute(part[:, :, layers - 1], "mesh", forward))
            pieces.append(lax.ppermute(part[:, :, 0], "mesh", backward))
        return pieces

    ends = sorted({a * coefs // 8 for span in CHUNKS for a in span})
    spans = list(zip(ends[:-1], ends[1:]))
    pieces = [halo(*span) for span in spans]

    x = displacement.reshape(coefs, comps, rows, axial)
    y = direction.reshape(coefs, comps, rows, axial)
    cells = face_cells.reshape(slots // LANES, LANES)
    send = send_rows.reshape(slots // LANES, LANES)
    whole = lambda shape: pl.BlockSpec(shape, lambda *_: (0,) * len(shape))
    scalar = pl.BlockSpec(memory_space=pltpu.SMEM)
    per_comp = pl.BlockSpec((coefs, 1, rows, axial), lambda comp: (0, comp, 0, 0))

    outgoing = pl.pallas_call(
        gather_kernel,
        grid=(comps,),
        in_specs=[whole(cells.shape), whole(send.shape), per_comp, per_comp],
        out_specs=whole(wire),
        out_shape=jax.ShapeDtypeStruct(wire, f32),
        scratch_shapes=[
            pltpu.VMEM((1, slots), jnp.int32),
            pltpu.VMEM((2 * axial, slots), jnp.bfloat16),
        ],
        compiler_params=params("arbitrary"),
        name="face_gather",
    )(cells, send, x, y)

    def exchange(block):
        if not direct:
            block = block.reshape(values, owners, cap).transpose(1, 0, 2)
        block = lax.all_to_all(block, "mesh", split_axis=0, concat_axis=0, tiled=True)
        if not direct:
            block = block.transpose(1, 0, 2).reshape(wire)
        return block

    arrived = exchange(outgoing)
    own_opening = pl.pallas_call(
        opening_kernel,
        in_specs=[whole(pair_rows.shape), whole(status.shape), whole(wire)],
        out_specs=whole((values + status.shape[0], pairs)),
        out_shape=jax.ShapeDtypeStruct((values + status.shape[0], pairs), f32),
        compiler_params=params(),
        name="pair_difference",
    )(pair_rows, status, arrived)
    everything = lax.all_gather(own_opening, "harm")
    table = transform_table(TIME, coef_total)
    back = ((2.0 / TIME) * table.T).reshape(harm_count, coefs, TIME)
    slot_force = pl.pallas_call(
        force_kernel,
        in_specs=[
            scalar,
            whole(pair_rows.shape),
            whole((1, pairs)),
            whole(table.shape),
            whole(back.shape),
            whole(everything.shape),
        ],
        out_specs=whole(wire),
        out_shape=jax.ShapeDtypeStruct(wire, f32),
        compiler_params=params(),
        name="pair_force",
    )(place, pair_rows, crack_gap.reshape(1, pairs), jnp.asarray(table), jnp.asarray(back), everything)
    returned = exchange(slot_force)

    per_harmonic = pl.BlockSpec((2, comps, rows, axial), lambda i: (i, 0, 0, 0))
    flat = jax.ShapeDtypeStruct(x.shape, f32)
    residual, product = pl.pallas_call(
        local_kernel,
        grid=(coefs // 2,),
        in_specs=[scalar, whole((rows, axial)), whole((rows, axial))] + [per_harmonic] * 3,
        out_specs=[per_harmonic] * 2,
        out_shape=[flat, flat],
        compiler_params=params("arbitrary"),
        name="local_terms",
    )(
        place,
        stiffness.reshape(rows, axial),
        lumped_mass.reshape(rows, axial),
        x,
        y,
        forcing.reshape(x.shape),
    )

    early, late = (spans[:-2], spans[-2:])
    near = [piece for chunk in pieces[: len(early)] for piece in chunk]
    near_specs = [
        pl.BlockSpec((last - first, 1, radial, axial), lambda comp: (0, comp, 0, 0))
        for first, last in early
        for _ in range(4)
    ]
    fixed = 3 + len(near)
    residual, product = pl.pallas_call(
        lambda *refs: scatter_kernel(*refs, spans=early),
        grid=(comps,),
        in_specs=[whole(cells.shape), whole(send.shape), whole(wire)] + near_specs + [per_comp] * 2,
        out_specs=[per_comp] * 2,
        out_shape=[flat, flat],
        input_output_aliases={fixed: 0, fixed + 1: 1},
        scratch_shapes=[
            pltpu.VMEM((1, slots), jnp.int32),
            pltpu.VMEM((axial, slots), jnp.bfloat16),
        ],
        compiler_params=params("arbitrary"),
        name="face_scatter",
    )(cells, send, returned, *near, residual, product)

    for (first, last), chunk in zip(late, pieces[len(early) :]):
        mine = pl.BlockSpec((1, comps, rows, axial), lambda i, first=first: (first + i, 0, 0, 0))
        edge = pl.BlockSpec((1, comps, radial, axial), lambda i: (i, 0, 0, 0))
        residual, product = pl.pallas_call(
            tail_kernel,
            grid=(last - first,),
            in_specs=[mine] * 2 + [edge] * 4,
            out_specs=[mine] * 2,
            out_shape=[flat, flat],
            input_output_aliases={0: 0, 1: 1},
            compiler_params=params("arbitrary"),
            name="edge_terms",
        )(residual, product, *chunk)
    return residual.reshape(displacement.shape), product.reshape(displacement.shape)


def solution(mesh):
    placed = (
        P("harm", None, "mesh", None, None),
        P("harm", None, "mesh", None, None),
        P("harm", None, "mesh", None, None),
        P("mesh", None, None),
        P("mesh", None, None),
        P("mesh"),
        P("mesh"),
        P(None, "mesh"),
        P("harm", "mesh"),
        P("mesh"),
    )
    return jax.shard_map(
        on_device,
        mesh=mesh,
        in_specs=placed,
        out_specs=(P("harm", None, "mesh", None, None), P("harm", None, "mesh", None, None)),
        check_vma=False,
    )
```

profile of v0, /device:TPU:4, one launch (start us, length us, event | category | flops | bytes accessed | tf_op | source)
XLA Modules:
  0.0 101.4 jit_solution(4128969286468050489)
XLA Ops:
  0.6 6.3 %face_gather.1 = f32[8,6,8,128]{3,2,1,0:T(8,128)} custom-call(s32[8,128]{1,0:T(8,128)} %bitcast.86, s32[8,128]{1,0:T(8,128)} %bitcast.88, f32[8,3,64,256]{3,2,1,0:T(8,128)} %bitcast.76, f32[8,3,64,256]{3,2,1,0:T(8,128)} %bitcast.78), custom_call_target="tpu_custom_call" | custom-call | tf_op jit(solution)/shard_map/face_gather/pallas_call | solution.py:290
  6.9 6.3 %all-to-all-start = ((f32[8,6,8,128]{3,2,1,0:T(8,128)}), f32[8,6,8,128]{3,2,1,0:T(8,128)S(1)}, u32[]{:S(2)}, u32[]{:S(2)}) async-start(f32[8,6,8,128]{3,2,1,0:T(8,128)} %face_gather.1), calls=%async_computation | async-start | bytes 393216 | tf_op jit(solution)/shard_map/all_to_all | solution.py:307
  13.2 0.7 slice_bitcast_fusion.10
  14.0 2.9 %collective-permute-start = (f32[1,3,32,256]{3,2,1,0:T(8,128)S(1)}, f32[1,3,32,256]{3,2,1,0:T(8,128)S(1)}, u32[]{:S(2)}, u32[]{:S(2)}) collective-permute-start(f32[1,3,32,256]{3,2,1,0:T(8,128)S(1)} %get-tuple-element.24), channel_id=1, source_target_pairs={{0,4},{4,8},{8,12},{12,16},{16,20},{20,24},{24,28},{28,0},{1,5},{5... | collective-permute-start | bytes 294920 | tf_op jit(solution)/shard_map/ppermute | solution.py:274
  16.9 0.8 slice_bitcast_fusion.2
  17.7 1.8 %collective-permute-start.9 = (f32[3,3,32,256]{3,2,1,0:T(8,128)S(1)}, f32[3,3,32,256]{3,2,1,0:T(8,128)S(1)}, u32[]{:S(2)}, u32[]{:S(2)}) collective-permute-start(f32[3,3,32,256]{3,2,1,0:T(8,128)S(1)} %get-tuple-element.30), channel_id=1, source_target_pairs={{4,0},{8,4},{12,8},{16,12},{20,16},{24,20},{28,24},{0,28},{5,1},{9... | collective-permute-start | bytes 884744 | tf_op jit(solution)/shard_map/ppermute | solution.py:275
  19.5 1.1 %collective-permute-start.8 = (f32[3,3,32,256]{3,2,1,0:T(8,128)}, f32[3,3,32,256]{3,2,1,0:T(8,128)S(1)}, u32[]{:S(2)}, u32[]{:S(2)}) collective-permute-start(f32[3,3,32,256]{3,2,1,0:T(8,128)} %get-tuple-element.31), channel_id=1, source_target_pairs={{0,4},{4,8},{8,12},{12,16},{16,20},{20,24},{24,28},{28,0},{1,5},{5... | collective-permute-start | bytes 884744 | tf_op jit(solution)/shard_map/ppermute | solution.py:274
  20.6 0.7 slice_bitcast_fusion.8
  21.4 3.6 %collective-permute-start.3 = (f32[1,3,32,256]{3,2,1,0:T(8,128)S(1)}, f32[1,3,32,256]{3,2,1,0:T(8,128)S(1)}, u32[]{:S(2)}, u32[]{:S(2)}) collective-permute-start(f32[1,3,32,256]{3,2,1,0:T(8,128)S(1)} %get-tuple-element.19), channel_id=1, source_target_pairs={{4,0},{8,4},{12,8},{16,12},{20,16},{24,20},{28,24},{0,28},{5,1},{9... | collective-permute-start | bytes 294920 | tf_op jit(solution)/shard_map/ppermute | solution.py:275
  25.0 6.4 %collective-permute-start.2 = (f32[1,3,32,256]{3,2,1,0:T(8,128)S(1)}, f32[1,3,32,256]{3,2,1,0:T(8,128)S(1)}, u32[]{:S(2)}, u32[]{:S(2)}) collective-permute-start(f32[1,3,32,256]{3,2,1,0:T(8,128)S(1)} %get-tuple-element.20), channel_id=1, source_target_pairs={{0,4},{4,8},{8,12},{12,16},{16,20},{20,24},{24,28},{28,0},{1,5},{5... | collective-permute-start | bytes 294920 | tf_op jit(solution)/shard_map/ppermute | solution.py:274
  31.5 0.6 copy-done.16
  32.2 0.8 slice_bitcast_fusion
  33.0 0.7 copy-done.3
  33.7 2.1 %pair_difference.1 = f32[64,256]{1,0:T(8,128)} custom-call(s32[2,256]{1,0:T(2,128)} %pairs_ref.3, s32[16,256]{1,0:T(8,128)} %status_ref.1, f32[8,6,8,128]{3,2,1,0:T(8,128)} %copy-done.3), custom_call_target="tpu_custom_call" | custom-call | tf_op jit(solution)/shard_map/pair_difference/pallas_call | solution.py:313
  35.8 3.8 %collective-permute-done.3.refs_6_ = f32[1,3,32,256]{3,2,1,0:T(8,128)S(1)} collective-permute-done((f32[1,3,32,256]{3,2,1,0:T(8,128)S(1)}, f32[1,3,32,256]{3,2,1,0:T(8,128)S(1)}, u32[]{:S(2)}, u32[]{:S(2)}) %collective-permute-start.3) | collective-permute-done | bytes 98336 | tf_op jit(solution)/shard_map/ppermute | solution.py:275
  39.6 1.3 %collective-permute-start.4 = (f32[3,3,32,256]{3,2,1,0:T(8,128)S(1)}, f32[3,3,32,256]{3,2,1,0:T(8,128)S(1)}, u32[]{:S(2)}, u32[]{:S(2)}) collective-permute-start(f32[3,3,32,256]{3,2,1,0:T(8,128)S(1)} %get-tuple-element.33), channel_id=1, source_target_pairs={{0,4},{4,8},{8,12},{12,16},{16,20},{20,24},{24,28},{28,0},{1,5},{5... | collective-permute-start | bytes 884744 | tf_op jit(solution)/shard_map/ppermute | solution.py:274
  40.9 5.4 %collective-permute-done.2.refs_5_ = f32[1,3,32,256]{3,2,1,0:T(8,128)S(1)} collective-permute-done((f32[1,3,32,256]{3,2,1,0:T(8,128)S(1)}, f32[1,3,32,256]{3,2,1,0:T(8,128)S(1)}, u32[]{:S(2)}, u32[]{:S(2)}) %collective-permute-start.2) | collective-permute-done | bytes 98336 | tf_op jit(solution)/shard_map/ppermute | solution.py:274
  46.3 5.0 %collective-permute-start.7 = (f32[3,3,32,256]{3,2,1,0:T(8,128)S(1)}, f32[3,3,32,256]{3,2,1,0:T(8,128)S(1)}, u32[]{:S(2)}, u32[]{:S(2)}) collective-permute-start(f32[3,3,32,256]{3,2,1,0:T(8,128)S(1)} %get-tuple-element.28), channel_id=1, source_target_pairs={{4,0},{8,4},{12,8},{16,12},{20,16},{24,20},{28,24},{0,28},{5,1},{9... | collective-permute-start | bytes 884744 | tf_op jit(solution)/shard_map/ppermute | solution.py:275
  51.3 7.4 %all-gather = f32[256,256]{1,0:T(8,128)} all-gather(f32[64,256]{1,0:T(8,128)} %pair_difference.1), channel_id=2, replica_groups=mesh['mesh'=8,'harm'=4] {'harm'}, dimensions={0}, use_global_device_ids=true | all-gather | bytes 327680 | tf_op jit(solution)/shard_map/all_gather | solution.py:321
  58.6 3.8 %pair_force.1 = f32[8,6,8,128]{3,2,1,0:T(8,128)} custom-call(s32[1]{0:T(128)} %bitcast.2.place_ref, s32[2,256]{1,0:T(2,128)} %pairs_ref.3, f32[1,256]{1,0:T(1,128)} %bitcast.90, f32[64,32]{1,0:T(8,128)} %constant.8.clone.table_ref, f32[4,8,64]{2,1,0:T(8,128)} %constant.9.clone.back_ref, f32[4,64,256]{2,1,0:T(8,128)} %bitcast.83), custom_call_target="tpu_custom_call" | custom-call | tf_op jit(solution)/shard_map/pair_force/pallas_call | solution.py:324
  62.5 6.0 %all-to-all-start.1 = ((f32[8,6,8,128]{3,2,1,0:T(8,128)}), f32[8,6,8,128]{3,2,1,0:T(8,128)S(1)}, u32[]{:S(2)}, u32[]{:S(2)}) async-start(f32[8,6,8,128]{3,2,1,0:T(8,128)} %pair_force.1), calls=%async_computation.1 | async-start | bytes 393216 | tf_op jit(solution)/shard_map/all_to_all | solution.py:307
  68.5 1.5 %collective-permute-start.10 = (f32[3,3,32,256]{3,2,1,0:T(8,128)S(1)}, f32[3,3,32,256]{3,2,1,0:T(8,128)S(1)}, u32[]{:S(2)}, u32[]{:S(2)}) collective-permute-start(f32[3,3,32,256]{3,2,1,0:T(8,128)S(1)} %get-tuple-element.27), channel_id=1, source_target_pairs={{0,4},{4,8},{8,12},{12,16},{16,20},{20,24},{24,28},{28,0},{1,5},{5... | collective-permute-start | bytes 884744 | tf_op jit(solution)/shard_map/ppermute | solution.py:274
  70.0 0.6 collective-permute-start.13
  70.7 2.4 %collective-permute-start.12 = (f32[1,3,32,256]{3,2,1,0:T(8,128)}, f32[1,3,32,256]{3,2,1,0:T(8,128)S(1)}, u32[]{:S(2)}, u32[]{:S(2)}) collective-permute-start(f32[1,3,32,256]{3,2,1,0:T(8,128)} %get-tuple-element.25), channel_id=1, source_target_pairs={{0,4},{4,8},{8,12},{12,16},{16,20},{20,24},{24,28},{28,0},{1,5},{5... | collective-permute-start | bytes 294920 | tf_op jit(solution)/shard_map/ppermute | solution.py:274
  73.5 2.5 %collective-permute-start.14 = (f32[1,3,32,256]{3,2,1,0:T(8,128)}, f32[1,3,32,256]{3,2,1,0:T(8,128)S(1)}, u32[]{:S(2)}, u32[]{:S(2)}) collective-permute-start(f32[1,3,32,256]{3,2,1,0:T(8,128)} %get-tuple-element.21), channel_id=1, source_target_pairs={{0,4},{4,8},{8,12},{12,16},{16,20},{20,24},{24,28},{28,0},{1,5},{5... | collective-permute-start | bytes 294920 | tf_op jit(solution)/shard_map/ppermute | solution.py:274
  76.0 5.4 %local_terms.1 = (f32[8,3,64,256]{3,2,1,0:T(8,128)}, f32[8,3,64,256]{3,2,1,0:T(8,128)}) custom-call(s32[1]{0:T(128)} %bitcast.2.place_ref, f32[64,256]{1,0:T(8,128)} %bitcast.84, f32[64,256]{1,0:T(8,128)} %bitcast.85, f32[8,3,64,256]{3,2,1,0:T(8,128)} %bitcast.77, f32[8,3,64,256]{3,2,1,0:T(8,128)} %bitcast.79, f32[8,3,64,256]{3,2,1,0:T(8,128)} %bitcast.82), custom_call_target="tpu_custom_call" | custom-call | tf_op jit(solution)/shard_map/local_terms/pallas_call | solution.py:343
  81.4 5.1 %all-to-all-done.1.refs_2_ = f32[8,6,8,128]{3,2,1,0:T(8,128)S(1)} async-done(((f32[8,6,8,128]{3,2,1,0:T(8,128)}), f32[8,6,8,128]{3,2,1,0:T(8,128)S(1)}, u32[]{:S(2)}, u32[]{:S(2)}) %all-to-all-start.1) | async-done | bytes 196640 | tf_op jit(solution)/shard_map/all_to_all | solution.py:307
  86.5 0.7 copy-done.2
  87.2 7.3 %face_scatter.1 = (f32[8,3,64,256]{3,2,1,0:T(8,128)}, f32[8,3,64,256]{3,2,1,0:T(8,128)}) custom-call(s32[8,128]{1,0:T(8,128)} %bitcast.87, s32[8,128]{1,0:T(8,128)} %bitcast.89, f32[8,6,8,128]{3,2,1,0:T(8,128)} %copy-done.2, f32[1,3,32,256]{3,2,1,0:T(8,128)} %copy-done.16, ...), custom_call_target="tpu_custom_call", output_to_operand_aliasing={{0}: (11, {}), {1}: (12, {})} | custom-call | tf_op jit(solution)/shard_map/face_scatter/pallas_call | solution.py:368
  94.5 0.7 copy-done.10
  95.2 3.5 %edge_terms.2 = (f32[8,3,64,256]{3,2,1,0:T(8,128)}, f32[8,3,64,256]{3,2,1,0:T(8,128)}) custom-call(f32[8,3,64,256]{3,2,1,0:T(8,128)} %get-tuple-element.12.res_in, f32[8,3,64,256]{3,2,1,0:T(8,128)} %get-tuple-element.13.jac_in, f32[3,3,32,256]{3,2,1,0:T(8,128)} %copy-done.5, ...), custom_call_target="tpu_custom_call", output_to_operand_aliasing={{0}: (0, {}), {1}: (1, {})} | custom-call | tf_op jit(solution)/shard_map/edge_terms/pallas_call | solution.py:386
  99.4 2.0 %edge_terms.3 = (f32[8,3,64,256]{3,2,1,0:T(8,128)}, f32[8,3,64,256]{3,2,1,0:T(8,128)}) custom-call(f32[8,3,64,256]{3,2,1,0:T(8,128)} %get-tuple-element.14.res_in, f32[8,3,64,256]{3,2,1,0:T(8,128)} %get-tuple-element.15.jac_in, f32[1,3,32,256]{3,2,1,0:T(8,128)} %copy-done.12, ...), custom_call_target="tpu_custom_call", output_to_operand_aliasing={{0}: (0, {}), {1}: (1, {})} | custom-call | tf_op jit(solution)/shard_map/edge_terms/pallas_call | solution.py:386
  (54 shorter events, 1.3 us)
Async XLA Ops:
  0.6 12.6 %copy-start = (f32[8,3,2,32,256]{4,3,2,1,0:T(8,128)S(1)}, f32[8,3,2,32,256]{4,3,2,1,0:T(8,128)}, u32[]{:S(2)}) copy-start(f32[8,3,2,32,256]{4,3,2,1,0:T(8,128)} %param.12) | copy-start | bytes 4718596
  6.9 26.1 %all-to-all-start = ((f32[8,6,8,128]{3,2,1,0:T(8,128)}), f32[8,6,8,128]{3,2,1,0:T(8,128)S(1)}, u32[]{:S(2)}, u32[]{:S(2)}) async-start(f32[8,6,8,128]{3,2,1,0:T(8,128)} %face_gather.1), calls=%async_computation | async-start | bytes 393216 | tf_op jit(solution)/shard_map/all_to_all | solution.py:307
  13.2 7.4 %copy-start.1 = (f32[8,3,2,32,256]{4,3,2,1,0:T(8,128)S(1)}, f32[8,3,2,32,256]{4,3,2,1,0:T(8,128)}, u32[]{:S(2)}) copy-start(f32[8,3,2,32,256]{4,3,2,1,0:T(8,128)} %param.13) | copy-start | bytes 4718596
  13.9 11.0 %collective-permute-start.1 = (f32[1,3,32,256]{3,2,1,0:T(8,128)S(1)}, f32[1,3,32,256]{3,2,1,0:T(8,128)S(1)}, u32[]{:S(2)}, u32[]{:S(2)}) collective-permute-start(f32[1,3,32,256]{3,2,1,0:T(8,128)S(1)} %get-tuple-element.23), channel_id=1, source_target_pairs={{4,0},{8,4},{12,8},{16,12},{20,16},{24,20},{28,24},{0,28},{5,1},{9... | collective-permute-start | bytes 294920 | tf_op jit(solution)/shard_map/ppermute | solution.py:275
  14.0 17.5 %collective-permute-start = (f32[1,3,32,256]{3,2,1,0:T(8,128)S(1)}, f32[1,3,32,256]{3,2,1,0:T(8,128)S(1)}, u32[]{:S(2)}, u32[]{:S(2)}) collective-permute-start(f32[1,3,32,256]{3,2,1,0:T(8,128)S(1)} %get-tuple-element.24), channel_id=1, source_target_pairs={{0,4},{4,8},{8,12},{12,16},{16,20},{20,24},{24,28},{28,0},{1,5},{5... | collective-permute-start | bytes 294920 | tf_op jit(solution)/shard_map/ppermute | solution.py:274
  17.7 28.6 %collective-permute-start.9 = (f32[3,3,32,256]{3,2,1,0:T(8,128)S(1)}, f32[3,3,32,256]{3,2,1,0:T(8,128)S(1)}, u32[]{:S(2)}, u32[]{:S(2)}) collective-permute-start(f32[3,3,32,256]{3,2,1,0:T(8,128)S(1)} %get-tuple-element.30), channel_id=1, source_target_pairs={{4,0},{8,4},{12,8},{16,12},{20,16},{24,20},{28,24},{0,28},{5,1},{9... | collective-permute-start | bytes 884744 | tf_op jit(solution)/shard_map/ppermute | solution.py:275
  19.5 31.7 %collective-permute-start.8 = (f32[3,3,32,256]{3,2,1,0:T(8,128)}, f32[3,3,32,256]{3,2,1,0:T(8,128)S(1)}, u32[]{:S(2)}, u32[]{:S(2)}) collective-permute-start(f32[3,3,32,256]{3,2,1,0:T(8,128)} %get-tuple-element.31), channel_id=1, source_target_pairs={{0,4},{4,8},{8,12},{12,16},{16,20},{20,24},{24,28},{28,0},{1,5},{5... | collective-permute-start | bytes 884744 | tf_op jit(solution)/shard_map/ppermute | solution.py:274
  21.4 18.2 %collective-permute-start.3 = (f32[1,3,32,256]{3,2,1,0:T(8,128)S(1)}, f32[1,3,32,256]{3,2,1,0:T(8,128)S(1)}, u32[]{:S(2)}, u32[]{:S(2)}) collective-permute-start(f32[1,3,32,256]{3,2,1,0:T(8,128)S(1)} %get-tuple-element.19), channel_id=1, source_target_pairs={{4,0},{8,4},{12,8},{16,12},{20,16},{24,20},{28,24},{0,28},{5,1},{9... | collective-permute-start | bytes 294920 | tf_op jit(solution)/shard_map/ppermute | solution.py:275
  25.0 14.6 %copy-start.15 = (f32[1,3,32,256]{3,2,1,0:T(8,128)}, f32[1,3,32,256]{3,2,1,0:T(8,128)S(1)}, u32[]{:S(2)}) copy-start(f32[1,3,32,256]{3,2,1,0:T(8,128)S(1)} %collective-permute-done.1.refs_4_) | copy-start | bytes 294916
  25.0 21.3 %collective-permute-start.2 = (f32[1,3,32,256]{3,2,1,0:T(8,128)S(1)}, f32[1,3,32,256]{3,2,1,0:T(8,128)S(1)}, u32[]{:S(2)}, u32[]{:S(2)}) collective-permute-start(f32[1,3,32,256]{3,2,1,0:T(8,128)S(1)} %get-tuple-element.20), channel_id=1, source_target_pairs={{0,4},{4,8},{8,12},{12,16},{16,20},{20,24},{24,28},{28,0},{1,5},{5... | collective-permute-start | bytes 294920 | tf_op jit(solution)/shard_map/ppermute | solution.py:274
  32.2 36.4 %collective-permute-start.5 = (f32[3,3,32,256]{3,2,1,0:T(8,128)S(1)}, f32[3,3,32,256]{3,2,1,0:T(8,128)S(1)}, u32[]{:S(2)}, u32[]{:S(2)}) collective-permute-start(f32[3,3,32,256]{3,2,1,0:T(8,128)S(1)} %get-tuple-element.32), channel_id=1, source_target_pairs={{4,0},{8,4},{12,8},{16,12},{20,16},{24,20},{28,24},{0,28},{5,1},{9... | collective-permute-start | bytes 884744 | tf_op jit(solution)/shard_map/ppermute | solution.py:275
  39.6 6.7 %copy-start.17 = (f32[1,3,32,256]{3,2,1,0:T(8,128)}, f32[1,3,32,256]{3,2,1,0:T(8,128)S(1)}, u32[]{:S(2)}) copy-start(f32[1,3,32,256]{3,2,1,0:T(8,128)S(1)} %collective-permute-done.3.refs_6_) | copy-start | bytes 294916
  39.6 30.4 %collective-permute-start.4 = (f32[3,3,32,256]{3,2,1,0:T(8,128)S(1)}, f32[3,3,32,256]{3,2,1,0:T(8,128)S(1)}, u32[]{:S(2)}, u32[]{:S(2)}) collective-permute-start(f32[3,3,32,256]{3,2,1,0:T(8,128)S(1)} %get-tuple-element.33), channel_id=1, source_target_pairs={{0,4},{4,8},{8,12},{12,16},{16,20},{20,24},{24,28},{28,0},{1,5},{5... | collective-permute-start | bytes 884744 | tf_op jit(solution)/shard_map/ppermute | solution.py:274
  46.3 23.8 %copy-start.18 = (f32[1,3,32,256]{3,2,1,0:T(8,128)}, f32[1,3,32,256]{3,2,1,0:T(8,128)S(1)}, u32[]{:S(2)}) copy-start(f32[1,3,32,256]{3,2,1,0:T(8,128)S(1)} %collective-permute-done.2.refs_5_) | copy-start | bytes 294916
  46.3 24.4 %collective-permute-start.11 = (f32[3,3,32,256]{3,2,1,0:T(8,128)}, f32[3,3,32,256]{3,2,1,0:T(8,128)S(1)}, u32[]{:S(2)}, u32[]{:S(2)}) collective-permute-start(f32[3,3,32,256]{3,2,1,0:T(8,128)} %get-tuple-element.26), channel_id=1, source_target_pairs={{4,0},{8,4},{12,8},{16,12},{20,16},{24,20},{28,24},{0,28},{5,1},{9... | collective-permute-start | bytes 884744 | tf_op jit(solution)/shard_map/ppermute | solution.py:275
  46.3 35.1 %copy-start.4 = (f32[3,3,32,256]{3,2,1,0:T(8,128)}, f32[3,3,32,256]{3,2,1,0:T(8,128)S(1)}, u32[]{:S(2)}) copy-start(f32[3,3,32,256]{3,2,1,0:T(8,128)S(1)} %collective-permute-done.9.refs_1_) | copy-start | bytes 884740
  46.3 26.7 %collective-permute-start.7 = (f32[3,3,32,256]{3,2,1,0:T(8,128)S(1)}, f32[3,3,32,256]{3,2,1,0:T(8,128)S(1)}, u32[]{:S(2)}, u32[]{:S(2)}) collective-permute-start(f32[3,3,32,256]{3,2,1,0:T(8,128)S(1)} %get-tuple-element.28), channel_id=1, source_target_pairs={{4,0},{8,4},{12,8},{16,12},{20,16},{24,20},{28,24},{0,28},{5,1},{9... | collective-permute-start | bytes 884744 | tf_op jit(solution)/shard_map/ppermute | solution.py:275
  51.3 30.1 %copy-start.5 = (f32[3,3,32,256]{3,2,1,0:T(8,128)}, f32[3,3,32,256]{3,2,1,0:T(8,128)S(1)}, u32[]{:S(2)}) copy-start(f32[3,3,32,256]{3,2,1,0:T(8,128)S(1)} %collective-permute-done.8.refs_0_) | copy-start | bytes 884740
  51.3 22.2 %collective-permute-start.6 = (f32[3,3,32,256]{3,2,1,0:T(8,128)S(1)}, f32[3,3,32,256]{3,2,1,0:T(8,128)}, u32[]{:S(2)}, u32[]{:S(2)}) collective-permute-start(f32[3,3,32,256]{3,2,1,0:T(8,128)S(1)} %get-tuple-element.29), channel_id=1, source_target_pairs={{0,4},{4,8},{8,12},{12,16},{16,20},{20,24},{24,28},{28,0},{1,5},{5... | collective-permute-start | bytes 884744 | tf_op jit(solution)/shard_map/ppermute | solution.py:274
  62.5 24.0 %all-to-all-start.1 = ((f32[8,6,8,128]{3,2,1,0:T(8,128)}), f32[8,6,8,128]{3,2,1,0:T(8,128)S(1)}, u32[]{:S(2)}, u32[]{:S(2)}) async-start(f32[8,6,8,128]{3,2,1,0:T(8,128)} %pair_force.1), calls=%async_computation.1 | async-start | bytes 393216 | tf_op jit(solution)/shard_map/all_to_all | solution.py:307
  68.5 12.8 %copy-start.6 = (f32[3,3,32,256]{3,2,1,0:T(8,128)}, f32[3,3,32,256]{3,2,1,0:T(8,128)S(1)}, u32[]{:S(2)}) copy-start(f32[3,3,32,256]{3,2,1,0:T(8,128)S(1)} %collective-permute-done.5.refs_8_) | copy-start | bytes 884740
  68.5 25.9 %collective-permute-start.10 = (f32[3,3,32,256]{3,2,1,0:T(8,128)S(1)}, f32[3,3,32,256]{3,2,1,0:T(8,128)S(1)}, u32[]{:S(2)}, u32[]{:S(2)}) collective-permute-start(f32[3,3,32,256]{3,2,1,0:T(8,128)S(1)} %get-tuple-element.27), channel_id=1, source_target_pairs={{0,4},{4,8},{8,12},{12,16},{16,20},{20,24},{24,28},{28,0},{1,5},{5... | collective-permute-start | bytes 884744 | tf_op jit(solution)/shard_map/ppermute | solution.py:274
  70.0 11.3 %copy-start.8 = (f32[3,3,32,256]{3,2,1,0:T(8,128)}, f32[3,3,32,256]{3,2,1,0:T(8,128)S(1)}, u32[]{:S(2)}) copy-start(f32[3,3,32,256]{3,2,1,0:T(8,128)S(1)} %collective-permute-done.4.refs_7_) | copy-start | bytes 884740
  70.0 28.6 %collective-permute-start.13 = (f32[1,3,32,256]{3,2,1,0:T(8,128)}, f32[1,3,32,256]{3,2,1,0:T(8,128)S(1)}, u32[]{:S(2)}, u32[]{:S(2)}) collective-permute-start(f32[1,3,32,256]{3,2,1,0:T(8,128)} %get-tuple-element.22), channel_id=1, source_target_pairs={{4,0},{8,4},{12,8},{16,12},{20,16},{24,20},{28,24},{0,28},{5,1},{9... | collective-permute-start | bytes 294920 | tf_op jit(solution)/shard_map/ppermute | solution.py:275
  70.7 10.7 %copy-start.7 = (f32[3,3,32,256]{3,2,1,0:T(8,128)}, f32[3,3,32,256]{3,2,1,0:T(8,128)S(1)}, u32[]{:S(2)}) copy-start(f32[3,3,32,256]{3,2,1,0:T(8,128)S(1)} %collective-permute-done.11.refs_3_) | copy-start | bytes 884740
  70.7 28.0 %collective-permute-start.12 = (f32[1,3,32,256]{3,2,1,0:T(8,128)}, f32[1,3,32,256]{3,2,1,0:T(8,128)S(1)}, u32[]{:S(2)}, u32[]{:S(2)}) collective-permute-start(f32[1,3,32,256]{3,2,1,0:T(8,128)} %get-tuple-element.25), channel_id=1, source_target_pairs={{0,4},{4,8},{8,12},{12,16},{16,20},{20,24},{24,28},{28,0},{1,5},{5... | collective-permute-start | bytes 294920 | tf_op jit(solution)/shard_map/ppermute | solution.py:274
  73.0 8.4 %copy-start.9 = (f32[3,3,32,256]{3,2,1,0:T(8,128)}, f32[3,3,32,256]{3,2,1,0:T(8,128)S(1)}, u32[]{:S(2)}) copy-start(f32[3,3,32,256]{3,2,1,0:T(8,128)S(1)} %collective-permute-done.7.refs_10_) | copy-start | bytes 884740
  73.0 25.7 %collective-permute-start.15 = (f32[1,3,32,256]{3,2,1,0:T(8,128)}, f32[1,3,32,256]{3,2,1,0:T(8,128)S(1)}, u32[]{:S(2)}, u32[]{:S(2)}) collective-permute-start(f32[1,3,32,256]{3,2,1,0:T(8,128)} %get-tuple-element.18), channel_id=1, source_target_pairs={{4,0},{8,4},{12,8},{16,12},{20,16},{24,20},{28,24},{0,28},{5,1},{9... | collective-permute-start | bytes 294920 | tf_op jit(solution)/shard_map/ppermute | solution.py:275
  73.5 25.2 %collective-permute-start.14 = (f32[1,3,32,256]{3,2,1,0:T(8,128)}, f32[1,3,32,256]{3,2,1,0:T(8,128)S(1)}, u32[]{:S(2)}, u32[]{:S(2)}) collective-permute-start(f32[1,3,32,256]{3,2,1,0:T(8,128)} %get-tuple-element.21), channel_id=1, source_target_pairs={{0,4},{4,8},{8,12},{12,16},{16,20},{20,24},{24,28},{28,0},{1,5},{5... | collective-permute-start | bytes 294920 | tf_op jit(solution)/shard_map/ppermute | solution.py:274
  86.5 0.7 copy-start.2
  94.5 0.7 copy-start.10
  98.7 0.7 copy-start.14
  (5 other events, 3.3 us)
where the time goes:
time: 102 us; the launch traced here: 101 us
  starting transfers between devices  42 us (41%)
  Pallas kernels  30.3 us (30%)
  waiting for transfers between devices  14.4 us (14%)
  blocking collectives  7.37 us (7%)
  local copies, waits for them, and re-layouts  6.53 us (6%)
    ppermute x8, starting transfers between devices, halo(): pieces.append(lax.ppermute(part[:, :, layers - 1], 'mesh', forward))  18.1 us
    all_to_all x2, starting transfers between devices, exchange(): lax.all_to_all(block, 'mesh', split_axis=0, concat_axis=0, tiled=True)  12.4 us
    ppermute x8, starting transfers between devices, halo(): pieces.append(lax.ppermute(part[:, :, 0], 'mesh', backward))  11.5 us
    all_gather x1, blocking collectives, on_device(): everything = lax.all_gather(own_opening, 'harm')  7.37 us
    pallas_call x1, Pallas kernels, on_device(): pl.pallas_call(lambda *refs: scatter_kernel(*refs, spans=early), grid=(co...  7.29 us
    pallas_call x1, Pallas kernels, on_device(): pl.pallas_call(gather_kernel, grid=(comps,), in_specs=[whole(cells.shape)...  6.25 us
    ppermute x8, waiting for transfers between devices, halo(): pieces.append(lax.ppermute(part[:, :, layers - 1], 'mesh', forward))  5.47 us
    pallas_call x2, Pallas kernels, on_device(): pl.pallas_call(tail_kernel, grid=(last - first,), in_specs=[mine] * 2 + [...  5.46 us
  transfers between devices with their start and end apart: 18, of which 4 were waited for; matrix products, arithmetic and copies ran while one was open for 3% of the time, Pallas kernels for 22%

commit v1 on v0

--- a/solution.py
+++ b/solution.py
@@ -16,8 +16,8 @@
 normal_penalty = 2.0
 shear_penalty = 1.0
 
-CHUNKS = ((0, 1), (1, 4), (4, 7), (7, 8))
-VMEM = 56 * 1024 * 1024
+CUTS = (0, 3, 7, 8)
+VMEM = 28 * 1024 * 1024
 
 
 def split2(value):
@@ -53,7 +53,9 @@
     return jnp.where(hit, 1.0, 0.0).astype(kind)
 
 
-def gather_kernel(cells_ref, send_ref, x_ref, y_ref, out_ref, cell_ref, low_ref):
+def gather_kernel(cells_ref, send_ref, x_ref, y_ref, out_ref, *refs, edges):
+    edge_refs = refs[: len(edges)]
+    cell_ref, low_ref = refs[len(edges) :]
     comp = pl.program_id(0)
     coefs, _, rows, axial = x_ref.shape
     slots = cell_ref.shape[1]
@@ -69,6 +71,8 @@
     row_of = cell_ref[...] // axial
     mask = lax.broadcasted_iota(jnp.int32, (rows, slots), 0) == row_of
     for field, ref in enumerate((x_ref, y_ref)):
+        for edge_ref, (start, first, last) in zip(edge_refs, edges):
+            edge_ref[field, :, 0] = ref[first:last, 0, start : start + rows // 2]
         flat = ref[...].reshape(coefs * rows, axial)
         high, low = split2(flat)
         picked = jnp.dot(
@@ -100,7 +104,13 @@
     return jnp.concatenate([ref[owner, block] for owner in range(ref.shape[0])], axis=1)
 
 
-def opening_kernel(pairs_ref, status_ref, arrived_ref, out_ref):
+def mark_kernel(piece_ref, out_ref):
+    del piece_ref
+    out_ref[...] = jnp.zeros_like(out_ref)
+
+
+def opening_kernel(pairs_ref, status_ref, mark_ref, arrived_ref, out_ref):
+    del mark_ref
     arrived = jnp.concatenate([by_slot(arrived_ref, block) for block in range(6)], axis=0)
     values, slots = arrived.shape
     table = pair_table(pairs_ref, slots)
@@ -153,40 +163,30 @@
             out_ref[block] = part
 
 
-def local_kernel(place_ref, stiff_ref, mass_ref, x_ref, y_ref, forcing_ref, res_ref, jac_ref):
-    _, comps, rows, axial = x_ref.shape
-    layer = rows // 2
-    harmonic = place_ref[0] * pl.num_programs(0) + pl.program_id(0) + 1
-    frequency = harmonic.astype(jnp.float32) * (1.5 / HARM)
-    mass = mass_ref[...]
-    diagonal = 6.0 + stiff_ref[...] - (frequency * frequency) * mass
-    turn = (frequency * damping_ratio) * mass
-    row = lax.broadcasted_iota(jnp.int32, (rows, axial), 0) % layer
-    column = lax.broadcasted_iota(jnp.int32, (rows, axial), 1)
-    for ref, out_ref, forced in ((x_ref, res_ref, True), (y_ref, jac_ref, False)):
-        for comp in range(comps):
-            cosine = ref[0, comp]
-            sine = ref[1, comp]
-            for part, value, turned in ((0, cosine, sine), (1, sine, -cosine)):
-                near = jnp.where(row == 0, 0.0, jnp.roll(value, 1, axis=0))
-                near = near + jnp.where(row == layer - 1, 0.0, jnp.roll(value, -1, axis=0))
-                near = near + jnp.where(column == 0, 0.0, pltpu.roll(value, 1, axis=1))
-                near = near + jnp.where(column == axial - 1, 0.0, pltpu.roll(value, axial - 1, axis=1))
-                near = near + jnp.concatenate([value[layer:], value[:layer]], axis=0)
-                result = diagonal * value + turn * turned - near
-                if forced:
-                    result = result - forcing_ref[part, comp]
-                out_ref[part, comp] = result
-
-
-def scatter_kernel(cells_ref, send_ref, back_ref, *refs, spans):
-    count = len(spans)
-    halos = refs[: 4 * count]
-    res_in, jac_in, res_ref, jac_ref, cell_ref, low_ref = refs[4 * count :]
+def combine_kernel(
+    place_ref,
+    cells_ref,
+    send_ref,
+    back_ref,
+    below_ref,
+    above_ref,
+    stiff_ref,
+    mass_ref,
+    x_ref,
+    y_ref,
+    forcing_ref,
+    res_ref,
+    jac_ref,
+    late_res_ref,
+    late_jac_ref,
+    cell_ref,
+    low_ref,
+):
     comp = pl.program_id(0)
-    coefs, _, rows, axial = res_ref.shape
+    coefs, _, rows, axial = x_ref.shape
     slots = cell_ref.shape[1]
     layer = rows // 2
+    early = below_ref.shape[1]
 
     @pl.when(comp == 0)
     def _():
@@ -196,9 +196,15 @@
 
     row_of = cell_ref[...] // axial
     mask = lax.broadcasted_iota(jnp.int32, (rows, slots), 0) == row_of
-    for field, (in_ref, out_ref) in enumerate(((res_in, res_ref), (jac_in, jac_ref))):
+    row = lax.broadcasted_iota(jnp.int32, (rows, axial), 0) % layer
+    column = lax.broadcasted_iota(jnp.int32, (rows, axial), 1)
+    mass = mass_ref[...]
+    stiff = 6.0 + stiff_ref[...]
+    for field, (ref, out_ref, late_ref) in enumerate(
+        ((x_ref, res_ref, late_res_ref), (y_ref, jac_ref, late_jac_ref))
+    ):
         force = by_slot(back_ref, field * 3 + comp)
-        total = None
+        contact = None
         for part in split2(force):
             wide = part.astype(jnp.float32)
             spread = jnp.where(mask[None], wide[:, None, :], 0.0).astype(jnp.bfloat16)
@@ -208,22 +214,37 @@
                 (((1,), (1,)), ((), ())),
                 preferred_element_type=jnp.float32,
             )
-            total = term if total is None else total + term
-        total = in_ref[...].reshape(coefs, rows, axial) + total.reshape(coefs, rows, axial)
-        out_ref[...] = total.reshape(coefs, 1, rows, axial)
-        for index, (first, last) in enumerate(spans):
-            below, above = halos[4 * index + 2 * field : 4 * index + 2 * field + 2]
-            out_ref[first:last, 0, 0:layer, :] = total[first:last, 0:layer] - below[:, 0]
-            out_ref[first:last, 0, layer:rows, :] = total[first:last, layer:rows] - above[:, 0]
-
-
-def tail_kernel(res_in, jac_in, *refs):
-    res_ref, jac_ref = refs[-2:]
+            contact = term if contact is None else contact + term
+        contact = contact.reshape(coefs, rows, axial)
+        for coef in range(coefs):
+            harmonic = place_ref[0] * (coefs // 2) + (coef // 2 + 1)
+            frequency = harmonic.astype(jnp.float32) * (1.5 / HARM)
+            value = ref[coef, 0]
+            turned = ref[coef + 1, 0] if coef % 2 == 0 else -ref[coef - 1, 0]
+            near = jnp.where(row == 0, 0.0, jnp.roll(value, 1, axis=0))
+            near = near + jnp.where(row == layer - 1, 0.0, jnp.roll(value, -1, axis=0))
+            near = near + jnp.where(column == 0, 0.0, pltpu.roll(value, 1, axis=1))
+            near = near + jnp.where(column == axial - 1, 0.0, pltpu.roll(value, axial - 1, axis=1))
+            near = near + jnp.concatenate([value[layer:], value[:layer]], axis=0)
+            result = (stiff - (frequency * frequency) * mass) * value - near
+            result = result + (frequency * damping_ratio) * mass * turned + contact[coef]
+            if field == 0:
+                result = result - forcing_ref[coef, 0]
+            if coef < early:
+                out_ref[coef, 0, :layer] = result[:layer] - below_ref[field, coef, comp]
+                out_ref[coef, 0, layer:] = result[layer:] - above_ref[field, coef, comp]
+            else:
+                late_ref[coef - early, comp] = result
+
+
+def edge_kernel(late_res, late_jac, below, above, res_in, jac_in, res_ref, jac_ref, *, offset):
+    del res_in, jac_in
     layer = res_ref.shape[2] // 2
-    for field, (in_ref, out_ref) in enumerate(((res_in, res_ref), (jac_in, jac_ref))):
-        below, above = refs[2 * field : 2 * field + 2]
-        out_ref[:, :, 0:layer, :] = in_ref[:, :, 0:layer, :] - below[...]
-        out_ref[:, :, layer:, :] = in_ref[:, :, layer:, :] - above[...]
+    step = pl.program_id(0)
+    for field, (late_ref, out_ref) in enumerate(((late_res, res_ref), (late_jac, jac_ref))):
+        value = late_ref[offset + step]
+        out_ref[0, :, :layer, :] = value[:, :layer] - below[field, step]
+        out_ref[0, :, layer:, :] = value[:, layer:] - above[field, step]
 
 
 def transform_table(time_count, coef_count):
@@ -231,6 +252,10 @@
     coef = np.arange(coef_count)[None, :]
     angles = ((coef // 2 + 1) * sample % time_count) * (2.0 * math.pi / time_count)
     return np.where(coef % 2 == 0, np.cos(angles), np.sin(angles)).astype(np.float32)
+
+
+SMALL = pl.CostEstimate(flops=1000, transcendentals=0, bytes_accessed=1000)
+LARGE = pl.CostEstimate(flops=10**12, transcendentals=10**9, bytes_accessed=10**10)
 
 
 def params(*semantics):
@@ -266,18 +291,16 @@
 
     forward = [(i, (i + 1) % owners) for i in range(owners)]
     backward = [(target, source) for source, target in forward]
-
-    def halo(first, last):
-        pieces = []
-        for field in (displacement, direction):
-            part = field[first:last]
-            pieces.append(lax.ppermute(part[:, :, layers - 1], "mesh", forward))
-            pieces.append(lax.ppermute(part[:, :, 0], "mesh", backward))
-        return pieces
-
-    ends = sorted({a * coefs // 8 for span in CHUNKS for a in span})
+    ahead = lambda piece: lax.ppermute(piece, "mesh", forward)
+    behind = lambda piece: lax.ppermute(piece, "mesh", backward)
+    keep = lambda value: pltpu.with_memory_space_constraint(value, pltpu.VMEM)
+
+    ends = [cut * coefs // 8 for cut in CUTS]
     spans = list(zip(ends[:-1], ends[1:]))
-    pieces = [halo(*span) for span in spans]
+    early = ends[1]
+    first_piece = jnp.stack([field[:early, :, layers - 1] for field in (displacement, direction)])
+    below = [ahead(first_piece)]
+    above = []
 
     x = displacement.reshape(coefs, comps, rows, axial)
     y = direction.reshape(coefs, comps, rows, axial)
@@ -285,19 +308,28 @@
     send = send_rows.reshape(slots // LANES, LANES)
     whole = lambda shape: pl.BlockSpec(shape, lambda *_: (0,) * len(shape))
     scalar = pl.BlockSpec(memory_space=pltpu.SMEM)
+    near_memory = pl.BlockSpec(memory_space=pltpu.VMEM)
     per_comp = pl.BlockSpec((coefs, 1, rows, axial), lambda comp: (0, comp, 0, 0))
 
-    outgoing = pl.pallas_call(
-        gather_kernel,
+    edges = [(0, 0, early)]
+    edges += [(start, first, last) for first, last in spans[1:] for start in (radial, 0)]
+    edge_shapes = [(2, last - first, comps, radial, axial) for _, first, last in edges]
+    outgoing, *sent = pl.pallas_call(
+        lambda *refs: gather_kernel(*refs, edges=edges),
         grid=(comps,),
         in_specs=[whole(cells.shape), whole(send.shape), per_comp, per_comp],
-        out_specs=whole(wire),
-        out_shape=jax.ShapeDtypeStruct(wire, f32),
+        out_specs=[whole(wire)]
+        + [
+            pl.BlockSpec(shape[:2] + (1,) + shape[3:], lambda comp: (0, 0, comp, 0, 0))
+            for shape in edge_shapes
+        ],
+        out_shape=[jax.ShapeDtypeStruct(shape, f32) for shape in [wire] + edge_shapes],
         scratch_shapes=[
             pltpu.VMEM((1, slots), jnp.int32),
             pltpu.VMEM((2 * axial, slots), jnp.bfloat16),
         ],
         compiler_params=params("arbitrary"),
+        cost_estimate=SMALL,
         name="face_gather",
     )(cells, send, x, y)
 
@@ -309,15 +341,26 @@
             block = block.transpose(1, 0, 2).reshape(wire)
         return block
 
+    outgoing, sent[0] = lax.optimization_barrier((outgoing, sent[0]))
+    mark = pl.pallas_call(
+        mark_kernel,
+        in_specs=[near_memory],
+        out_specs=near_memory,
+        out_shape=pltpu.VMEM((8, LANES), f32),
+        cost_estimate=LARGE,
+        name="first_piece_arrived",
+    )(keep(below[0]))
+    above.append(behind(sent[0]))
     arrived = exchange(outgoing)
     own_opening = pl.pallas_call(
         opening_kernel,
-        in_specs=[whole(pair_rows.shape), whole(status.shape), whole(wire)],
+        in_specs=[whole(pair_rows.shape), whole(status.shape), near_memory, near_memory],
         out_specs=whole((values + status.shape[0], pairs)),
         out_shape=jax.ShapeDtypeStruct((values + status.shape[0], pairs), f32),
         compiler_params=params(),
+        cost_estimate=SMALL,
         name="pair_difference",
-    )(pair_rows, status, arrived)
+    )(pair_rows, status, keep(mark), pltpu.with_memory_space_constraint(arrived, pltpu.VMEM))
     everything = lax.all_gather(own_opening, "harm")
     table = transform_table(TIME, coef_total)
     back = ((2.0 / TIME) * table.T).reshape(harm_count, coefs, TIME)
@@ -334,65 +377,62 @@
         out_specs=whole(wire),
         out_shape=jax.ShapeDtypeStruct(wire, f32),
         compiler_params=params(),
+        cost_estimate=LARGE,
         name="pair_force",
     )(place, pair_rows, crack_gap.reshape(1, pairs), jnp.asarray(table), jnp.asarray(back), everything)
     returned = exchange(slot_force)
-
-    per_harmonic = pl.BlockSpec((2, comps, rows, axial), lambda i: (i, 0, 0, 0))
+    above[0], sent[1:], _ = lax.optimization_barrier((above[0], sent[1:], slot_force))
+    below.append(ahead(sent[1]))
+    above.append(behind(sent[2]))
+
     flat = jax.ShapeDtypeStruct(x.shape, f32)
-    residual, product = pl.pallas_call(
-        local_kernel,
-        grid=(coefs // 2,),
-        in_specs=[scalar, whole((rows, axial)), whole((rows, axial))] + [per_harmonic] * 3,
-        out_specs=[per_harmonic] * 2,
-        out_shape=[flat, flat],
+    late_shape = pltpu.VMEM((coefs - early, comps, rows, axial), f32)
+    residual, product, late_res, late_jac = pl.pallas_call(
+        combine_kernel,
+        grid=(comps,),
+        in_specs=[scalar, whole(cells.shape), whole(send.shape)]
+        + [near_memory] * 3
+        + [whole((rows, axial))] * 2
+        + [per_comp] * 3,
+        out_specs=[per_comp] * 2 + [near_memory] * 2,
+        out_shape=[flat, flat, late_shape, late_shape],
+        scratch_shapes=[
+            pltpu.VMEM((1, slots), jnp.int32),
+            pltpu.VMEM((axial, slots), jnp.bfloat16),
+        ],
         compiler_params=params("arbitrary"),
-        name="local_terms",
+        cost_estimate=LARGE,
+        name="combine_terms",
     )(
         place,
+        cells,
+        send,
+        keep(returned),
+        keep(below[0]),
+        keep(above[0]),
         stiffness.reshape(rows, axial),
         lumped_mass.reshape(rows, axial),
         x,
         y,
         forcing.reshape(x.shape),
     )
-
-    early, late = (spans[:-2], spans[-2:])
-    near = [piece for chunk in pieces[: len(early)] for piece in chunk]
-    near_specs = [
-        pl.BlockSpec((last - first, 1, radial, axial), lambda comp: (0, comp, 0, 0))
-        for first, last in early
-        for _ in range(4)
-    ]
-    fixed = 3 + len(near)
-    residual, product = pl.pallas_call(
-        lambda *refs: scatter_kernel(*refs, spans=early),
-        grid=(comps,),
-        in_specs=[whole(cells.shape), whole(send.shape), whole(wire)] + near_specs + [per_comp] * 2,
-        out_specs=[per_comp] * 2,
-        out_shape=[flat, flat],
-        input_output_aliases={fixed: 0, fixed + 1: 1},
-        scratch_shapes=[
-            pltpu.VMEM((1, slots), jnp.int32),
-            pltpu.VMEM((axial, slots), jnp.bfloat16),
-        ],
-        compiler_params=params("arbitrary"),
-        name="face_scatter",
-    )(cells, send, returned, *near, residual, product)
-
-    for (first, last), chunk in zip(late, pieces[len(early) :]):
+    residual, sent[3:] = lax.optimization_barrier((residual, sent[3:]))
+    below.append(ahead(sent[3]))
+    above.append(behind(sent[4]))
+
+    for (first, last), low_edge, high_edge in zip(spans[1:], below[1:], above[1:]):
         mine = pl.BlockSpec((1, comps, rows, axial), lambda i, first=first: (first + i, 0, 0, 0))
-        edge = pl.BlockSpec((1, comps, radial, axial), lambda i: (i, 0, 0, 0))
         residual, product = pl.pallas_call(
-            tail_kernel,
+            lambda *refs, offset=first - early: edge_kernel(*refs, offset=offset),
             grid=(last - first,),
-            in_specs=[mine] * 2 + [edge] * 4,
+            in_specs=[near_memory] * 4 + [pl.BlockSpec(memory_space=pl.ANY)] * 2,
             out_specs=[mine] * 2,
             out_shape=[flat, flat],
-            input_output_aliases={0: 0, 1: 1},
+            input_output_aliases={4: 0, 5: 1},
             compiler_params=params("arbitrary"),
+            cost_estimate=LARGE if last < coefs else SMALL,
             name="edge_terms",
-        )(residual, product, *chunk)
+        )(keep(late_res), keep(late_jac), keep(low_edge), keep(high_edge), residual, product)
     return residual.reshape(displacement.shape), product.reshape(displacement.shape)
 
 

time: 102 us -> 91 us (0.89)
  the two profiles are of different devices: /device:TPU:4 before, /device:TPU:0 now
where the time goes in v1:
time: 91 us; the launch traced here: 90.4 us
  starting transfers between devices  42.4 us (47%)
  Pallas kernels  22.4 us (25%)
  waiting for transfers between devices  11.2 us (12%)
  local copies, waits for them, and re-layouts  7.75 us (9%)
  blocking collectives  5.79 us (6%)
    ppermute x3, starting transfers between devices, on_device(): ahead = lambda piece: lax.ppermute(piece, 'mesh', forward)  26.6 us
    all_to_all x2, starting transfers between devices, exchange(): lax.all_to_all(block, 'mesh', split_axis=0, concat_axis=0, tiled=True)  8.26 us
    pallas_call x1, Pallas kernels, on_device(): pl.pallas_call(combine_kernel, grid=(comps,), in_specs=[scalar, whole(cel...  7.83 us
    ppermute x3, starting transfers between devices, on_device(): behind = lambda piece: lax.ppermute(piece, 'mesh', backward)  7.59 us
    all_to_all x2, waiting for transfers between devices, exchange(): lax.all_to_all(block, 'mesh', split_axis=0, concat_axis=0, tiled=True)  7.28 us
    unnamed x40, local copies, waits for them, and re-layouts  6.54 us
    all_gather x1, blocking collectives, on_device(): everything = lax.all_gather(own_opening, 'harm')  5.79 us
    pallas_call x1, Pallas kernels, on_device(): pl.pallas_call(lambda *refs: gather_kernel(*refs, edges=edges), grid=(com...  5.47 us
  transfers between devices with their start and end apart: 8, of which 4 were waited for; matrix products, arithmetic and copies ran while one was open for 0% of the time, Pallas kernels for 23%

profile of v1, /device:TPU:0, one launch (start us, length us, event | category | flops | bytes accessed | tf_op | source)
XLA Modules:
  0.0 90.4 jit_solution(4588632968373418723)
XLA Ops:
  0.6 0.0 copy-start.7
  0.7 0.0 copy-start.5
  0.7 1.2 %slice_bitcast_fusion = (f32[1,3,3,32,256]{4,3,2,1,0:T(8,128)S(1)}, f32[1,3,3,32,256]{4,3,2,1,0:T(8,128)S(1)}) fusion(f32[8,3,2,32,256]{4,3,2,1,0:T(8,128)} %param.13, f32[8,3,2,32,256]{4,3,2,1,0:T(8,128)} %param.12), kind=kLoop, calls=%fused_computation.1 | loop fusion | bytes 1179648 | tf_op jit(solution)/shard_map/stack;squeeze | solution.py:301
  1.9 3.0 %collective-permute-start = (f32[2,3,3,32,256]{4,3,2,1,0:T(8,128)S(1)}, f32[2,3,3,32,256]{4,3,2,1,0:T(8,128)S(1)}, u32[]{:S(2)}, u32[]{:S(2)}) collective-permute-start(f32[2,3,3,32,256]{4,3,2,1,0:T(8,128)S(1)} %pad_maximum_fusion), channel_id=1, source_target_pairs={{0,4},{4,8},{8,12},{12,16},{16,20},{20,24},{24,28},{28,0},{1,5},{5... | collective-permute-start | bytes 1769480 | tf_op jit(solution)/shard_map/ppermute | solution.py:294
  5.0 1.4 %copy-done.2 = f32[8,3,2,32,256]{4,3,2,1,0:T(8,128)S(1)} copy-done((f32[8,3,2,32,256]{4,3,2,1,0:T(8,128)S(1)}, f32[8,3,2,32,256]{4,3,2,1,0:T(8,128)}, u32[]{:S(2)}) %copy-start.2) | copy-done | bytes 1572888
  6.4 5.5 %face_gather.1 = (f32[8,6,8,128]{3,2,1,0:T(8,128)}, f32[2,3,3,32,256]{4,3,2,1,0:T(8,128)}, f32[2,4,3,32,256]{4,3,2,1,0:T(8,128)S(1)}, f32[2,4,3,32,256]{4,3,2,1,...) custom-call(s32[8,128]{1,0:T(8,128)S(1)} %bitcast.25, s32[8,128]{1,0:T(8,128)S(1)} %bitcast.27, ...), custom_call_target="tpu_custom_call" | custom-call | flops 1000 | bytes 1000 | tf_op jit(solution)/shard_map/face_gather/pallas_call | solution.py:317
  11.8 0.9 copy-done.11
  12.7 0.9 %copy-done.12 = f32[2,4,3,32,256]{4,3,2,1,0:T(8,128)} copy-done((f32[2,4,3,32,256]{4,3,2,1,0:T(8,128)}, f32[2,4,3,32,256]{4,3,2,1,0:T(8,128)S(1)}, u32[]{:S(2)}) %copy-start.12) | copy-done | bytes 786456
  13.7 4.9 %all-to-all-start = ((f32[8,6,8,128]{3,2,1,0:T(8,128)}), f32[8,6,8,128]{3,2,1,0:T(8,128)}, u32[]{:S(2)}, u32[]{:S(2)}) async-start(f32[8,6,8,128]{3,2,1,0:T(8,128)} %get-tuple-element.28), calls=%async_computation | async-start | bytes 393216 | tf_op jit(solution)/shard_map/all_to_all | solution.py:339
  18.5 4.7 %collective-permute-start.1 = (f32[2,3,3,32,256]{4,3,2,1,0:T(8,128)}, f32[2,3,3,32,256]{4,3,2,1,0:T(8,128)}, u32[]{:S(2)}, u32[]{:S(2)}) collective-permute-start(f32[2,3,3,32,256]{4,3,2,1,0:T(8,128)} %get-tuple-element.29), channel_id=1, source_target_pairs={{4,0},{8,4},{12,8},{16,12},{20,16},{24,20},{28,24},{0,28},{5,1},{9... | collective-permute-start | bytes 1769480 | tf_op jit(solution)/shard_map/ppermute | solution.py:295
  23.3 0.0 copy-start.17
  23.3 0.0 copy-start.18
  23.3 0.0 copy-start.19
  23.3 0.8 copy-done.13
  24.1 3.0 %all-to-all-done.arrived_ref = f32[8,6,8,128]{3,2,1,0:T(8,128)} async-done(((f32[8,6,8,128]{3,2,1,0:T(8,128)}), f32[8,6,8,128]{3,2,1,0:T(8,128)}, u32[]{:S(2)}, u32[]{:S(2)}) %all-to-all-start) | async-done | bytes 196640 | tf_op jit(solution)/shard_map/all_to_all | solution.py:339
  27.1 1.4 %pair_difference.1 = f32[64,256]{1,0:T(8,128)S(1)} custom-call(s32[2,256]{1,0:T(2,128)S(1)} %copy-done.9, s32[16,256]{1,0:T(8,128)S(1)} %copy-done.4, f32[8,128]{1,0:T(8,128)S(1)} %first_piece_arrived.1.mark_ref, f32[8,6,8,128]{3,2,1,0:T(8,128)} %all-to-all-done.arrived_ref), custom_call_target="tpu_custom_call" | custom-call | flops 1000 | bytes 1000 | tf_op jit(solution)/shard_map/pair_difference/pallas_call | solution.py:355
  28.5 5.8 %all-gather = f32[256,256]{1,0:T(8,128)S(1)} all-gather(f32[64,256]{1,0:T(8,128)S(1)} %pair_difference.1), channel_id=2, replica_groups=mesh['mesh'=8,'harm'=4] {'harm'}, dimensions={0}, use_global_device_ids=true | all-gather | bytes 327680 | tf_op jit(solution)/shard_map/all_gather | solution.py:364
  34.3 0.0 copy-start.3
  34.3 0.0 copy-start.15
  34.4 2.8 %pair_force.1 = f32[8,6,8,128]{3,2,1,0:T(8,128)} custom-call(s32[1]{0:T(128)} %bitcast.place_ref, s32[2,256]{1,0:T(2,128)S(1)} %copy-done.9, f32[1,256]{1,0:T(1,128)S(1)} %bitcast.32, f32[64,32]{1,0:T(8,128)S(1)} %copy-done.18, f32[4,8,64]{2,1,0:T(8,128)S(1)} %copy-done.19, f32[4,64,256]{2,1,0:T(8,128)S(1)} %bitcast.24), custom_call_target="tpu_custom_call" | custom-call | flops 999999995904 | bytes 10000000000 | tf_op jit(solution)/shard_map/pair_force/pallas_call | solution.py:367
  37.2 3.4 %all-to-all-start.1 = ((f32[8,6,8,128]{3,2,1,0:T(8,128)}), f32[8,6,8,128]{3,2,1,0:T(8,128)S(1)}, u32[]{:S(2)}, u32[]{:S(2)}) async-start(f32[8,6,8,128]{3,2,1,0:T(8,128)} %pair_force.1), calls=%async_computation.1 | async-start | bytes 393216 | tf_op jit(solution)/shard_map/all_to_all | solution.py:339
  40.6 1.9 %collective-permute-start.4 = (f32[2,4,3,32,256]{4,3,2,1,0:T(8,128)}, f32[2,4,3,32,256]{4,3,2,1,0:T(8,128)}, u32[]{:S(2)}, u32[]{:S(2)}) collective-permute-start(f32[2,4,3,32,256]{4,3,2,1,0:T(8,128)} %copy-done.12), channel_id=1, source_target_pairs={{0,4},{4,8},{8,12},{12,16},{16,20},{20,24},{24,28},{28,0},{1,5},{5... | collective-permute-start | bytes 2359304 | tf_op jit(solution)/shard_map/ppermute | solution.py:294
  42.5 2.9 %collective-permute-start.5 = (f32[2,4,3,32,256]{4,3,2,1,0:T(8,128)}, f32[2,4,3,32,256]{4,3,2,1,0:T(8,128)}, u32[]{:S(2)}, u32[]{:S(2)}) collective-permute-start(f32[2,4,3,32,256]{4,3,2,1,0:T(8,128)} %copy-done.11), channel_id=1, source_target_pairs={{4,0},{8,4},{12,8},{16,12},{20,16},{24,20},{28,24},{0,28},{5,1},{9... | collective-permute-start | bytes 2359304 | tf_op jit(solution)/shard_map/ppermute | solution.py:295
  45.4 4.3 %all-to-all-done.1.back_ref = f32[8,6,8,128]{3,2,1,0:T(8,128)S(1)} async-done(((f32[8,6,8,128]{3,2,1,0:T(8,128)}), f32[8,6,8,128]{3,2,1,0:T(8,128)S(1)}, u32[]{:S(2)}, u32[]{:S(2)}) %all-to-all-start.1) | async-done | bytes 196640 | tf_op jit(solution)/shard_map/all_to_all | solution.py:339
  49.7 1.4 %copy-done.10 = f32[8,3,2,32,256]{4,3,2,1,0:T(8,128)S(1)} copy-done((f32[8,3,2,32,256]{4,3,2,1,0:T(8,128)S(1)}, f32[8,3,2,32,256]{4,3,2,1,0:T(8,128)}, u32[]{:S(2)}) %copy-start.10) | copy-done | bytes 1572888
  51.1 1.1 %copy-done.14 = f32[2,3,3,32,256]{4,3,2,1,0:T(8,128)S(1)} copy-done((f32[2,3,3,32,256]{4,3,2,1,0:T(8,128)S(1)}, f32[2,3,3,32,256]{4,3,2,1,0:T(8,128)}, u32[]{:S(2)}) %copy-start.14) | copy-done | bytes 589848
  52.2 7.8 %combine_terms.1 = (f32[8,3,64,256]{3,2,1,0:T(8,128)}, f32[8,3,64,256]{3,2,1,0:T(8,128)}, f32[5,3,64,256]{3,2,1,0:T(8,128)S(1)}, f32[5,3,64,256]{3,2,1,0:T(8,128)S(1)}) custom-call(s32[1]{0:T(128)} %bitcast.place_ref, s32[8,128]{1,0:T(8,128)S(1)} %bitcast.26, s32[8,128]{1,0:T(8,128)S(1)} %bitcast.28, f32[8,6,8,128]{3,2,1,0:T(8,128)S(1)} %all-to-all-done.1.back_ref, ...), custom_call_target="tpu_custom_call" | custom-call | flops 999999995904 | bytes 10000000000 | tf_op jit(solution)/shard_map/combine_terms/pallas_call | solution.py:390
  60.0 21.6 %collective-permute-start.2 = (f32[2,1,3,32,256]{4,3,2,1,0:T(8,128)}, f32[2,1,3,32,256]{4,3,2,1,0:T(8,128)}, u32[]{:S(2)}, u32[]{:S(2)}) collective-permute-start(f32[2,1,3,32,256]{4,3,2,1,0:T(8,128)} %get-tuple-element.40), channel_id=1, source_target_pairs={{0,4},{4,8},{8,12},{12,16},{16,20},{20,24},{24,28},{28,0},{1,5},{5... | collective-permute-start | bytes 589832 | tf_op jit(solution)/shard_map/ppermute | solution.py:294
  81.7 3.3 %collective-permute-done.5.refs_3_ = f32[2,4,3,32,256]{4,3,2,1,0:T(8,128)} collective-permute-done((f32[2,4,3,32,256]{4,3,2,1,0:T(8,128)}, f32[2,4,3,32,256]{4,3,2,1,0:T(8,128)}, u32[]{:S(2)}, u32[]{:S(2)}) %collective-permute-start.5) | collective-permute-done | bytes 786464 | tf_op jit(solution)/shard_map/ppermute | solution.py:295
  85.0 3.1 %edge_terms.2 = (f32[8,3,64,256]{3,2,1,0:T(8,128)}, f32[8,3,64,256]{3,2,1,0:T(8,128)}) custom-call(f32[5,3,64,256]{3,2,1,0:T(8,128)S(1)} %get-tuple-element.35.refs_0_, f32[5,3,64,256]{3,2,1,0:T(8,128)S(1)} %get-tuple-element.36.refs_1_, f32[2,4,3,32,256]{4,3,2,1,0:T(8,128)} %collective-permute-done.4.refs_2_, ...), custom_call_target="tpu_custom_call", output_to_operand_aliasing={{0}: (4, {}), {1}: (5, {})} | custom-call | flops 999999995904 | bytes 10000000000 | tf_op jit(solution)/shard_map/edge_terms/pallas_call | solution.py:425
  88.0 0.6 collective-permute-done.3.refs_3_
  88.7 1.8 %edge_terms.3 = (f32[8,3,64,256]{3,2,1,0:T(8,128)}, f32[8,3,64,256]{3,2,1,0:T(8,128)}) custom-call(f32[5,3,64,256]{3,2,1,0:T(8,128)S(1)} %get-tuple-element.35.refs_0_, f32[5,3,64,256]{3,2,1,0:T(8,128)S(1)} %get-tuple-element.36.refs_1_, f32[2,1,3,32,256]{4,3,2,1,0:T(8,128)} %collective-permute-done.2.refs_2_, ...), custom_call_target="tpu_custom_call", output_to_operand_aliasing={{0}: (4, {}), {1}: (5, {})} | custom-call | flops 1000 | bytes 1000 | tf_op jit(solution)/shard_map/edge_terms/pallas_call | solution.py:425
  (34 shorter events, 0.1 us)
Async XLA Ops:
  0.6 4.3 %copy-start = (f32[8,3,2,32,256]{4,3,2,1,0:T(8,128)S(1)}, f32[8,3,2,32,256]{4,3,2,1,0:T(8,128)}, u32[]{:S(2)}) copy-start(f32[8,3,2,32,256]{4,3,2,1,0:T(8,128)} %param.13) | copy-start | bytes 4718596
  0.6 4.3 %copy-start.7 = (s32[1024]{0:T(1024)S(1)}, s32[1024]{0:T(1024)}, u32[]{:S(2)}) copy-start(s32[1024]{0:T(1024)} %param.18) | copy-start | bytes 12292
  0.7 4.3 %copy-start.5 = (s32[1024]{0:T(1024)S(1)}, s32[1024]{0:T(1024)}, u32[]{:S(2)}) copy-start(s32[1024]{0:T(1024)} %param.17) | copy-start | bytes 12292
  1.9 21.3 %collective-permute-start = (f32[2,3,3,32,256]{4,3,2,1,0:T(8,128)S(1)}, f32[2,3,3,32,256]{4,3,2,1,0:T(8,128)S(1)}, u32[]{:S(2)}, u32[]{:S(2)}) collective-permute-start(f32[2,3,3,32,256]{4,3,2,1,0:T(8,128)S(1)} %pad_maximum_fusion), channel_id=1, source_target_pairs={{0,4},{4,8},{8,12},{12,16},{16,20},{20,24},{24,28},{28,0},{1,5},{5... | collective-permute-start | bytes 1769480 | tf_op jit(solution)/shard_map/ppermute | solution.py:294
  5.0 1.4 %copy-start.2 = (f32[8,3,2,32,256]{4,3,2,1,0:T(8,128)S(1)}, f32[8,3,2,32,256]{4,3,2,1,0:T(8,128)}, u32[]{:S(2)}) copy-start(f32[8,3,2,32,256]{4,3,2,1,0:T(8,128)} %param.12) | copy-start | bytes 4718596
  11.8 0.9 copy-start.11
  12.7 0.9 %copy-start.12 = (f32[2,4,3,32,256]{4,3,2,1,0:T(8,128)}, f32[2,4,3,32,256]{4,3,2,1,0:T(8,128)S(1)}, u32[]{:S(2)}) copy-start(f32[2,4,3,32,256]{4,3,2,1,0:T(8,128)S(1)} %get-tuple-element.42) | copy-start | bytes 2359300
  13.7 13.4 %all-to-all-start = ((f32[8,6,8,128]{3,2,1,0:T(8,128)}), f32[8,6,8,128]{3,2,1,0:T(8,128)}, u32[]{:S(2)}, u32[]{:S(2)}) async-start(f32[8,6,8,128]{3,2,1,0:T(8,128)} %get-tuple-element.28), calls=%async_computation | async-start | bytes 393216 | tf_op jit(solution)/shard_map/all_to_all | solution.py:339
  18.5 22.1 %collective-permute-start.1 = (f32[2,3,3,32,256]{4,3,2,1,0:T(8,128)}, f32[2,3,3,32,256]{4,3,2,1,0:T(8,128)}, u32[]{:S(2)}, u32[]{:S(2)}) collective-permute-start(f32[2,3,3,32,256]{4,3,2,1,0:T(8,128)} %get-tuple-element.29), channel_id=1, source_target_pairs={{4,0},{8,4},{12,8},{16,12},{20,16},{24,20},{28,24},{0,28},{5,1},{9... | collective-permute-start | bytes 1769480 | tf_op jit(solution)/shard_map/ppermute | solution.py:295
  23.3 0.8 copy-start.13
  23.3 3.8 %copy-start.4 = (s32[16,256]{1,0:T(8,128)S(1)}, s32[16,256]{1,0:T(8,128)}, u32[]{:S(2)}) copy-start(s32[16,256]{1,0:T(8,128)} %status_ref.1) | copy-start | bytes 49156
  23.3 3.8 %copy-start.9 = (s32[2,256]{1,0:T(2,128)S(1)}, s32[2,256]{1,0:T(2,128)}, u32[]{:S(2)}) copy-start(s32[2,256]{1,0:T(2,128)} %pairs_ref.3) | copy-start | bytes 6148
  23.3 11.0 %copy-start.17 = (f32[256]{0:T(256)S(1)}, f32[256]{0:T(256)}, u32[]{:S(2)}) copy-start(f32[256]{0:T(256)} %param.21) | copy-start | bytes 3076
  23.3 11.0 %copy-start.18 = (f32[64,32]{1,0:T(8,128)S(1)}, f32[64,32]{1,0:T(8,128)}, u32[]{:S(2)}) copy-start(f32[64,32]{1,0:T(8,128)} %constant.8.clone.table_ref) | copy-start | bytes 24580
  23.3 11.0 %copy-start.19 = (f32[4,8,64]{2,1,0:T(8,128)S(1)}, f32[4,8,64]{2,1,0:T(8,128)}, u32[]{:S(2)}) copy-start(f32[4,8,64]{2,1,0:T(8,128)} %constant.9.clone.back_ref) | copy-start | bytes 24580
  34.3 15.4 %copy-start.1 = (f32[8,3,2,32,256]{4,3,2,1,0:T(8,128)S(1)}, f32[8,3,2,32,256]{4,3,2,1,0:T(8,128)}, u32[]{:S(2)}) copy-start(f32[8,3,2,32,256]{4,3,2,1,0:T(8,128)} %param.13) | copy-start | bytes 4718596
  34.3 15.4 %copy-start.3 = (f32[8,3,2,32,256]{4,3,2,1,0:T(8,128)S(1)}, f32[8,3,2,32,256]{4,3,2,1,0:T(8,128)}, u32[]{:S(2)}) copy-start(f32[8,3,2,32,256]{4,3,2,1,0:T(8,128)} %param.12) | copy-start | bytes 4718596
  34.3 15.4 %copy-start.6 = (s32[1024]{0:T(1024)S(1)}, s32[1024]{0:T(1024)}, u32[]{:S(2)}) copy-start(s32[1024]{0:T(1024)} %param.17) | copy-start | bytes 12292
  34.3 15.3 %copy-start.8 = (s32[1024]{0:T(1024)S(1)}, s32[1024]{0:T(1024)}, u32[]{:S(2)}) copy-start(s32[1024]{0:T(1024)} %param.18) | copy-start | bytes 12292
  34.3 15.3 %copy-start.15 = (f32[2,32,256]{2,1,0:T(8,128)S(1)}, f32[2,32,256]{2,1,0:T(8,128)}, u32[]{:S(2)}) copy-start(f32[2,32,256]{2,1,0:T(8,128)} %param.15) | copy-start | bytes 196612
  34.4 15.3 %copy-start.16 = (f32[2,32,256]{2,1,0:T(8,128)S(1)}, f32[2,32,256]{2,1,0:T(8,128)}, u32[]{:S(2)}) copy-start(f32[2,32,256]{2,1,0:T(8,128)} %param.16) | copy-start | bytes 196612
  37.2 12.5 %all-to-all-start.1 = ((f32[8,6,8,128]{3,2,1,0:T(8,128)}), f32[8,6,8,128]{3,2,1,0:T(8,128)S(1)}, u32[]{:S(2)}, u32[]{:S(2)}) async-start(f32[8,6,8,128]{3,2,1,0:T(8,128)} %pair_force.1), calls=%async_computation.1 | async-start | bytes 393216 | tf_op jit(solution)/shard_map/all_to_all | solution.py:339
  40.6 41.1 %collective-permute-start.4 = (f32[2,4,3,32,256]{4,3,2,1,0:T(8,128)}, f32[2,4,3,32,256]{4,3,2,1,0:T(8,128)}, u32[]{:S(2)}, u32[]{:S(2)}) collective-permute-start(f32[2,4,3,32,256]{4,3,2,1,0:T(8,128)} %copy-done.12), channel_id=1, source_target_pairs={{0,4},{4,8},{8,12},{12,16},{16,20},{20,24},{24,28},{28,0},{1,5},{5... | collective-permute-start | bytes 2359304 | tf_op jit(solution)/shard_map/ppermute | solution.py:294
  42.5 42.5 %collective-permute-start.5 = (f32[2,4,3,32,256]{4,3,2,1,0:T(8,128)}, f32[2,4,3,32,256]{4,3,2,1,0:T(8,128)}, u32[]{:S(2)}, u32[]{:S(2)}) collective-permute-start(f32[2,4,3,32,256]{4,3,2,1,0:T(8,128)} %copy-done.11), channel_id=1, source_target_pairs={{4,0},{8,4},{12,8},{16,12},{20,16},{24,20},{28,24},{0,28},{5,1},{9... | collective-permute-start | bytes 2359304 | tf_op jit(solution)/shard_map/ppermute | solution.py:295
  49.7 1.4 %copy-start.10 = (f32[8,3,2,32,256]{4,3,2,1,0:T(8,128)S(1)}, f32[8,3,2,32,256]{4,3,2,1,0:T(8,128)}, u32[]{:S(2)}) copy-start(f32[8,3,2,32,256]{4,3,2,1,0:T(8,128)} %param.14) | copy-start | bytes 4718596
  51.1 1.1 %copy-start.14 = (f32[2,3,3,32,256]{4,3,2,1,0:T(8,128)S(1)}, f32[2,3,3,32,256]{4,3,2,1,0:T(8,128)}, u32[]{:S(2)}) copy-start(f32[2,3,3,32,256]{4,3,2,1,0:T(8,128)} %copy-done.13) | copy-start | bytes 1769476
  60.0 28.0 %collective-permute-start.2 = (f32[2,1,3,32,256]{4,3,2,1,0:T(8,128)}, f32[2,1,3,32,256]{4,3,2,1,0:T(8,128)}, u32[]{:S(2)}, u32[]{:S(2)}) collective-permute-start(f32[2,1,3,32,256]{4,3,2,1,0:T(8,128)} %get-tuple-element.40), channel_id=1, source_target_pairs={{0,4},{4,8},{8,12},{12,16},{16,20},{20,24},{24,28},{28,0},{1,5},{5... | collective-permute-start | bytes 589832 | tf_op jit(solution)/shard_map/ppermute | solution.py:294
  81.7 7.0 %collective-permute-start.3 = (f32[2,1,3,32,256]{4,3,2,1,0:T(8,128)}, f32[2,1,3,32,256]{4,3,2,1,0:T(8,128)}, u32[]{:S(2)}, u32[]{:S(2)}) collective-permute-start(f32[2,1,3,32,256]{4,3,2,1,0:T(8,128)} %get-tuple-element.41), channel_id=1, source_target_pairs={{4,0},{8,4},{12,8},{16,12},{20,16},{24,20},{28,24},{0,28},{5,1},{9... | collective-permute-start | bytes 589832 | tf_op jit(solution)/shard_map/ppermute | solution.py:295

commit v2 on v1

--- a/solution.py
+++ b/solution.py
@@ -16,7 +16,7 @@
 normal_penalty = 2.0
 shear_penalty = 1.0
 
-CUTS = (0, 3, 7, 8)
+CUTS = ((3, 0), (3, 4), (7, 7), (8, 8))
 VMEM = 28 * 1024 * 1024
 
 
@@ -163,31 +163,14 @@
             out_ref[block] = part
 
 
-def combine_kernel(
-    place_ref,
-    cells_ref,
-    send_ref,
-    back_ref,
-    below_ref,
-    above_ref,
-    stiff_ref,
-    mass_ref,
-    x_ref,
-    y_ref,
-    forcing_ref,
-    res_ref,
-    jac_ref,
-    late_res_ref,
-    late_jac_ref,
-    cell_ref,
-    low_ref,
-):
+def combine_kernel(place_ref, cells_ref, send_ref, back_ref, *refs, edges, late):
+    piece_refs = refs[: len(edges)]
+    stiff_ref, mass_ref, x_ref, y_ref, forcing_ref = refs[len(edges) : len(edges) + 5]
+    res_ref, jac_ref, late_res_ref, late_jac_ref, cell_ref, low_ref = refs[len(edges) + 5 :]
     comp = pl.program_id(0)
     coefs, _, rows, axial = x_ref.shape
     slots = cell_ref.shape[1]
     layer = rows // 2
-    early = below_ref.shape[1]
-
     @pl.when(comp == 0)
     def _():
         cell = slot_cells(cells_ref, send_ref)
@@ -230,21 +213,41 @@
             result = result + (frequency * damping_ratio) * mass * turned + contact[coef]
             if field == 0:
                 result = result - forcing_ref[coef, 0]
-            if coef < early:
-                out_ref[coef, 0, :layer] = result[:layer] - below_ref[field, coef, comp]
-                out_ref[coef, 0, layer:] = result[layer:] - above_ref[field, coef, comp]
-            else:
-                late_ref[coef - early, comp] = result
-
-
-def edge_kernel(late_res, late_jac, below, above, res_in, jac_in, res_ref, jac_ref, *, offset):
+            parts = [result[:layer], result[layer:]]
+            for piece_ref, (start, first, last) in zip(piece_refs, edges):
+                if first <= coef < last:
+                    side = 0 if start > 0 else 1
+                    parts[side] = parts[side] - piece_ref[field, coef - first, 0]
+            for side in (0, 1):
+                rows_of = pl.ds(side * layer, layer)
+                if coef < late:
+                    out_ref[coef, 0, rows_of] = parts[side]
+                else:
+                    late_ref[coef - late, comp, rows_of] = parts[side]
+
+
+def edge_kernel(late_res, late_jac, below, above, res_in, jac_in, res_ref, jac_ref, *refs, late, starts):
     del res_in, jac_in
-    layer = res_ref.shape[2] // 2
-    step = pl.program_id(0)
+    stage, sems = refs
+    first = min(starts)
+    count = stage.shape[1]
+    layer = stage.shape[3] // 2
+    copies = []
     for field, (late_ref, out_ref) in enumerate(((late_res, res_ref), (late_jac, jac_ref))):
-        value = late_ref[offset + step]
-        out_ref[0, :, :layer, :] = value[:, :layer] - below[field, step]
-        out_ref[0, :, layer:, :] = value[:, layer:] - above[field, step]
+        value = late_ref[first - late : first - late + count]
+        for piece, start, side in ((below, starts[0], 0), (above, starts[1], 1)):
+            rows = slice(side * layer, (side + 1) * layer)
+            skip = start - first
+            if skip > 0:
+                stage[field, :skip, :, rows] = value[:skip, :, rows]
+            stage[field, skip:, :, rows] = value[skip:, :, rows] - piece[field]
+        copy = pltpu.make_async_copy(
+            stage.at[field], out_ref.at[first : first + count], sems.at[field]
+        )
+        copy.start()
+        copies.append(copy)
+    for copy in copies:
+        copy.wait()
 
 
 def transform_table(time_count, coef_count):
@@ -294,13 +297,33 @@
     ahead = lambda piece: lax.ppermute(piece, "mesh", forward)
     behind = lambda piece: lax.ppermute(piece, "mesh", backward)
     keep = lambda value: pltpu.with_memory_space_constraint(value, pltpu.VMEM)
-
-    ends = [cut * coefs // 8 for cut in CUTS]
-    spans = list(zip(ends[:-1], ends[1:]))
-    early = ends[1]
-    first_piece = jnp.stack([field[:early, :, layers - 1] for field in (displacement, direction)])
-    below = [ahead(first_piece)]
-    above = []
+    stay = lambda value: pltpu.with_memory_space_constraint(value, pltpu.HBM)
+
+    groups = []
+    done = [0, 0]
+    for ends in CUTS:
+        group = []
+        for side, end in enumerate(ends):
+            last = end * coefs // 8
+            if last > done[side]:
+                group.append((radial * (1 - side), done[side], last))
+                done[side] = last
+        groups.append(group)
+    shift = lambda edge, piece: ahead(piece) if edge[0] > 0 else behind(piece)
+    pieces = [
+        [
+            shift(
+                edge,
+                jnp.stack(
+                    [
+                        field[edge[1] : edge[2], :, edge[0] // radial]
+                        for field in (displacement, direction)
+                    ]
+                ),
+            )
+            for edge in groups[0]
+        ]
+    ]
 
     x = displacement.reshape(coefs, comps, rows, axial)
     y = direction.reshape(coefs, comps, rows, axial)
@@ -311,8 +334,7 @@
     near_memory = pl.BlockSpec(memory_space=pltpu.VMEM)
     per_comp = pl.BlockSpec((coefs, 1, rows, axial), lambda comp: (0, comp, 0, 0))
 
-    edges = [(0, 0, early)]
-    edges += [(start, first, last) for first, last in spans[1:] for start in (radial, 0)]
+    edges = [edge for group in groups[1:] for edge in group]
     edge_shapes = [(2, last - first, comps, radial, axial) for _, first, last in edges]
     outgoing, *sent = pl.pallas_call(
         lambda *refs: gather_kernel(*refs, edges=edges),
@@ -323,7 +345,7 @@
             pl.BlockSpec(shape[:2] + (1,) + shape[3:], lambda comp: (0, 0, comp, 0, 0))
             for shape in edge_shapes
         ],
-        out_shape=[jax.ShapeDtypeStruct(shape, f32) for shape in [wire] + edge_shapes],
+        out_shape=[pltpu.HBM(shape, f32) for shape in [wire] + edge_shapes],
         scratch_shapes=[
             pltpu.VMEM((1, slots), jnp.int32),
             pltpu.VMEM((2 * axial, slots), jnp.bfloat16),
@@ -331,7 +353,7 @@
         compiler_params=params("arbitrary"),
         cost_estimate=SMALL,
         name="face_gather",
-    )(cells, send, x, y)
+    )(cells, send, stay(x), stay(y))
 
     def exchange(block):
         if not direct:
@@ -341,16 +363,23 @@
             block = block.transpose(1, 0, 2).reshape(wire)
         return block
 
-    outgoing, sent[0] = lax.optimization_barrier((outgoing, sent[0]))
+    queue = []
+    for group in groups[1:]:
+        queue.append(sent[: len(group)])
+        sent = sent[len(group) :]
+    send_group = lambda index: [
+        shift(edge, piece) for edge, piece in zip(groups[index], queue[index - 1])
+    ]
+    outgoing, queue[0] = lax.optimization_barrier((outgoing, queue[0]))
     mark = pl.pallas_call(
         mark_kernel,
-        in_specs=[near_memory],
+        in_specs=[pl.BlockSpec(memory_space=pl.ANY)],
         out_specs=near_memory,
         out_shape=pltpu.VMEM((8, LANES), f32),
         cost_estimate=LARGE,
         name="first_piece_arrived",
-    )(keep(below[0]))
-    above.append(behind(sent[0]))
+    )(pieces[0][-1])
+    pieces.append(send_group(1))
     arrived = exchange(outgoing)
     own_opening = pl.pallas_call(
         opening_kernel,
@@ -381,17 +410,22 @@
         name="pair_force",
     )(place, pair_rows, crack_gap.reshape(1, pairs), jnp.asarray(table), jnp.asarray(back), everything)
     returned = exchange(slot_force)
-    above[0], sent[1:], _ = lax.optimization_barrier((above[0], sent[1:], slot_force))
-    below.append(ahead(sent[1]))
-    above.append(behind(sent[2]))
+    pieces[1], queue[1:], _ = lax.optimization_barrier((pieces[1], queue[1:], slot_force))
+    pieces.append(send_group(2))
 
     flat = jax.ShapeDtypeStruct(x.shape, f32)
-    late_shape = pltpu.VMEM((coefs - early, comps, rows, axial), f32)
+    piece_spec = lambda piece: pl.BlockSpec(
+        piece.shape[:2] + (1,) + piece.shape[3:], lambda comp: (0, 0, comp, 0, 0)
+    )
+    early = groups[0] + groups[1]
+    late = min(group[1] for group in groups[2])
+    late_shape = pltpu.VMEM((coefs - late, comps, rows, axial), f32)
     residual, product, late_res, late_jac = pl.pallas_call(
-        combine_kernel,
+        lambda *refs: combine_kernel(*refs, edges=early, late=late),
         grid=(comps,),
         in_specs=[scalar, whole(cells.shape), whole(send.shape)]
-        + [near_memory] * 3
+        + [near_memory]
+        + [piece_spec(piece) for piece in pieces[0] + pieces[1]]
         + [whole((rows, axial))] * 2
         + [per_comp] * 3,
         out_specs=[per_comp] * 2 + [near_memory] * 2,
@@ -408,31 +442,34 @@
         cells,
         send,
         keep(returned),
-        keep(below[0]),
-        keep(above[0]),
+        *pieces[0],
+        *pieces[1],
         stiffness.reshape(rows, axial),
         lumped_mass.reshape(rows, axial),
-        x,
-        y,
-        forcing.reshape(x.shape),
+        stay(x),
+        stay(y),
+        stay(forcing.reshape(x.shape)),
     )
-    residual, sent[3:] = lax.optimization_barrier((residual, sent[3:]))
-    below.append(ahead(sent[3]))
-    above.append(behind(sent[4]))
-
-    for (first, last), low_edge, high_edge in zip(spans[1:], below[1:], above[1:]):
-        mine = pl.BlockSpec((1, comps, rows, axial), lambda i, first=first: (first + i, 0, 0, 0))
+    residual, queue[2] = lax.optimization_barrier((residual, queue[2]))
+    pieces.append(send_group(3))
+
+    for group, piece in zip(groups[2:], pieces[2:]):
+        starts = [edge[1] for edge in group]
+        last = group[0][2]
         residual, product = pl.pallas_call(
-            lambda *refs, offset=first - early: edge_kernel(*refs, offset=offset),
-            grid=(last - first,),
+            lambda *refs, starts=starts: edge_kernel(*refs, late=late, starts=starts),
             in_specs=[near_memory] * 4 + [pl.BlockSpec(memory_space=pl.ANY)] * 2,
-            out_specs=[mine] * 2,
+            out_specs=[pl.BlockSpec(memory_space=pl.ANY)] * 2,
             out_shape=[flat, flat],
             input_output_aliases={4: 0, 5: 1},
-            compiler_params=params("arbitrary"),
+            scratch_shapes=[
+                pltpu.VMEM((2, last - min(starts), comps, rows, axial), f32),
+                pltpu.SemaphoreType.DMA((2,)),
+            ],
+            compiler_params=params(),
             cost_estimate=LARGE if last < coefs else SMALL,
             name="edge_terms",
-        )(keep(late_res), keep(late_jac), keep(low_edge), keep(high_edge), residual, product)
+        )(keep(late_res), keep(late_jac), *[keep(value) for value in piece], residual, product)
     return residual.reshape(displacement.shape), product.reshape(displacement.shape)
 
 

time: 91 us -> 84.7 us (0.931)
  starting transfers between devices: 42.4 us -> 23.8 us
  waiting for transfers between devices: 11.2 us -> 28.6 us
  local copies, waits for them, and re-layouts: 7.75 us -> 1.98 us
    ppermute x3, starting transfers between devices: 26.6 us -> 3.74 us  [on_device(): ahead = lambda piece: lax.ppermute(piece, 'mesh', forward)]
    ppermute x3, waiting for transfers between devices: 3.93 us -> 21.5 us  [on_device(): behind = lambda piece: lax.ppermute(piece, 'mesh', backward)]
    unnamed x40 -> x26, local copies, waits for them, and re-layouts: 6.54 us -> 0.88 us
    ppermute x3, starting transfers between devices: 7.59 us -> 11.7 us  [on_device(): behind = lambda piece: lax.ppermute(piece, 'mesh', backward)]
    pallas_call x1, Pallas kernels: 5.47 us -> 6.64 us  [on_device(): pl.pallas_call(lambda *refs: gather_kernel(*refs, edges=edges), grid=(com...]
  transfers between devices with their start and end apart: 8 -> 8, of which waited for: 4 -> 7; matrix products, arithmetic and copies ran while one was open for 0% -> 0% of each run, Pallas kernels for 23% -> 25%
where the time goes in v2:
time: 84.7 us; the launch traced here: 84.2 us
  waiting for transfers between devices  28.6 us (34%)
  starting transfers between devices  23.8 us (28%)
  Pallas kernels  23.2 us (27%)
  blocking collectives  5.79 us (7%)
  local copies, waits for them, and re-layouts  1.98 us (2%)
    ppermute x3, waiting for transfers between devices, on_device(): behind = lambda piece: lax.ppermute(piece, 'mesh', backward)  21.5 us
    ppermute x3, starting transfers between devices, on_device(): behind = lambda piece: lax.ppermute(piece, 'mesh', backward)  11.7 us
    all_to_all x2, starting transfers between devices, exchange(): lax.all_to_all(block, 'mesh', split_axis=0, concat_axis=0, tiled=True)  8.36 us
    pallas_call x1, Pallas kernels, on_device(): pl.pallas_call(lambda *refs: combine_kernel(*refs, edges=early, late=late...  8.01 us
    all_to_all x2, waiting for transfers between devices, exchange(): lax.all_to_all(block, 'mesh', split_axis=0, concat_axis=0, tiled=True)  6.69 us
    pallas_call x1, Pallas kernels, on_device(): pl.pallas_call(lambda *refs: gather_kernel(*refs, edges=edges), grid=(com...  6.64 us
    all_gather x1, blocking collectives, on_device(): everything = lax.all_gather(own_opening, 'harm')  5.79 us
    pallas_call x2, Pallas kernels, on_device(): pl.pallas_call(lambda *refs, starts=starts: edge_kernel(*refs, late=late,...  4.33 us
  transfers between devices with their start and end apart: 8, of which 7 were waited for; matrix products, arithmetic and copies ran while one was open for 0% of the time, Pallas kernels for 25%

profile of v2, /device:TPU:0, one launch (start us, length us, event | category | flops | bytes accessed | tf_op | source)
XLA Modules:
  0.0 84.2 jit_solution(16505114063020140919)
XLA Ops:
  0.6 0.0 copy-start.3
  0.6 0.0 copy-start.1
  0.7 1.1 %slice_bitcast_fusion = (f32[1,3,3,32,256]{4,3,2,1,0:T(8,128)S(1)}, f32[1,3,3,32,256]{4,3,2,1,0:T(8,128)S(1)}) fusion(f32[8,3,2,32,256]{4,3,2,1,0:T(8,128)} %param.13, f32[8,3,2,32,256]{4,3,2,1,0:T(8,128)} %param.12), kind=kLoop, calls=%fused_computation.1 | loop fusion | bytes 1179648 | tf_op jit(solution)/shard_map/stack;squeeze | solution.py:317
  1.8 3.0 %collective-permute-start = (f32[2,3,3,32,256]{4,3,2,1,0:T(8,128)S(1)}, f32[2,3,3,32,256]{4,3,2,1,0:T(8,128)S(1)}, u32[]{:S(2)}, u32[]{:S(2)}) collective-permute-start(f32[2,3,3,32,256]{4,3,2,1,0:T(8,128)S(1)} %pad_maximum_fusion), channel_id=1, source_target_pairs={{0,4},{4,8},{8,12},{12,16},{16,20},{20,24},{24,28},{28,0},{1,5},{5... | collective-permute-start | bytes 1769480 | tf_op jit(solution)/shard_map/ppermute | solution.py:297
  4.8 6.6 %face_gather.1 = (f32[8,6,8,128]{3,2,1,0:T(8,128)}, f32[2,4,3,32,256]{4,3,2,1,0:T(8,128)}, f32[2,4,3,32,256]{4,3,2,1,0:T(8,128)}, f32[2,3,3,32,256]{4,3,2,1,0:T(...) custom-call(s32[8,128]{1,0:T(8,128)S(1)} %bitcast.21, s32[8,128]{1,0:T(8,128)S(1)} %bitcast.23, ...), custom_call_target="tpu_custom_call" | custom-call | flops 1000 | bytes 1000 | tf_op jit(solution)/shard_map/face_gather/pallas_call | solution.py:339
  11.5 4.9 %all-to-all-start = ((f32[8,6,8,128]{3,2,1,0:T(8,128)}), f32[8,6,8,128]{3,2,1,0:T(8,128)}, u32[]{:S(2)}, u32[]{:S(2)}) async-start(f32[8,6,8,128]{3,2,1,0:T(8,128)} %get-tuple-element.28), calls=%async_computation | async-start | bytes 393216 | tf_op jit(solution)/shard_map/all_to_all | solution.py:361
  16.4 4.7 %collective-permute-start.1 = (f32[2,4,3,32,256]{4,3,2,1,0:T(8,128)}, f32[2,4,3,32,256]{4,3,2,1,0:T(8,128)}, u32[]{:S(2)}, u32[]{:S(2)}) collective-permute-start(f32[2,4,3,32,256]{4,3,2,1,0:T(8,128)} %get-tuple-element.29), channel_id=1, source_target_pairs={{4,0},{8,4},{12,8},{16,12},{20,16},{24,20},{28,24},{0,28},{5,1},{9... | collective-permute-start | bytes 2359304 | tf_op jit(solution)/shard_map/ppermute | solution.py:298
  21.1 0.4 collective-permute-done.piece_ref.refs_4_
  21.5 0.8 copy-done.6
  22.3 0.0 copy-start.12
  22.3 2.6 %all-to-all-done.arrived_ref = f32[8,6,8,128]{3,2,1,0:T(8,128)} async-done(((f32[8,6,8,128]{3,2,1,0:T(8,128)}), f32[8,6,8,128]{3,2,1,0:T(8,128)}, u32[]{:S(2)}, u32[]{:S(2)}) %all-to-all-start) | async-done | bytes 196640 | tf_op jit(solution)/shard_map/all_to_all | solution.py:361
  24.9 1.4 %pair_difference.1 = f32[64,256]{1,0:T(8,128)S(1)} custom-call(s32[2,256]{1,0:T(2,128)S(1)} %copy-done.5, s32[16,256]{1,0:T(8,128)S(1)} %copy-done, f32[8,128]{1,0:T(8,128)S(1)} %first_piece_arrived.1.mark_ref, f32[8,6,8,128]{3,2,1,0:T(8,128)} %all-to-all-done.arrived_ref), custom_call_target="tpu_custom_call" | custom-call | flops 1000 | bytes 1000 | tf_op jit(solution)/shard_map/pair_difference/pallas_call | solution.py:384
  26.3 5.8 %all-gather = f32[256,256]{1,0:T(8,128)S(1)} all-gather(f32[64,256]{1,0:T(8,128)S(1)} %pair_difference.1), channel_id=2, replica_groups=mesh['mesh'=8,'harm'=4] {'harm'}, dimensions={0}, use_global_device_ids=true | all-gather | bytes 327680 | tf_op jit(solution)/shard_map/all_gather | solution.py:393
  32.1 0.0 copy-start.4
  32.1 0.0 copy-start.7
  32.2 0.0 copy-start.8
  32.2 0.0 copy-start.9
  32.2 2.8 %pair_force.1 = f32[8,6,8,128]{3,2,1,0:T(8,128)} custom-call(s32[1]{0:T(128)} %bitcast.place_ref.refs_0_, s32[2,256]{1,0:T(2,128)S(1)} %copy-done.5, f32[1,256]{1,0:T(1,128)S(1)} %bitcast.27, f32[64,32]{1,0:T(8,128)S(1)} %copy-done.11, f32[4,8,64]{2,1,0:T(8,128)S(1)} %copy-done.12, f32[4,64,256]{2,1,0:T(8,128)S(1)} %bitcast.20), custom_call_target="tpu_custom_call" | custom-call | flops 999999995904 | bytes 10000000000 | tf_op jit(solution)/shard_map/pair_force/pallas_call | solution.py:396
  35.0 3.5 %all-to-all-start.1 = ((f32[8,6,8,128]{3,2,1,0:T(8,128)}), f32[8,6,8,128]{3,2,1,0:T(8,128)S(1)}, u32[]{:S(2)}, u32[]{:S(2)}) async-start(f32[8,6,8,128]{3,2,1,0:T(8,128)} %pair_force.1), calls=%async_computation.1 | async-start | bytes 393216 | tf_op jit(solution)/shard_map/all_to_all | solution.py:361
  38.5 1.8 %collective-permute-done.1.refs_5_ = f32[2,4,3,32,256]{4,3,2,1,0:T(8,128)} collective-permute-done((f32[2,4,3,32,256]{4,3,2,1,0:T(8,128)}, f32[2,4,3,32,256]{4,3,2,1,0:T(8,128)}, u32[]{:S(2)}, u32[]{:S(2)}) %collective-permute-start.1) | collective-permute-done | bytes 786464 | tf_op jit(solution)/shard_map/ppermute | solution.py:298
  40.3 2.9 %collective-permute-start.5 = (f32[2,3,3,32,256]{4,3,2,1,0:T(8,128)}, f32[2,3,3,32,256]{4,3,2,1,0:T(8,128)}, u32[]{:S(2)}, u32[]{:S(2)}) collective-permute-start(f32[2,3,3,32,256]{4,3,2,1,0:T(8,128)} %get-tuple-element.43), channel_id=1, source_target_pairs={{4,0},{8,4},{12,8},{16,12},{20,16},{24,20},{28,24},{0,28},{5,1},{9... | collective-permute-start | bytes 1769480 | tf_op jit(solution)/shard_map/ppermute | solution.py:298
  43.2 0.0 collective-permute-start.4
  43.2 4.1 %all-to-all-done.1.refs_3_ = f32[8,6,8,128]{3,2,1,0:T(8,128)S(1)} async-done(((f32[8,6,8,128]{3,2,1,0:T(8,128)}), f32[8,6,8,128]{3,2,1,0:T(8,128)S(1)}, u32[]{:S(2)}, u32[]{:S(2)}) %all-to-all-start.1) | async-done | bytes 196640 | tf_op jit(solution)/shard_map/all_to_all | solution.py:361
  47.3 8.0 %combine_terms.1 = (f32[8,3,64,256]{3,2,1,0:T(8,128)}, f32[8,3,64,256]{3,2,1,0:T(8,128)}, f32[5,3,64,256]{3,2,1,0:T(8,128)S(1)}, f32[5,3,64,256]{3,2,1,0:T(8,128)S(1)}) custom-call(s32[1]{0:T(128)} %bitcast.place_ref.refs_0_, s32[8,128]{1,0:T(8,128)S(1)} %bitcast.22, s32[8,128]{1,0:T(8,128)S(1)} %bitcast.24, f32[8,6,8,128]{3,2,1,0:T(8,128)S(1)} %all-to-all-done.1.refs_3_, ...), custom_call_target="tpu_custom_call" | custom-call | flops 999999995904 | bytes 10000000000 | tf_op jit(solution)/shard_map/combine_terms/pallas_call | solution.py:423
  55.4 0.7 collective-permute-start.2
  56.1 4.0 %collective-permute-start.3 = (f32[2,1,3,32,256]{4,3,2,1,0:T(8,128)}, f32[2,1,3,32,256]{4,3,2,1,0:T(8,128)}, u32[]{:S(2)}, u32[]{:S(2)}) collective-permute-start(f32[2,1,3,32,256]{4,3,2,1,0:T(8,128)} %get-tuple-element.41), channel_id=1, source_target_pairs={{4,0},{8,4},{12,8},{16,12},{20,16},{24,20},{28,24},{0,28},{5,1},{9... | collective-permute-start | bytes 589832 | tf_op jit(solution)/shard_map/ppermute | solution.py:298
  60.1 18.5 %collective-permute-done.5.refs_3_ = f32[2,3,3,32,256]{4,3,2,1,0:T(8,128)} collective-permute-done((f32[2,3,3,32,256]{4,3,2,1,0:T(8,128)}, f32[2,3,3,32,256]{4,3,2,1,0:T(8,128)}, u32[]{:S(2)}, u32[]{:S(2)}) %collective-permute-start.5) | collective-permute-done | bytes 589856 | tf_op jit(solution)/shard_map/ppermute | solution.py:298
  78.6 0.0 collective-permute-done.4.refs_2_
  78.6 2.5 %edge_terms.2 = (f32[8,3,64,256]{3,2,1,0:T(8,128)}, f32[8,3,64,256]{3,2,1,0:T(8,128)}) custom-call(f32[5,3,64,256]{3,2,1,0:T(8,128)S(1)} %get-tuple-element.35.refs_0_, f32[5,3,64,256]{3,2,1,0:T(8,128)S(1)} %get-tuple-element.36.refs_1_, f32[2,4,3,32,256]{4,3,2,1,0:T(8,128)} %collective-permute-done.4.refs_2_, ...), custom_call_target="tpu_custom_call", output_to_operand_aliasing={{0}: (4, {}), {1}: (5, {})} | custom-call | flops 999999995904 | bytes 10000000000 | tf_op jit(solution)/shard_map/edge_terms/pallas_call | solution.py:459
  81.2 0.1 collective-permute-done.2.refs_2_
  81.3 1.1 %collective-permute-done.3.refs_3_ = f32[2,1,3,32,256]{4,3,2,1,0:T(8,128)} collective-permute-done((f32[2,1,3,32,256]{4,3,2,1,0:T(8,128)}, f32[2,1,3,32,256]{4,3,2,1,0:T(8,128)}, u32[]{:S(2)}, u32[]{:S(2)}) %collective-permute-start.3) | collective-permute-done | bytes 196640 | tf_op jit(solution)/shard_map/ppermute | solution.py:298
  82.4 1.8 %edge_terms.3 = (f32[8,3,64,256]{3,2,1,0:T(8,128)}, f32[8,3,64,256]{3,2,1,0:T(8,128)}) custom-call(f32[5,3,64,256]{3,2,1,0:T(8,128)S(1)} %get-tuple-element.35.refs_0_, f32[5,3,64,256]{3,2,1,0:T(8,128)S(1)} %get-tuple-element.36.refs_1_, f32[2,1,3,32,256]{4,3,2,1,0:T(8,128)} %collective-permute-done.2.refs_2_, ...), custom_call_target="tpu_custom_call", output_to_operand_aliasing={{0}: (4, {}), {1}: (5, {})} | custom-call | flops 1000 | bytes 1000 | tf_op jit(solution)/shard_map/edge_terms/pallas_call | solution.py:459
  (20 shorter events, 0.1 us)
Async XLA Ops:
  0.6 4.2 %copy-start.3 = (s32[1024]{0:T(1024)S(1)}, s32[1024]{0:T(1024)}, u32[]{:S(2)}) copy-start(s32[1024]{0:T(1024)} %param.18) | copy-start | bytes 12292
  0.6 4.2 %copy-start.1 = (s32[1024]{0:T(1024)S(1)}, s32[1024]{0:T(1024)}, u32[]{:S(2)}) copy-start(s32[1024]{0:T(1024)} %param.17) | copy-start | bytes 12292
  1.8 19.6 %collective-permute-start = (f32[2,3,3,32,256]{4,3,2,1,0:T(8,128)S(1)}, f32[2,3,3,32,256]{4,3,2,1,0:T(8,128)S(1)}, u32[]{:S(2)}, u32[]{:S(2)}) collective-permute-start(f32[2,3,3,32,256]{4,3,2,1,0:T(8,128)S(1)} %pad_maximum_fusion), channel_id=1, source_target_pairs={{0,4},{4,8},{8,12},{12,16},{16,20},{20,24},{24,28},{28,0},{1,5},{5... | collective-permute-start | bytes 1769480 | tf_op jit(solution)/shard_map/ppermute | solution.py:297
  11.5 13.4 %all-to-all-start = ((f32[8,6,8,128]{3,2,1,0:T(8,128)}), f32[8,6,8,128]{3,2,1,0:T(8,128)}, u32[]{:S(2)}, u32[]{:S(2)}) async-start(f32[8,6,8,128]{3,2,1,0:T(8,128)} %get-tuple-element.28), calls=%async_computation | async-start | bytes 393216 | tf_op jit(solution)/shard_map/all_to_all | solution.py:361
  16.4 23.9 %collective-permute-start.1 = (f32[2,4,3,32,256]{4,3,2,1,0:T(8,128)}, f32[2,4,3,32,256]{4,3,2,1,0:T(8,128)}, u32[]{:S(2)}, u32[]{:S(2)}) collective-permute-start(f32[2,4,3,32,256]{4,3,2,1,0:T(8,128)} %get-tuple-element.29), channel_id=1, source_target_pairs={{4,0},{8,4},{12,8},{16,12},{20,16},{24,20},{28,24},{0,28},{5,1},{9... | collective-permute-start | bytes 2359304 | tf_op jit(solution)/shard_map/ppermute | solution.py:298
  21.4 0.8 copy-start.6
  22.3 2.6 %copy-start = (s32[16,256]{1,0:T(8,128)S(1)}, s32[16,256]{1,0:T(8,128)}, u32[]{:S(2)}) copy-start(s32[16,256]{1,0:T(8,128)} %status_ref.1) | copy-start | bytes 49156
  22.3 2.6 %copy-start.5 = (s32[2,256]{1,0:T(2,128)S(1)}, s32[2,256]{1,0:T(2,128)}, u32[]{:S(2)}) copy-start(s32[2,256]{1,0:T(2,128)} %pairs_ref.3) | copy-start | bytes 6148
  22.3 9.9 %copy-start.10 = (f32[256]{0:T(256)S(1)}, f32[256]{0:T(256)}, u32[]{:S(2)}) copy-start(f32[256]{0:T(256)} %param.21) | copy-start | bytes 3076
  22.3 9.9 %copy-start.11 = (f32[64,32]{1,0:T(8,128)S(1)}, f32[64,32]{1,0:T(8,128)}, u32[]{:S(2)}) copy-start(f32[64,32]{1,0:T(8,128)} %constant.8.clone.table_ref) | copy-start | bytes 24580
  22.3 9.9 %copy-start.12 = (f32[4,8,64]{2,1,0:T(8,128)S(1)}, f32[4,8,64]{2,1,0:T(8,128)}, u32[]{:S(2)}) copy-start(f32[4,8,64]{2,1,0:T(8,128)} %constant.9.clone.back_ref) | copy-start | bytes 24580
  32.1 15.2 %copy-start.2 = (s32[1024]{0:T(1024)S(1)}, s32[1024]{0:T(1024)}, u32[]{:S(2)}) copy-start(s32[1024]{0:T(1024)} %param.17) | copy-start | bytes 12292
  32.1 15.2 %copy-start.4 = (s32[1024]{0:T(1024)S(1)}, s32[1024]{0:T(1024)}, u32[]{:S(2)}) copy-start(s32[1024]{0:T(1024)} %param.18) | copy-start | bytes 12292
  32.1 15.2 %copy-start.7 = (f32[2,3,3,32,256]{4,3,2,1,0:T(8,128)S(1)}, f32[2,3,3,32,256]{4,3,2,1,0:T(8,128)}, u32[]{:S(2)}) copy-start(f32[2,3,3,32,256]{4,3,2,1,0:T(8,128)} %copy-done.6) | copy-start | bytes 1769476
  32.2 15.2 %copy-start.8 = (f32[2,32,256]{2,1,0:T(8,128)S(1)}, f32[2,32,256]{2,1,0:T(8,128)}, u32[]{:S(2)}) copy-start(f32[2,32,256]{2,1,0:T(8,128)} %param.15) | copy-start | bytes 196612
  32.2 15.2 %copy-start.9 = (f32[2,32,256]{2,1,0:T(8,128)S(1)}, f32[2,32,256]{2,1,0:T(8,128)}, u32[]{:S(2)}) copy-start(f32[2,32,256]{2,1,0:T(8,128)} %param.16) | copy-start | bytes 196612
  35.0 12.3 %all-to-all-start.1 = ((f32[8,6,8,128]{3,2,1,0:T(8,128)}), f32[8,6,8,128]{3,2,1,0:T(8,128)S(1)}, u32[]{:S(2)}, u32[]{:S(2)}) async-start(f32[8,6,8,128]{3,2,1,0:T(8,128)} %pair_force.1), calls=%async_computation.1 | async-start | bytes 393216 | tf_op jit(solution)/shard_map/all_to_all | solution.py:361
  40.3 38.4 %collective-permute-start.5 = (f32[2,3,3,32,256]{4,3,2,1,0:T(8,128)}, f32[2,3,3,32,256]{4,3,2,1,0:T(8,128)}, u32[]{:S(2)}, u32[]{:S(2)}) collective-permute-start(f32[2,3,3,32,256]{4,3,2,1,0:T(8,128)} %get-tuple-element.43), channel_id=1, source_target_pairs={{4,0},{8,4},{12,8},{16,12},{20,16},{24,20},{28,24},{0,28},{5,1},{9... | collective-permute-start | bytes 1769480 | tf_op jit(solution)/shard_map/ppermute | solution.py:298
  43.2 35.4 %collective-permute-start.4 = (f32[2,4,3,32,256]{4,3,2,1,0:T(8,128)}, f32[2,4,3,32,256]{4,3,2,1,0:T(8,128)}, u32[]{:S(2)}, u32[]{:S(2)}) collective-permute-start(f32[2,4,3,32,256]{4,3,2,1,0:T(8,128)} %get-tuple-element.42), channel_id=1, source_target_pairs={{0,4},{4,8},{8,12},{12,16},{16,20},{20,24},{24,28},{28,0},{1,5},{5... | collective-permute-start | bytes 2359304 | tf_op jit(solution)/shard_map/ppermute | solution.py:297
  55.4 25.9 %collective-permute-start.2 = (f32[2,1,3,32,256]{4,3,2,1,0:T(8,128)}, f32[2,1,3,32,256]{4,3,2,1,0:T(8,128)}, u32[]{:S(2)}, u32[]{:S(2)}) collective-permute-start(f32[2,1,3,32,256]{4,3,2,1,0:T(8,128)} %get-tuple-element.40), channel_id=1, source_target_pairs={{0,4},{4,8},{8,12},{12,16},{16,20},{20,24},{24,28},{28,0},{1,5},{5... | collective-permute-start | bytes 589832 | tf_op jit(solution)/shard_map/ppermute | solution.py:297
  56.1 26.3 %collective-permute-start.3 = (f32[2,1,3,32,256]{4,3,2,1,0:T(8,128)}, f32[2,1,3,32,256]{4,3,2,1,0:T(8,128)}, u32[]{:S(2)}, u32[]{:S(2)}) collective-permute-start(f32[2,1,3,32,256]{4,3,2,1,0:T(8,128)} %get-tuple-element.41), channel_id=1, source_target_pairs={{4,0},{8,4},{12,8},{16,12},{20,16},{24,20},{28,24},{0,28},{5,1},{9... | collective-permute-start | bytes 589832 | tf_op jit(solution)/shard_map/ppermute | solution.py:298

commit v3 on v2

--- a/solution.py
+++ b/solution.py
@@ -16,7 +16,7 @@
 normal_penalty = 2.0
 shear_penalty = 1.0
 
-CUTS = ((3, 0), (3, 4), (7, 7), (8, 8))
+CUTS = ((3, 0), (3, 5), (7, 7), (8, 8))
 VMEM = 28 * 1024 * 1024
 
 
@@ -163,7 +163,8 @@
             out_ref[block] = part
 
 
-def combine_kernel(place_ref, cells_ref, send_ref, back_ref, *refs, edges, late):
+def combine_kernel(mark_ref, place_ref, cells_ref, send_ref, back_ref, *refs, edges, late):
+    del mark_ref
     piece_refs = refs[: len(edges)]
     stiff_ref, mass_ref, x_ref, y_ref, forcing_ref = refs[len(edges) : len(edges) + 5]
     res_ref, jac_ref, late_res_ref, late_jac_ref, cell_ref, low_ref = refs[len(edges) + 5 :]
@@ -371,14 +372,15 @@
         shift(edge, piece) for edge, piece in zip(groups[index], queue[index - 1])
     ]
     outgoing, queue[0] = lax.optimization_barrier((outgoing, queue[0]))
-    mark = pl.pallas_call(
+    arrival = pl.pallas_call(
         mark_kernel,
         in_specs=[pl.BlockSpec(memory_space=pl.ANY)],
         out_specs=near_memory,
         out_shape=pltpu.VMEM((8, LANES), f32),
         cost_estimate=LARGE,
-        name="first_piece_arrived",
-    )(pieces[0][-1])
+        name="piece_arrived",
+    )
+    mark = arrival(pieces[0][-1])
     pieces.append(send_group(1))
     arrived = exchange(outgoing)
     own_opening = pl.pallas_call(
@@ -410,7 +412,8 @@
         name="pair_force",
     )(place, pair_rows, crack_gap.reshape(1, pairs), jnp.asarray(table), jnp.asarray(back), everything)
     returned = exchange(slot_force)
-    pieces[1], queue[1:], _ = lax.optimization_barrier((pieces[1], queue[1:], slot_force))
+    queue[1:], _ = lax.optimization_barrier((queue[1:], slot_force))
+    second_mark = arrival(pieces[1][-1])
     pieces.append(send_group(2))
 
     flat = jax.ShapeDtypeStruct(x.shape, f32)
@@ -423,7 +426,7 @@
     residual, product, late_res, late_jac = pl.pallas_call(
         lambda *refs: combine_kernel(*refs, edges=early, late=late),
         grid=(comps,),
-        in_specs=[scalar, whole(cells.shape), whole(send.shape)]
+        in_specs=[near_memory, scalar, whole(cells.shape), whole(send.shape)]
         + [near_memory]
         + [piece_spec(piece) for piece in pieces[0] + pieces[1]]
         + [whole((rows, axial))] * 2
@@ -435,9 +438,10 @@
             pltpu.VMEM((axial, slots), jnp.bfloat16),
         ],
         compiler_params=params("arbitrary"),
-        cost_estimate=LARGE,
+        cost_estimate=SMALL,
         name="combine_terms",
     )(
+        keep(second_mark),
         place,
         cells,
         send,

time: 84.7 us -> 82.6 us (0.975)
  waiting for transfers between devices: 28.6 us -> 20.5 us
  starting transfers between devices: 23.8 us -> 29.7 us
    ppermute x3, waiting for transfers between devices: 21.5 us -> 12.6 us  [on_device(): behind = lambda piece: lax.ppermute(piece, 'mesh', backward)]
    ppermute x3, starting transfers between devices: 11.7 us -> 16.8 us  [on_device(): behind = lambda piece: lax.ppermute(piece, 'mesh', backward)]
  transfers between devices with their start and end apart: 8 -> 8, of which waited for: 7 -> 6; matrix products, arithmetic and copies ran while one was open for 0% -> 0% of each run, Pallas kernels for 25% -> 26%
where the time goes in v3:
time: 82.6 us; the launch traced here: 82.1 us
  starting transfers between devices  29.7 us (36%)
  Pallas kernels  23.3 us (28%)
  waiting for transfers between devices  20.5 us (25%)
  blocking collectives  5.79 us (7%)
  local copies, waits for them, and re-layouts  1.97 us (2%)
    ppermute x3, starting transfers between devices, on_device(): behind = lambda piece: lax.ppermute(piece, 'mesh', backward)  16.8 us
    ppermute x3, waiting for transfers between devices, on_device(): behind = lambda piece: lax.ppermute(piece, 'mesh', backward)  12.6 us
    all_to_all x2, starting transfers between devices, exchange(): lax.all_to_all(block, 'mesh', split_axis=0, concat_axis=0, tiled=True)  8.89 us
    pallas_call x1, Pallas kernels, on_device(): pl.pallas_call(lambda *refs: combine_kernel(*refs, edges=early, late=late...  8.14 us
    all_to_all x2, waiting for transfers between devices, exchange(): lax.all_to_all(block, 'mesh', split_axis=0, concat_axis=0, tiled=True)  7.5 us
    pallas_call x1, Pallas kernels, on_device(): pl.pallas_call(lambda *refs: gather_kernel(*refs, edges=edges), grid=(com...  6.65 us
    all_gather x1, blocking collectives, on_device(): everything = lax.all_gather(own_opening, 'harm')  5.79 us
    pallas_call x2, Pallas kernels, on_device(): pl.pallas_call(lambda *refs, starts=starts: edge_kernel(*refs, late=late,...  4.26 us
  transfers between devices with their start and end apart: 8, of which 6 were waited for; matrix products, arithmetic and copies ran while one was open for 0% of the time, Pallas kernels for 26%

profile of v3, /device:TPU:0, one launch (start us, length us, event | category | flops | bytes accessed | tf_op | source)
XLA Modules:
  0.0 82.1 jit_solution(9224815751221852239)
XLA Ops:
  0.6 0.0 copy-start.6
  0.6 0.0 copy-start.4
  0.7 1.1 %slice_bitcast_fusion = (f32[1,3,3,32,256]{4,3,2,1,0:T(8,128)S(1)}, f32[1,3,3,32,256]{4,3,2,1,0:T(8,128)S(1)}) fusion(f32[8,3,2,32,256]{4,3,2,1,0:T(8,128)} %param.13, f32[8,3,2,32,256]{4,3,2,1,0:T(8,128)} %param.12), kind=kLoop, calls=%fused_computation.1 | loop fusion | bytes 1179648 | tf_op jit(solution)/shard_map/stack;squeeze | solution.py:318
  1.8 3.0 %collective-permute-start.1 = (f32[2,3,3,32,256]{4,3,2,1,0:T(8,128)S(1)}, f32[2,3,3,32,256]{4,3,2,1,0:T(8,128)S(1)}, u32[]{:S(2)}, u32[]{:S(2)}) collective-permute-start(f32[2,3,3,32,256]{4,3,2,1,0:T(8,128)S(1)} %pad_maximum_fusion), channel_id=1, source_target_pairs={{0,4},{4,8},{8,12},{12,16},{16,20},{20,24},{24,28},{28,0},{1,5},{5... | collective-permute-start | bytes 1769480 | tf_op jit(solution)/shard_map/ppermute | solution.py:298
  4.8 0.0 copy-done.6
  4.8 0.0 copy-done.4
  4.8 6.6 %face_gather.1 = (f32[8,6,8,128]{3,2,1,0:T(8,128)}, f32[2,5,3,32,256]{4,3,2,1,0:T(8,128)}, f32[2,4,3,32,256]{4,3,2,1,0:T(8,128)}, f32[2,2,3,32,256]{4,3,2,1,0:T(...) custom-call(s32[8,128]{1,0:T(8,128)S(1)} %bitcast.23, s32[8,128]{1,0:T(8,128)S(1)} %bitcast.25, ...), custom_call_target="tpu_custom_call" | custom-call | flops 1000 | bytes 1000 | tf_op jit(solution)/shard_map/face_gather/pallas_call | solution.py:340
  11.5 4.9 %all-to-all-start = ((f32[8,6,8,128]{3,2,1,0:T(8,128)}), f32[8,6,8,128]{3,2,1,0:T(8,128)}, u32[]{:S(2)}, u32[]{:S(2)}) async-start(f32[8,6,8,128]{3,2,1,0:T(8,128)} %get-tuple-element.28), calls=%async_computation | async-start | bytes 393216 | tf_op jit(solution)/shard_map/all_to_all | solution.py:362
  16.4 4.7 %collective-permute-start = (f32[2,5,3,32,256]{4,3,2,1,0:T(8,128)}, f32[2,5,3,32,256]{4,3,2,1,0:T(8,128)}, u32[]{:S(2)}, u32[]{:S(2)}) collective-permute-start(f32[2,5,3,32,256]{4,3,2,1,0:T(8,128)} %get-tuple-element.27), channel_id=1, source_target_pairs={{4,0},{8,4},{12,8},{16,12},{20,16},{24,20},{28,24},{0,28},{5,1},{9... | collective-permute-start | bytes 2949128 | tf_op jit(solution)/shard_map/ppermute | solution.py:299
  21.1 0.4 collective-permute-done.1.piece_ref.refs_5_
  21.5 0.8 copy-done
  22.3 0.0 copy-start.12
  22.3 2.6 %all-to-all-done.arrived_ref = f32[8,6,8,128]{3,2,1,0:T(8,128)} async-done(((f32[8,6,8,128]{3,2,1,0:T(8,128)}), f32[8,6,8,128]{3,2,1,0:T(8,128)}, u32[]{:S(2)}, u32[]{:S(2)}) %all-to-all-start) | async-done | bytes 196640 | tf_op jit(solution)/shard_map/all_to_all | solution.py:362
  24.9 1.4 %pair_difference.1 = f32[64,256]{1,0:T(8,128)S(1)} custom-call(s32[2,256]{1,0:T(2,128)S(1)} %copy-done.9, s32[16,256]{1,0:T(8,128)S(1)} %copy-done.8, f32[8,128]{1,0:T(8,128)S(1)} %piece_arrived.3.mark_ref, f32[8,6,8,128]{3,2,1,0:T(8,128)} %all-to-all-done.arrived_ref), custom_call_target="tpu_custom_call" | custom-call | flops 1000 | bytes 1000 | tf_op jit(solution)/shard_map/pair_difference/pallas_call | solution.py:386
  26.3 5.8 %all-gather = f32[256,256]{1,0:T(8,128)S(1)} all-gather(f32[64,256]{1,0:T(8,128)S(1)} %pair_difference.1), channel_id=2, replica_groups=mesh['mesh'=8,'harm'=4] {'harm'}, dimensions={0}, use_global_device_ids=true | all-gather | bytes 327680 | tf_op jit(solution)/shard_map/all_gather | solution.py:395
  32.1 2.8 %pair_force.1 = f32[8,6,8,128]{3,2,1,0:T(8,128)} custom-call(s32[1]{0:T(128)} %bitcast.4.place_ref.refs_1_, s32[2,256]{1,0:T(2,128)S(1)} %copy-done.9, f32[1,256]{1,0:T(1,128)S(1)} %bitcast.27, f32[64,32]{1,0:T(8,128)S(1)} %copy-done.11, f32[4,8,64]{2,1,0:T(8,128)S(1)} %copy-done.12, f32[4,64,256]{2,1,0:T(8,128)S(1)} %bitcast.20), custom_call_target="tpu_custom_call" | custom-call | flops 999999995904 | bytes 10000000000 | tf_op jit(solution)/shard_map/pair_force/pallas_call | solution.py:398
  34.9 4.0 %all-to-all-start.1 = ((f32[8,6,8,128]{3,2,1,0:T(8,128)}), f32[8,6,8,128]{3,2,1,0:T(8,128)}, u32[]{:S(2)}, u32[]{:S(2)}) async-start(f32[8,6,8,128]{3,2,1,0:T(8,128)} %pair_force.1), calls=%async_computation.1 | async-start | bytes 393216 | tf_op jit(solution)/shard_map/all_to_all | solution.py:362
  39.0 4.6 %collective-permute-start.5 = (f32[2,2,3,32,256]{4,3,2,1,0:T(8,128)}, f32[2,2,3,32,256]{4,3,2,1,0:T(8,128)}, u32[]{:S(2)}, u32[]{:S(2)}) collective-permute-start(f32[2,2,3,32,256]{4,3,2,1,0:T(8,128)} %get-tuple-element.41), channel_id=1, source_target_pairs={{4,0},{8,4},{12,8},{16,12},{20,16},{24,20},{28,24},{0,28},{5,1},{9... | collective-permute-start | bytes 1179656 | tf_op jit(solution)/shard_map/ppermute | solution.py:299
  43.6 0.0 collective-permute-start.4
  43.6 2.1 %collective-permute-done.piece_ref.refs_6_ = f32[2,5,3,32,256]{4,3,2,1,0:T(8,128)} collective-permute-done((f32[2,5,3,32,256]{4,3,2,1,0:T(8,128)}, f32[2,5,3,32,256]{4,3,2,1,0:T(8,128)}, u32[]{:S(2)}, u32[]{:S(2)}) %collective-permute-start) | collective-permute-done | bytes 983072 | tf_op jit(solution)/shard_map/ppermute | solution.py:299
  45.7 0.0 copy-start.7
  45.7 4.9 %all-to-all-done.1.refs_4_ = f32[8,6,8,128]{3,2,1,0:T(8,128)} async-done(((f32[8,6,8,128]{3,2,1,0:T(8,128)}), f32[8,6,8,128]{3,2,1,0:T(8,128)}, u32[]{:S(2)}, u32[]{:S(2)}) %all-to-all-start.1) | async-done | bytes 196640 | tf_op jit(solution)/shard_map/all_to_all | solution.py:362
  50.6 0.0 copy-done.1
  50.6 8.1 %combine_terms.1 = (f32[8,3,64,256]{3,2,1,0:T(8,128)}, f32[8,3,64,256]{3,2,1,0:T(8,128)}, f32[5,3,64,256]{3,2,1,0:T(8,128)S(1)}, f32[5,3,64,256]{3,2,1,0:T(8,128)S(1)}) custom-call(f32[8,128]{1,0:T(8,128)S(1)} %piece_arrived.2.refs_0_, s32[1]{0:T(128)} %bitcast.4.place_ref.refs_1_, s32[8,128]{1,0:T(8,128)S(1)} %bitcast.24, s32[8,128]{1,0:T(8,128)S(1)} %bitcast.26, ...), custom_call_target="tpu_custom_call" | custom-call | flops 1000 | bytes 1000 | tf_op jit(solution)/shard_map/combine_terms/pallas_call | solution.py:426
  58.8 1.0 %collective-permute-start.2 = (f32[2,1,3,32,256]{4,3,2,1,0:T(8,128)}, f32[2,1,3,32,256]{4,3,2,1,0:T(8,128)}, u32[]{:S(2)}, u32[]{:S(2)}) collective-permute-start(f32[2,1,3,32,256]{4,3,2,1,0:T(8,128)} %get-tuple-element.38), channel_id=1, source_target_pairs={{0,4},{4,8},{8,12},{12,16},{16,20},{20,24},{24,28},{28,0},{1,5},{5... | collective-permute-start | bytes 589832 | tf_op jit(solution)/shard_map/ppermute | solution.py:298
  59.8 7.4 %collective-permute-start.3 = (f32[2,1,3,32,256]{4,3,2,1,0:T(8,128)}, f32[2,1,3,32,256]{4,3,2,1,0:T(8,128)}, u32[]{:S(2)}, u32[]{:S(2)}) collective-permute-start(f32[2,1,3,32,256]{4,3,2,1,0:T(8,128)} %get-tuple-element.39), channel_id=1, source_target_pairs={{4,0},{8,4},{12,8},{16,12},{20,16},{24,20},{28,24},{0,28},{5,1},{9... | collective-permute-start | bytes 589832 | tf_op jit(solution)/shard_map/ppermute | solution.py:299
  67.2 9.0 %collective-permute-done.5.refs_3_ = f32[2,2,3,32,256]{4,3,2,1,0:T(8,128)} collective-permute-done((f32[2,2,3,32,256]{4,3,2,1,0:T(8,128)}, f32[2,2,3,32,256]{4,3,2,1,0:T(8,128)}, u32[]{:S(2)}, u32[]{:S(2)}) %collective-permute-start.5) | collective-permute-done | bytes 393248 | tf_op jit(solution)/shard_map/ppermute | solution.py:299
  76.2 0.0 collective-permute-done.4.refs_2_
  76.2 2.5 %edge_terms.2 = (f32[8,3,64,256]{3,2,1,0:T(8,128)}, f32[8,3,64,256]{3,2,1,0:T(8,128)}) custom-call(f32[5,3,64,256]{3,2,1,0:T(8,128)S(1)} %get-tuple-element.29.refs_0_, f32[5,3,64,256]{3,2,1,0:T(8,128)S(1)} %get-tuple-element.30.refs_1_, f32[2,4,3,32,256]{4,3,2,1,0:T(8,128)} %collective-permute-done.4.refs_2_, ...), custom_call_target="tpu_custom_call", output_to_operand_aliasing={{0}: (4, {}), {1}: (5, {})} | custom-call | flops 999999995904 | bytes 10000000000 | tf_op jit(solution)/shard_map/edge_terms/pallas_call | solution.py:463
  78.7 0.0 collective-permute-done.2.refs_2_
  78.7 1.6 %collective-permute-done.3.refs_3_ = f32[2,1,3,32,256]{4,3,2,1,0:T(8,128)} collective-permute-done((f32[2,1,3,32,256]{4,3,2,1,0:T(8,128)}, f32[2,1,3,32,256]{4,3,2,1,0:T(8,128)}, u32[]{:S(2)}, u32[]{:S(2)}) %collective-permute-start.3) | collective-permute-done | bytes 196640 | tf_op jit(solution)/shard_map/ppermute | solution.py:299
  80.3 1.8 %edge_terms.3 = (f32[8,3,64,256]{3,2,1,0:T(8,128)}, f32[8,3,64,256]{3,2,1,0:T(8,128)}) custom-call(f32[5,3,64,256]{3,2,1,0:T(8,128)S(1)} %get-tuple-element.29.refs_0_, f32[5,3,64,256]{3,2,1,0:T(8,128)S(1)} %get-tuple-element.30.refs_1_, f32[2,1,3,32,256]{4,3,2,1,0:T(8,128)} %collective-permute-done.2.refs_2_, ...), custom_call_target="tpu_custom_call", output_to_operand_aliasing={{0}: (4, {}), {1}: (5, {})} | custom-call | flops 1000 | bytes 1000 | tf_op jit(solution)/shard_map/edge_terms/pallas_call | solution.py:463
  (21 shorter events, 0.1 us)
Async XLA Ops:
  0.6 4.2 %copy-start.6 = (s32[1024]{0:T(1024)S(1)}, s32[1024]{0:T(1024)}, u32[]{:S(2)}) copy-start(s32[1024]{0:T(1024)} %param.18) | copy-start | bytes 12292
  0.6 4.2 %copy-start.4 = (s32[1024]{0:T(1024)S(1)}, s32[1024]{0:T(1024)}, u32[]{:S(2)}) copy-start(s32[1024]{0:T(1024)} %param.17) | copy-start | bytes 12292
  1.8 19.6 %collective-permute-start.1 = (f32[2,3,3,32,256]{4,3,2,1,0:T(8,128)S(1)}, f32[2,3,3,32,256]{4,3,2,1,0:T(8,128)S(1)}, u32[]{:S(2)}, u32[]{:S(2)}) collective-permute-start(f32[2,3,3,32,256]{4,3,2,1,0:T(8,128)S(1)} %pad_maximum_fusion), channel_id=1, source_target_pairs={{0,4},{4,8},{8,12},{12,16},{16,20},{20,24},{24,28},{28,0},{1,5},{5... | collective-permute-start | bytes 1769480 | tf_op jit(solution)/shard_map/ppermute | solution.py:298
  11.5 13.4 %all-to-all-start = ((f32[8,6,8,128]{3,2,1,0:T(8,128)}), f32[8,6,8,128]{3,2,1,0:T(8,128)}, u32[]{:S(2)}, u32[]{:S(2)}) async-start(f32[8,6,8,128]{3,2,1,0:T(8,128)} %get-tuple-element.28), calls=%async_computation | async-start | bytes 393216 | tf_op jit(solution)/shard_map/all_to_all | solution.py:362
  16.4 29.3 %collective-permute-start = (f32[2,5,3,32,256]{4,3,2,1,0:T(8,128)}, f32[2,5,3,32,256]{4,3,2,1,0:T(8,128)}, u32[]{:S(2)}, u32[]{:S(2)}) collective-permute-start(f32[2,5,3,32,256]{4,3,2,1,0:T(8,128)} %get-tuple-element.27), channel_id=1, source_target_pairs={{4,0},{8,4},{12,8},{16,12},{20,16},{24,20},{28,24},{0,28},{5,1},{9... | collective-permute-start | bytes 2949128 | tf_op jit(solution)/shard_map/ppermute | solution.py:299
  21.4 0.8 copy-start
  22.3 2.6 %copy-start.8 = (s32[16,256]{1,0:T(8,128)S(1)}, s32[16,256]{1,0:T(8,128)}, u32[]{:S(2)}) copy-start(s32[16,256]{1,0:T(8,128)} %status_ref.1) | copy-start | bytes 49156
  22.3 2.6 %copy-start.9 = (s32[2,256]{1,0:T(2,128)S(1)}, s32[2,256]{1,0:T(2,128)}, u32[]{:S(2)}) copy-start(s32[2,256]{1,0:T(2,128)} %pairs_ref.3) | copy-start | bytes 6148
  22.3 9.9 %copy-start.10 = (f32[256]{0:T(256)S(1)}, f32[256]{0:T(256)}, u32[]{:S(2)}) copy-start(f32[256]{0:T(256)} %param.21) | copy-start | bytes 3076
  22.3 9.9 %copy-start.11 = (f32[64,32]{1,0:T(8,128)S(1)}, f32[64,32]{1,0:T(8,128)}, u32[]{:S(2)}) copy-start(f32[64,32]{1,0:T(8,128)} %constant.8.clone.table_ref) | copy-start | bytes 24580
  22.3 9.9 %copy-start.12 = (f32[4,8,64]{2,1,0:T(8,128)S(1)}, f32[4,8,64]{2,1,0:T(8,128)}, u32[]{:S(2)}) copy-start(f32[4,8,64]{2,1,0:T(8,128)} %constant.9.clone.back_ref) | copy-start | bytes 24580
  34.9 15.7 %all-to-all-start.1 = ((f32[8,6,8,128]{3,2,1,0:T(8,128)}), f32[8,6,8,128]{3,2,1,0:T(8,128)}, u32[]{:S(2)}, u32[]{:S(2)}) async-start(f32[8,6,8,128]{3,2,1,0:T(8,128)} %pair_force.1), calls=%async_computation.1 | async-start | bytes 393216 | tf_op jit(solution)/shard_map/all_to_all | solution.py:362
  39.0 37.2 %collective-permute-start.5 = (f32[2,2,3,32,256]{4,3,2,1,0:T(8,128)}, f32[2,2,3,32,256]{4,3,2,1,0:T(8,128)}, u32[]{:S(2)}, u32[]{:S(2)}) collective-permute-start(f32[2,2,3,32,256]{4,3,2,1,0:T(8,128)} %get-tuple-element.41), channel_id=1, source_target_pairs={{4,0},{8,4},{12,8},{16,12},{20,16},{24,20},{28,24},{0,28},{5,1},{9... | collective-permute-start | bytes 1179656 | tf_op jit(solution)/shard_map/ppermute | solution.py:299
  43.6 32.6 %collective-permute-start.4 = (f32[2,4,3,32,256]{4,3,2,1,0:T(8,128)}, f32[2,4,3,32,256]{4,3,2,1,0:T(8,128)}, u32[]{:S(2)}, u32[]{:S(2)}) collective-permute-start(f32[2,4,3,32,256]{4,3,2,1,0:T(8,128)} %get-tuple-element.40), channel_id=1, source_target_pairs={{0,4},{4,8},{8,12},{12,16},{16,20},{20,24},{24,28},{28,0},{1,5},{5... | collective-permute-start | bytes 2359304 | tf_op jit(solution)/shard_map/ppermute | solution.py:298
  45.6 5.0 %copy-start.1 = (f32[2,3,3,32,256]{4,3,2,1,0:T(8,128)S(1)}, f32[2,3,3,32,256]{4,3,2,1,0:T(8,128)}, u32[]{:S(2)}) copy-start(f32[2,3,3,32,256]{4,3,2,1,0:T(8,128)} %copy-done) | copy-start | bytes 1769476
  45.6 5.0 %copy-start.2 = (f32[2,32,256]{2,1,0:T(8,128)S(1)}, f32[2,32,256]{2,1,0:T(8,128)}, u32[]{:S(2)}) copy-start(f32[2,32,256]{2,1,0:T(8,128)} %param.15) | copy-start | bytes 196612
  45.6 5.0 %copy-start.3 = (f32[2,32,256]{2,1,0:T(8,128)S(1)}, f32[2,32,256]{2,1,0:T(8,128)}, u32[]{:S(2)}) copy-start(f32[2,32,256]{2,1,0:T(8,128)} %param.16) | copy-start | bytes 196612
  45.6 5.0 %copy-start.5 = (s32[1024]{0:T(1024)S(1)}, s32[1024]{0:T(1024)}, u32[]{:S(2)}) copy-start(s32[1024]{0:T(1024)} %param.17) | copy-start | bytes 12292
  45.7 5.0 %copy-start.7 = (s32[1024]{0:T(1024)S(1)}, s32[1024]{0:T(1024)}, u32[]{:S(2)}) copy-start(s32[1024]{0:T(1024)} %param.18) | copy-start | bytes 12292
  58.8 19.9 %collective-permute-start.2 = (f32[2,1,3,32,256]{4,3,2,1,0:T(8,128)}, f32[2,1,3,32,256]{4,3,2,1,0:T(8,128)}, u32[]{:S(2)}, u32[]{:S(2)}) collective-permute-start(f32[2,1,3,32,256]{4,3,2,1,0:T(8,128)} %get-tuple-element.38), channel_id=1, source_target_pairs={{0,4},{4,8},{8,12},{12,16},{16,20},{20,24},{24,28},{28,0},{1,5},{5... | collective-permute-start | bytes 589832 | tf_op jit(solution)/shard_map/ppermute | solution.py:298
  59.8 20.5 %collective-permute-start.3 = (f32[2,1,3,32,256]{4,3,2,1,0:T(8,128)}, f32[2,1,3,32,256]{4,3,2,1,0:T(8,128)}, u32[]{:S(2)}, u32[]{:S(2)}) collective-permute-start(f32[2,1,3,32,256]{4,3,2,1,0:T(8,128)} %get-tuple-element.39), channel_id=1, source_target_pairs={{4,0},{8,4},{12,8},{16,12},{20,16},{24,20},{28,24},{0,28},{5,1},{9... | collective-permute-start | bytes 589832 | tf_op jit(solution)/shard_map/ppermute | solution.py:299

commit v4 on v3

--- a/solution.py
+++ b/solution.py
@@ -234,19 +234,19 @@
     count = stage.shape[1]
     layer = stage.shape[3] // 2
     copies = []
-    for field, (late_ref, out_ref) in enumerate(((late_res, res_ref), (late_jac, jac_ref))):
-        value = late_ref[first - late : first - late + count]
-        for piece, start, side in ((below, starts[0], 0), (above, starts[1], 1)):
-            rows = slice(side * layer, (side + 1) * layer)
-            skip = start - first
-            if skip > 0:
-                stage[field, :skip, :, rows] = value[:skip, :, rows]
-            stage[field, skip:, :, rows] = value[skip:, :, rows] - piece[field]
-        copy = pltpu.make_async_copy(
-            stage.at[field], out_ref.at[first : first + count], sems.at[field]
-        )
-        copy.start()
-        copies.append(copy)
+    for coef in range(first, first + count):
+        for field, (late_ref, out_ref) in enumerate(((late_res, res_ref), (late_jac, jac_ref))):
+            for piece, start, side in ((below, starts[0], 0), (above, starts[1], 1)):
+                rows = slice(side * layer, (side + 1) * layer)
+                value = late_ref[coef - late, :, rows]
+                if coef >= start:
+                    value = value - piece[field, coef - start]
+                stage[field, coef - first, :, rows] = value
+            copy = pltpu.make_async_copy(
+                stage.at[field, coef - first], out_ref.at[coef], sems.at[field, coef - first]
+            )
+            copy.start()
+            copies.append(copy)
     for copy in copies:
         copy.wait()
 
@@ -468,7 +468,7 @@
             input_output_aliases={4: 0, 5: 1},
             scratch_shapes=[
                 pltpu.VMEM((2, last - min(starts), comps, rows, axial), f32),
-                pltpu.SemaphoreType.DMA((2,)),
+                pltpu.SemaphoreType.DMA((2, last - min(starts))),
             ],
             compiler_params=params(),
             cost_estimate=LARGE if last < coefs else SMALL,

time: 82.6 us -> 82.6 us (level)
  no operation moved by 1% of the time
where the time goes in v4:
time: 82.6 us; the launch traced here: 82.1 us
  starting transfers between devices  29.7 us (36%)
  Pallas kernels  23.3 us (28%)
  waiting for transfers between devices  20.5 us (25%)
  blocking collectives  5.79 us (7%)
  local copies, waits for them, and re-layouts  1.97 us (2%)
    ppermute x3, starting transfers between devices, on_device(): behind = lambda piece: lax.ppermute(piece, 'mesh', backward)  16.8 us
    ppermute x3, waiting for transfers between devices, on_device(): behind = lambda piece: lax.ppermute(piece, 'mesh', backward)  12.7 us
    all_to_all x2, starting transfers between devices, exchange(): lax.all_to_all(block, 'mesh', split_axis=0, concat_axis=0, tiled=True)  8.89 us
    pallas_call x1, Pallas kernels, on_device(): pl.pallas_call(lambda *refs: combine_kernel(*refs, edges=early, late=late...  8.14 us
    all_to_all x2, waiting for transfers between devices, exchange(): lax.all_to_all(block, 'mesh', split_axis=0, concat_axis=0, tiled=True)  7.5 us
    pallas_call x1, Pallas kernels, on_device(): pl.pallas_call(lambda *refs: gather_kernel(*refs, edges=edges), grid=(com...  6.65 us
    all_gather x1, blocking collectives, on_device(): everything = lax.all_gather(own_opening, 'harm')  5.79 us
    pallas_call x2, Pallas kernels, on_device(): pl.pallas_call(lambda *refs, starts=starts: edge_kernel(*refs, late=late,...  4.25 us
  transfers between devices with their start and end apart: 8, of which 6 were waited for; matrix products, arithmetic and copies ran while one was open for 0% of the time, Pallas kernels for 26%

profile of v4, /device:TPU:0, one launch (start us, length us, event | category | flops | bytes accessed | tf_op | source)
XLA Modules:
  0.0 82.1 jit_solution(8422543653541155727)
XLA Ops:
  0.6 0.0 copy-start.6
  0.6 0.0 copy-start.4
  0.7 1.1 %slice_bitcast_fusion = (f32[1,3,3,32,256]{4,3,2,1,0:T(8,128)S(1)}, f32[1,3,3,32,256]{4,3,2,1,0:T(8,128)S(1)}) fusion(f32[8,3,2,32,256]{4,3,2,1,0:T(8,128)} %param.13, f32[8,3,2,32,256]{4,3,2,1,0:T(8,128)} %param.12), kind=kLoop, calls=%fused_computation.1 | loop fusion | bytes 1179648 | tf_op jit(solution)/shard_map/stack;squeeze | solution.py:318
  1.8 3.0 %collective-permute-start.1 = (f32[2,3,3,32,256]{4,3,2,1,0:T(8,128)S(1)}, f32[2,3,3,32,256]{4,3,2,1,0:T(8,128)S(1)}, u32[]{:S(2)}, u32[]{:S(2)}) collective-permute-start(f32[2,3,3,32,256]{4,3,2,1,0:T(8,128)S(1)} %pad_maximum_fusion), channel_id=1, source_target_pairs={{0,4},{4,8},{8,12},{12,16},{16,20},{20,24},{24,28},{28,0},{1,5},{5... | collective-permute-start | bytes 1769480 | tf_op jit(solution)/shard_map/ppermute | solution.py:298
  4.8 0.0 copy-done.6
  4.8 0.0 copy-done.4
  4.8 6.6 %face_gather.1 = (f32[8,6,8,128]{3,2,1,0:T(8,128)}, f32[2,5,3,32,256]{4,3,2,1,0:T(8,128)}, f32[2,4,3,32,256]{4,3,2,1,0:T(8,128)}, f32[2,2,3,32,256]{4,3,2,1,0:T(...) custom-call(s32[8,128]{1,0:T(8,128)S(1)} %bitcast.23, s32[8,128]{1,0:T(8,128)S(1)} %bitcast.25, ...), custom_call_target="tpu_custom_call" | custom-call | flops 1000 | bytes 1000 | tf_op jit(solution)/shard_map/face_gather/pallas_call | solution.py:340
  11.5 4.9 %all-to-all-start = ((f32[8,6,8,128]{3,2,1,0:T(8,128)}), f32[8,6,8,128]{3,2,1,0:T(8,128)}, u32[]{:S(2)}, u32[]{:S(2)}) async-start(f32[8,6,8,128]{3,2,1,0:T(8,128)} %get-tuple-element.28), calls=%async_computation | async-start | bytes 393216 | tf_op jit(solution)/shard_map/all_to_all | solution.py:362
  16.4 4.7 %collective-permute-start = (f32[2,5,3,32,256]{4,3,2,1,0:T(8,128)}, f32[2,5,3,32,256]{4,3,2,1,0:T(8,128)}, u32[]{:S(2)}, u32[]{:S(2)}) collective-permute-start(f32[2,5,3,32,256]{4,3,2,1,0:T(8,128)} %get-tuple-element.27), channel_id=1, source_target_pairs={{4,0},{8,4},{12,8},{16,12},{20,16},{24,20},{28,24},{0,28},{5,1},{9... | collective-permute-start | bytes 2949128 | tf_op jit(solution)/shard_map/ppermute | solution.py:299
  21.1 0.4 collective-permute-done.1.piece_ref.refs_5_
  21.5 0.8 copy-done
  22.3 0.0 copy-start.12
  22.3 2.6 %all-to-all-done.arrived_ref = f32[8,6,8,128]{3,2,1,0:T(8,128)} async-done(((f32[8,6,8,128]{3,2,1,0:T(8,128)}), f32[8,6,8,128]{3,2,1,0:T(8,128)}, u32[]{:S(2)}, u32[]{:S(2)}) %all-to-all-start) | async-done | bytes 196640 | tf_op jit(solution)/shard_map/all_to_all | solution.py:362
  24.9 1.4 %pair_difference.1 = f32[64,256]{1,0:T(8,128)S(1)} custom-call(s32[2,256]{1,0:T(2,128)S(1)} %copy-done.9, s32[16,256]{1,0:T(8,128)S(1)} %copy-done.8, f32[8,128]{1,0:T(8,128)S(1)} %piece_arrived.3.mark_ref, f32[8,6,8,128]{3,2,1,0:T(8,128)} %all-to-all-done.arrived_ref), custom_call_target="tpu_custom_call" | custom-call | flops 1000 | bytes 1000 | tf_op jit(solution)/shard_map/pair_difference/pallas_call | solution.py:386
  26.3 5.8 %all-gather = f32[256,256]{1,0:T(8,128)S(1)} all-gather(f32[64,256]{1,0:T(8,128)S(1)} %pair_difference.1), channel_id=2, replica_groups=mesh['mesh'=8,'harm'=4] {'harm'}, dimensions={0}, use_global_device_ids=true | all-gather | bytes 327680 | tf_op jit(solution)/shard_map/all_gather | solution.py:395
  32.1 2.8 %pair_force.1 = f32[8,6,8,128]{3,2,1,0:T(8,128)} custom-call(s32[1]{0:T(128)} %bitcast.4.place_ref.refs_1_, s32[2,256]{1,0:T(2,128)S(1)} %copy-done.9, f32[1,256]{1,0:T(1,128)S(1)} %bitcast.27, f32[64,32]{1,0:T(8,128)S(1)} %copy-done.11, f32[4,8,64]{2,1,0:T(8,128)S(1)} %copy-done.12, f32[4,64,256]{2,1,0:T(8,128)S(1)} %bitcast.20), custom_call_target="tpu_custom_call" | custom-call | flops 999999995904 | bytes 10000000000 | tf_op jit(solution)/shard_map/pair_force/pallas_call | solution.py:398
  34.9 4.0 %all-to-all-start.1 = ((f32[8,6,8,128]{3,2,1,0:T(8,128)}), f32[8,6,8,128]{3,2,1,0:T(8,128)}, u32[]{:S(2)}, u32[]{:S(2)}) async-start(f32[8,6,8,128]{3,2,1,0:T(8,128)} %pair_force.1), calls=%async_computation.1 | async-start | bytes 393216 | tf_op jit(solution)/shard_map/all_to_all | solution.py:362
  39.0 4.6 %collective-permute-start.5 = (f32[2,2,3,32,256]{4,3,2,1,0:T(8,128)}, f32[2,2,3,32,256]{4,3,2,1,0:T(8,128)}, u32[]{:S(2)}, u32[]{:S(2)}) collective-permute-start(f32[2,2,3,32,256]{4,3,2,1,0:T(8,128)} %get-tuple-element.41), channel_id=1, source_target_pairs={{4,0},{8,4},{12,8},{16,12},{20,16},{24,20},{28,24},{0,28},{5,1},{9... | collective-permute-start | bytes 1179656 | tf_op jit(solution)/shard_map/ppermute | solution.py:299
  43.6 0.0 collective-permute-start.4
  43.6 2.1 %collective-permute-done.piece_ref.refs_6_ = f32[2,5,3,32,256]{4,3,2,1,0:T(8,128)} collective-permute-done((f32[2,5,3,32,256]{4,3,2,1,0:T(8,128)}, f32[2,5,3,32,256]{4,3,2,1,0:T(8,128)}, u32[]{:S(2)}, u32[]{:S(2)}) %collective-permute-start) | collective-permute-done | bytes 983072 | tf_op jit(solution)/shard_map/ppermute | solution.py:299
  45.7 0.0 copy-start.7
  45.7 4.9 %all-to-all-done.1.refs_4_ = f32[8,6,8,128]{3,2,1,0:T(8,128)} async-done(((f32[8,6,8,128]{3,2,1,0:T(8,128)}), f32[8,6,8,128]{3,2,1,0:T(8,128)}, u32[]{:S(2)}, u32[]{:S(2)}) %all-to-all-start.1) | async-done | bytes 196640 | tf_op jit(solution)/shard_map/all_to_all | solution.py:362
  50.6 0.0 copy-done.1
  50.6 8.1 %combine_terms.1 = (f32[8,3,64,256]{3,2,1,0:T(8,128)}, f32[8,3,64,256]{3,2,1,0:T(8,128)}, f32[5,3,64,256]{3,2,1,0:T(8,128)S(1)}, f32[5,3,64,256]{3,2,1,0:T(8,128)S(1)}) custom-call(f32[8,128]{1,0:T(8,128)S(1)} %piece_arrived.2.refs_0_, s32[1]{0:T(128)} %bitcast.4.place_ref.refs_1_, s32[8,128]{1,0:T(8,128)S(1)} %bitcast.24, s32[8,128]{1,0:T(8,128)S(1)} %bitcast.26, ...), custom_call_target="tpu_custom_call" | custom-call | flops 1000 | bytes 1000 | tf_op jit(solution)/shard_map/combine_terms/pallas_call | solution.py:426
  58.8 1.0 %collective-permute-start.2 = (f32[2,1,3,32,256]{4,3,2,1,0:T(8,128)}, f32[2,1,3,32,256]{4,3,2,1,0:T(8,128)}, u32[]{:S(2)}, u32[]{:S(2)}) collective-permute-start(f32[2,1,3,32,256]{4,3,2,1,0:T(8,128)} %get-tuple-element.38), channel_id=1, source_target_pairs={{0,4},{4,8},{8,12},{12,16},{16,20},{20,24},{24,28},{28,0},{1,5},{5... | collective-permute-start | bytes 589832 | tf_op jit(solution)/shard_map/ppermute | solution.py:298
  59.8 7.4 %collective-permute-start.3 = (f32[2,1,3,32,256]{4,3,2,1,0:T(8,128)}, f32[2,1,3,32,256]{4,3,2,1,0:T(8,128)}, u32[]{:S(2)}, u32[]{:S(2)}) collective-permute-start(f32[2,1,3,32,256]{4,3,2,1,0:T(8,128)} %get-tuple-element.39), channel_id=1, source_target_pairs={{4,0},{8,4},{12,8},{16,12},{20,16},{24,20},{28,24},{0,28},{5,1},{9... | collective-permute-start | bytes 589832 | tf_op jit(solution)/shard_map/ppermute | solution.py:299
  67.2 9.0 %collective-permute-done.5.refs_3_ = f32[2,2,3,32,256]{4,3,2,1,0:T(8,128)} collective-permute-done((f32[2,2,3,32,256]{4,3,2,1,0:T(8,128)}, f32[2,2,3,32,256]{4,3,2,1,0:T(8,128)}, u32[]{:S(2)}, u32[]{:S(2)}) %collective-permute-start.5) | collective-permute-done | bytes 393248 | tf_op jit(solution)/shard_map/ppermute | solution.py:299
  76.2 0.0 collective-permute-done.4.refs_2_
  76.2 2.4 %edge_terms.2 = (f32[8,3,64,256]{3,2,1,0:T(8,128)}, f32[8,3,64,256]{3,2,1,0:T(8,128)}) custom-call(f32[5,3,64,256]{3,2,1,0:T(8,128)S(1)} %get-tuple-element.29.refs_0_, f32[5,3,64,256]{3,2,1,0:T(8,128)S(1)} %get-tuple-element.30.refs_1_, f32[2,4,3,32,256]{4,3,2,1,0:T(8,128)} %collective-permute-done.4.refs_2_, ...), custom_call_target="tpu_custom_call", output_to_operand_aliasing={{0}: (4, {}), {1}: (5, {})} | custom-call | flops 999999995904 | bytes 10000000000 | tf_op jit(solution)/shard_map/edge_terms/pallas_call | solution.py:463
  78.6 0.0 collective-permute-done.2.refs_2_
  78.7 1.6 %collective-permute-done.3.refs_3_ = f32[2,1,3,32,256]{4,3,2,1,0:T(8,128)} collective-permute-done((f32[2,1,3,32,256]{4,3,2,1,0:T(8,128)}, f32[2,1,3,32,256]{4,3,2,1,0:T(8,128)}, u32[]{:S(2)}, u32[]{:S(2)}) %collective-permute-start.3) | collective-permute-done | bytes 196640 | tf_op jit(solution)/shard_map/ppermute | solution.py:299
  80.3 1.8 %edge_terms.3 = (f32[8,3,64,256]{3,2,1,0:T(8,128)}, f32[8,3,64,256]{3,2,1,0:T(8,128)}) custom-call(f32[5,3,64,256]{3,2,1,0:T(8,128)S(1)} %get-tuple-element.29.refs_0_, f32[5,3,64,256]{3,2,1,0:T(8,128)S(1)} %get-tuple-element.30.refs_1_, f32[2,1,3,32,256]{4,3,2,1,0:T(8,128)} %collective-permute-done.2.refs_2_, ...), custom_call_target="tpu_custom_call", output_to_operand_aliasing={{0}: (4, {}), {1}: (5, {})} | custom-call | flops 1000 | bytes 1000 | tf_op jit(solution)/shard_map/edge_terms/pallas_call | solution.py:463
  (21 shorter events, 0.1 us)
Async XLA Ops:
  0.6 4.2 %copy-start.6 = (s32[1024]{0:T(1024)S(1)}, s32[1024]{0:T(1024)}, u32[]{:S(2)}) copy-start(s32[1024]{0:T(1024)} %param.18) | copy-start | bytes 12292
  0.6 4.2 %copy-start.4 = (s32[1024]{0:T(1024)S(1)}, s32[1024]{0:T(1024)}, u32[]{:S(2)}) copy-start(s32[1024]{0:T(1024)} %param.17) | copy-start | bytes 12292
  1.8 19.6 %collective-permute-start.1 = (f32[2,3,3,32,256]{4,3,2,1,0:T(8,128)S(1)}, f32[2,3,3,32,256]{4,3,2,1,0:T(8,128)S(1)}, u32[]{:S(2)}, u32[]{:S(2)}) collective-permute-start(f32[2,3,3,32,256]{4,3,2,1,0:T(8,128)S(1)} %pad_maximum_fusion), channel_id=1, source_target_pairs={{0,4},{4,8},{8,12},{12,16},{16,20},{20,24},{24,28},{28,0},{1,5},{5... | collective-permute-start | bytes 1769480 | tf_op jit(solution)/shard_map/ppermute | solution.py:298
  11.5 13.4 %all-to-all-start = ((f32[8,6,8,128]{3,2,1,0:T(8,128)}), f32[8,6,8,128]{3,2,1,0:T(8,128)}, u32[]{:S(2)}, u32[]{:S(2)}) async-start(f32[8,6,8,128]{3,2,1,0:T(8,128)} %get-tuple-element.28), calls=%async_computation | async-start | bytes 393216 | tf_op jit(solution)/shard_map/all_to_all | solution.py:362
  16.4 29.3 %collective-permute-start = (f32[2,5,3,32,256]{4,3,2,1,0:T(8,128)}, f32[2,5,3,32,256]{4,3,2,1,0:T(8,128)}, u32[]{:S(2)}, u32[]{:S(2)}) collective-permute-start(f32[2,5,3,32,256]{4,3,2,1,0:T(8,128)} %get-tuple-element.27), channel_id=1, source_target_pairs={{4,0},{8,4},{12,8},{16,12},{20,16},{24,20},{28,24},{0,28},{5,1},{9... | collective-permute-start | bytes 2949128 | tf_op jit(solution)/shard_map/ppermute | solution.py:299
  21.4 0.8 copy-start
  22.3 2.6 %copy-start.8 = (s32[16,256]{1,0:T(8,128)S(1)}, s32[16,256]{1,0:T(8,128)}, u32[]{:S(2)}) copy-start(s32[16,256]{1,0:T(8,128)} %status_ref.1) | copy-start | bytes 49156
  22.3 2.6 %copy-start.9 = (s32[2,256]{1,0:T(2,128)S(1)}, s32[2,256]{1,0:T(2,128)}, u32[]{:S(2)}) copy-start(s32[2,256]{1,0:T(2,128)} %pairs_ref.3) | copy-start | bytes 6148
  22.3 9.9 %copy-start.10 = (f32[256]{0:T(256)S(1)}, f32[256]{0:T(256)}, u32[]{:S(2)}) copy-start(f32[256]{0:T(256)} %param.21) | copy-start | bytes 3076
  22.3 9.9 %copy-start.11 = (f32[64,32]{1,0:T(8,128)S(1)}, f32[64,32]{1,0:T(8,128)}, u32[]{:S(2)}) copy-start(f32[64,32]{1,0:T(8,128)} %constant.8.clone.table_ref) | copy-start | bytes 24580
  22.3 9.9 %copy-start.12 = (f32[4,8,64]{2,1,0:T(8,128)S(1)}, f32[4,8,64]{2,1,0:T(8,128)}, u32[]{:S(2)}) copy-start(f32[4,8,64]{2,1,0:T(8,128)} %constant.9.clone.back_ref) | copy-start | bytes 24580
  34.9 15.7 %all-to-all-start.1 = ((f32[8,6,8,128]{3,2,1,0:T(8,128)}), f32[8,6,8,128]{3,2,1,0:T(8,128)}, u32[]{:S(2)}, u32[]{:S(2)}) async-start(f32[8,6,8,128]{3,2,1,0:T(8,128)} %pair_force.1), calls=%async_computation.1 | async-start | bytes 393216 | tf_op jit(solution)/shard_map/all_to_all | solution.py:362
  39.0 37.2 %collective-permute-start.5 = (f32[2,2,3,32,256]{4,3,2,1,0:T(8,128)}, f32[2,2,3,32,256]{4,3,2,1,0:T(8,128)}, u32[]{:S(2)}, u32[]{:S(2)}) collective-permute-start(f32[2,2,3,32,256]{4,3,2,1,0:T(8,128)} %get-tuple-element.41), channel_id=1, source_target_pairs={{4,0},{8,4},{12,8},{16,12},{20,16},{24,20},{28,24},{0,28},{5,1},{9... | collective-permute-start | bytes 1179656 | tf_op jit(solution)/shard_map/ppermute | solution.py:299
  43.6 32.6 %collective-permute-start.4 = (f32[2,4,3,32,256]{4,3,2,1,0:T(8,128)}, f32[2,4,3,32,256]{4,3,2,1,0:T(8,128)}, u32[]{:S(2)}, u32[]{:S(2)}) collective-permute-start(f32[2,4,3,32,256]{4,3,2,1,0:T(8,128)} %get-tuple-element.40), channel_id=1, source_target_pairs={{0,4},{4,8},{8,12},{12,16},{16,20},{20,24},{24,28},{28,0},{1,5},{5... | collective-permute-start | bytes 2359304 | tf_op jit(solution)/shard_map/ppermute | solution.py:298
  45.6 5.0 %copy-start.1 = (f32[2,3,3,32,256]{4,3,2,1,0:T(8,128)S(1)}, f32[2,3,3,32,256]{4,3,2,1,0:T(8,128)}, u32[]{:S(2)}) copy-start(f32[2,3,3,32,256]{4,3,2,1,0:T(8,128)} %copy-done) | copy-start | bytes 1769476
  45.6 5.0 %copy-start.2 = (f32[2,32,256]{2,1,0:T(8,128)S(1)}, f32[2,32,256]{2,1,0:T(8,128)}, u32[]{:S(2)}) copy-start(f32[2,32,256]{2,1,0:T(8,128)} %param.15) | copy-start | bytes 196612
  45.6 5.0 %copy-start.3 = (f32[2,32,256]{2,1,0:T(8,128)S(1)}, f32[2,32,256]{2,1,0:T(8,128)}, u32[]{:S(2)}) copy-start(f32[2,32,256]{2,1,0:T(8,128)} %param.16) | copy-start | bytes 196612
  45.6 5.0 %copy-start.5 = (s32[1024]{0:T(1024)S(1)}, s32[1024]{0:T(1024)}, u32[]{:S(2)}) copy-start(s32[1024]{0:T(1024)} %param.17) | copy-start | bytes 12292
  45.7 5.0 %copy-start.7 = (s32[1024]{0:T(1024)S(1)}, s32[1024]{0:T(1024)}, u32[]{:S(2)}) copy-start(s32[1024]{0:T(1024)} %param.18) | copy-start | bytes 12292
  58.8 19.9 %collective-permute-start.2 = (f32[2,1,3,32,256]{4,3,2,1,0:T(8,128)}, f32[2,1,3,32,256]{4,3,2,1,0:T(8,128)}, u32[]{:S(2)}, u32[]{:S(2)}) collective-permute-start(f32[2,1,3,32,256]{4,3,2,1,0:T(8,128)} %get-tuple-element.38), channel_id=1, source_target_pairs={{0,4},{4,8},{8,12},{12,16},{16,20},{20,24},{24,28},{28,0},{1,5},{5... | collective-permute-start | bytes 589832 | tf_op jit(solution)/shard_map/ppermute | solution.py:298
  59.8 20.5 %collective-permute-start.3 = (f32[2,1,3,32,256]{4,3,2,1,0:T(8,128)}, f32[2,1,3,32,256]{4,3,2,1,0:T(8,128)}, u32[]{:S(2)}, u32[]{:S(2)}) collective-permute-start(f32[2,1,3,32,256]{4,3,2,1,0:T(8,128)} %get-tuple-element.39), channel_id=1, source_target_pairs={{4,0},{8,4},{12,8},{16,12},{20,16},{24,20},{28,24},{0,28},{5,1},{9... | collective-permute-start | bytes 589832 | tf_op jit(solution)/shard_map/ppermute | solution.py:299

commit v5 on v4

--- a/solution.py
+++ b/solution.py
@@ -17,7 +17,7 @@
 shear_penalty = 1.0
 
 CUTS = ((3, 0), (3, 5), (7, 7), (8, 8))
-VMEM = 28 * 1024 * 1024
+VMEM = 20 * 1024 * 1024
 
 
 def split2(value):

time: 82.6 us -> 82.6 us (level)
  no operation moved by 1% of the time
where the time goes in v5:
time: 82.6 us; the launch traced here: 82.1 us
  starting transfers between devices  29.7 us (36%)
  Pallas kernels  23.3 us (28%)
  waiting for transfers between devices  20.5 us (25%)
  blocking collectives  5.79 us (7%)
  local copies, waits for them, and re-layouts  1.97 us (2%)
    ppermute x3, starting transfers between devices, on_device(): behind = lambda piece: lax.ppermute(piece, 'mesh', backward)  16.8 us
    ppermute x3, waiting for transfers between devices, on_device(): behind = lambda piece: lax.ppermute(piece, 'mesh', backward)  12.7 us
    all_to_all x2, starting transfers between devices, exchange(): lax.all_to_all(block, 'mesh', split_axis=0, concat_axis=0, tiled=True)  8.89 us
    pallas_call x1, Pallas kernels, on_device(): pl.pallas_call(lambda *refs: combine_kernel(*refs, edges=early, late=late...  8.14 us
    all_to_all x2, waiting for transfers between devices, exchange(): lax.all_to_all(block, 'mesh', split_axis=0, concat_axis=0, tiled=True)  7.5 us
    pallas_call x1, Pallas kernels, on_device(): pl.pallas_call(lambda *refs: gather_kernel(*refs, edges=edges), grid=(com...  6.65 us
    all_gather x1, blocking collectives, on_device(): everything = lax.all_gather(own_opening, 'harm')  5.79 us
    pallas_call x2, Pallas kernels, on_device(): pl.pallas_call(lambda *refs, starts=starts: edge_kernel(*refs, late=late,...  4.25 us
  transfers between devices with their start and end apart: 8, of which 6 were waited for; matrix products, arithmetic and copies ran while one was open for 0% of the time, Pallas kernels for 26%

profile of v5, /device:TPU:0, one launch (start us, length us, event | category | flops | bytes accessed | tf_op | source)
XLA Modules:
  0.0 82.1 jit_solution(8297769563235980589)
XLA Ops:
  0.6 0.0 copy-start.6
  0.6 0.0 copy-start.4
  0.7 1.1 %slice_bitcast_fusion = (f32[1,3,3,32,256]{4,3,2,1,0:T(8,128)S(1)}, f32[1,3,3,32,256]{4,3,2,1,0:T(8,128)S(1)}) fusion(f32[8,3,2,32,256]{4,3,2,1,0:T(8,128)} %param.13, f32[8,3,2,32,256]{4,3,2,1,0:T(8,128)} %param.12), kind=kLoop, calls=%fused_computation.1 | loop fusion | bytes 1179648 | tf_op jit(solution)/shard_map/stack;squeeze | solution.py:318
  1.8 3.0 %collective-permute-start.1 = (f32[2,3,3,32,256]{4,3,2,1,0:T(8,128)S(1)}, f32[2,3,3,32,256]{4,3,2,1,0:T(8,128)S(1)}, u32[]{:S(2)}, u32[]{:S(2)}) collective-permute-start(f32[2,3,3,32,256]{4,3,2,1,0:T(8,128)S(1)} %pad_maximum_fusion), channel_id=1, source_target_pairs={{0,4},{4,8},{8,12},{12,16},{16,20},{20,24},{24,28},{28,0},{1,5},{5... | collective-permute-start | bytes 1769480 | tf_op jit(solution)/shard_map/ppermute | solution.py:298
  4.8 0.0 copy-done.6
  4.8 0.0 copy-done.4
  4.8 6.6 %face_gather.1 = (f32[8,6,8,128]{3,2,1,0:T(8,128)}, f32[2,5,3,32,256]{4,3,2,1,0:T(8,128)}, f32[2,4,3,32,256]{4,3,2,1,0:T(8,128)}, f32[2,2,3,32,256]{4,3,2,1,0:T(...) custom-call(s32[8,128]{1,0:T(8,128)S(1)} %bitcast.23, s32[8,128]{1,0:T(8,128)S(1)} %bitcast.25, ...), custom_call_target="tpu_custom_call" | custom-call | flops 1000 | bytes 1000 | tf_op jit(solution)/shard_map/face_gather/pallas_call | solution.py:340
  11.5 4.9 %all-to-all-start = ((f32[8,6,8,128]{3,2,1,0:T(8,128)}), f32[8,6,8,128]{3,2,1,0:T(8,128)}, u32[]{:S(2)}, u32[]{:S(2)}) async-start(f32[8,6,8,128]{3,2,1,0:T(8,128)} %get-tuple-element.28), calls=%async_computation | async-start | bytes 393216 | tf_op jit(solution)/shard_map/all_to_all | solution.py:362
  16.4 4.7 %collective-permute-start = (f32[2,5,3,32,256]{4,3,2,1,0:T(8,128)}, f32[2,5,3,32,256]{4,3,2,1,0:T(8,128)}, u32[]{:S(2)}, u32[]{:S(2)}) collective-permute-start(f32[2,5,3,32,256]{4,3,2,1,0:T(8,128)} %get-tuple-element.27), channel_id=1, source_target_pairs={{4,0},{8,4},{12,8},{16,12},{20,16},{24,20},{28,24},{0,28},{5,1},{9... | collective-permute-start | bytes 2949128 | tf_op jit(solution)/shard_map/ppermute | solution.py:299
  21.1 0.4 collective-permute-done.1.piece_ref.refs_5_
  21.5 0.8 copy-done
  22.3 0.0 copy-start.12
  22.3 2.6 %all-to-all-done.arrived_ref = f32[8,6,8,128]{3,2,1,0:T(8,128)} async-done(((f32[8,6,8,128]{3,2,1,0:T(8,128)}), f32[8,6,8,128]{3,2,1,0:T(8,128)}, u32[]{:S(2)}, u32[]{:S(2)}) %all-to-all-start) | async-done | bytes 196640 | tf_op jit(solution)/shard_map/all_to_all | solution.py:362
  24.9 1.4 %pair_difference.1 = f32[64,256]{1,0:T(8,128)S(1)} custom-call(s32[2,256]{1,0:T(2,128)S(1)} %copy-done.9, s32[16,256]{1,0:T(8,128)S(1)} %copy-done.8, f32[8,128]{1,0:T(8,128)S(1)} %piece_arrived.3.mark_ref, f32[8,6,8,128]{3,2,1,0:T(8,128)} %all-to-all-done.arrived_ref), custom_call_target="tpu_custom_call" | custom-call | flops 1000 | bytes 1000 | tf_op jit(solution)/shard_map/pair_difference/pallas_call | solution.py:386
  26.3 5.8 %all-gather = f32[256,256]{1,0:T(8,128)S(1)} all-gather(f32[64,256]{1,0:T(8,128)S(1)} %pair_difference.1), channel_id=2, replica_groups=mesh['mesh'=8,'harm'=4] {'harm'}, dimensions={0}, use_global_device_ids=true | all-gather | bytes 327680 | tf_op jit(solution)/shard_map/all_gather | solution.py:395
  32.1 2.8 %pair_force.1 = f32[8,6,8,128]{3,2,1,0:T(8,128)} custom-call(s32[1]{0:T(128)} %bitcast.4.place_ref.refs_1_, s32[2,256]{1,0:T(2,128)S(1)} %copy-done.9, f32[1,256]{1,0:T(1,128)S(1)} %bitcast.27, f32[64,32]{1,0:T(8,128)S(1)} %copy-done.11, f32[4,8,64]{2,1,0:T(8,128)S(1)} %copy-done.12, f32[4,64,256]{2,1,0:T(8,128)S(1)} %bitcast.20), custom_call_target="tpu_custom_call" | custom-call | flops 999999995904 | bytes 10000000000 | tf_op jit(solution)/shard_map/pair_force/pallas_call | solution.py:398
  34.9 4.0 %all-to-all-start.1 = ((f32[8,6,8,128]{3,2,1,0:T(8,128)}), f32[8,6,8,128]{3,2,1,0:T(8,128)}, u32[]{:S(2)}, u32[]{:S(2)}) async-start(f32[8,6,8,128]{3,2,1,0:T(8,128)} %pair_force.1), calls=%async_computation.1 | async-start | bytes 393216 | tf_op jit(solution)/shard_map/all_to_all | solution.py:362
  39.0 4.6 %collective-permute-start.5 = (f32[2,2,3,32,256]{4,3,2,1,0:T(8,128)}, f32[2,2,3,32,256]{4,3,2,1,0:T(8,128)}, u32[]{:S(2)}, u32[]{:S(2)}) collective-permute-start(f32[2,2,3,32,256]{4,3,2,1,0:T(8,128)} %get-tuple-element.41), channel_id=1, source_target_pairs={{4,0},{8,4},{12,8},{16,12},{20,16},{24,20},{28,24},{0,28},{5,1},{9... | collective-permute-start | bytes 1179656 | tf_op jit(solution)/shard_map/ppermute | solution.py:299
  43.6 0.0 collective-permute-start.4
  43.6 2.1 %collective-permute-done.piece_ref.refs_6_ = f32[2,5,3,32,256]{4,3,2,1,0:T(8,128)} collective-permute-done((f32[2,5,3,32,256]{4,3,2,1,0:T(8,128)}, f32[2,5,3,32,256]{4,3,2,1,0:T(8,128)}, u32[]{:S(2)}, u32[]{:S(2)}) %collective-permute-start) | collective-permute-done | bytes 983072 | tf_op jit(solution)/shard_map/ppermute | solution.py:299
  45.7 0.0 copy-start.7
  45.7 4.9 %all-to-all-done.1.refs_4_ = f32[8,6,8,128]{3,2,1,0:T(8,128)} async-done(((f32[8,6,8,128]{3,2,1,0:T(8,128)}), f32[8,6,8,128]{3,2,1,0:T(8,128)}, u32[]{:S(2)}, u32[]{:S(2)}) %all-to-all-start.1) | async-done | bytes 196640 | tf_op jit(solution)/shard_map/all_to_all | solution.py:362
  50.6 0.0 copy-done.1
  50.6 8.1 %combine_terms.1 = (f32[8,3,64,256]{3,2,1,0:T(8,128)}, f32[8,3,64,256]{3,2,1,0:T(8,128)}, f32[5,3,64,256]{3,2,1,0:T(8,128)S(1)}, f32[5,3,64,256]{3,2,1,0:T(8,128)S(1)}) custom-call(f32[8,128]{1,0:T(8,128)S(1)} %piece_arrived.2.refs_0_, s32[1]{0:T(128)} %bitcast.4.place_ref.refs_1_, s32[8,128]{1,0:T(8,128)S(1)} %bitcast.24, s32[8,128]{1,0:T(8,128)S(1)} %bitcast.26, ...), custom_call_target="tpu_custom_call" | custom-call | flops 1000 | bytes 1000 | tf_op jit(solution)/shard_map/combine_terms/pallas_call | solution.py:426
  58.8 1.0 %collective-permute-start.2 = (f32[2,1,3,32,256]{4,3,2,1,0:T(8,128)}, f32[2,1,3,32,256]{4,3,2,1,0:T(8,128)}, u32[]{:S(2)}, u32[]{:S(2)}) collective-permute-start(f32[2,1,3,32,256]{4,3,2,1,0:T(8,128)} %get-tuple-element.38), channel_id=1, source_target_pairs={{0,4},{4,8},{8,12},{12,16},{16,20},{20,24},{24,28},{28,0},{1,5},{5... | collective-permute-start | bytes 589832 | tf_op jit(solution)/shard_map/ppermute | solution.py:298
  59.8 7.4 %collective-permute-start.3 = (f32[2,1,3,32,256]{4,3,2,1,0:T(8,128)}, f32[2,1,3,32,256]{4,3,2,1,0:T(8,128)}, u32[]{:S(2)}, u32[]{:S(2)}) collective-permute-start(f32[2,1,3,32,256]{4,3,2,1,0:T(8,128)} %get-tuple-element.39), channel_id=1, source_target_pairs={{4,0},{8,4},{12,8},{16,12},{20,16},{24,20},{28,24},{0,28},{5,1},{9... | collective-permute-start | bytes 589832 | tf_op jit(solution)/shard_map/ppermute | solution.py:299
  67.2 9.0 %collective-permute-done.5.refs_3_ = f32[2,2,3,32,256]{4,3,2,1,0:T(8,128)} collective-permute-done((f32[2,2,3,32,256]{4,3,2,1,0:T(8,128)}, f32[2,2,3,32,256]{4,3,2,1,0:T(8,128)}, u32[]{:S(2)}, u32[]{:S(2)}) %collective-permute-start.5) | collective-permute-done | bytes 393248 | tf_op jit(solution)/shard_map/ppermute | solution.py:299
  76.2 0.0 collective-permute-done.4.refs_2_
  76.2 2.4 %edge_terms.2 = (f32[8,3,64,256]{3,2,1,0:T(8,128)}, f32[8,3,64,256]{3,2,1,0:T(8,128)}) custom-call(f32[5,3,64,256]{3,2,1,0:T(8,128)S(1)} %get-tuple-element.29.refs_0_, f32[5,3,64,256]{3,2,1,0:T(8,128)S(1)} %get-tuple-element.30.refs_1_, f32[2,4,3,32,256]{4,3,2,1,0:T(8,128)} %collective-permute-done.4.refs_2_, ...), custom_call_target="tpu_custom_call", output_to_operand_aliasing={{0}: (4, {}), {1}: (5, {})} | custom-call | flops 999999995904 | bytes 10000000000 | tf_op jit(solution)/shard_map/edge_terms/pallas_call | solution.py:463
  78.6 0.0 collective-permute-done.2.refs_2_
  78.7 1.6 %collective-permute-done.3.refs_3_ = f32[2,1,3,32,256]{4,3,2,1,0:T(8,128)} collective-permute-done((f32[2,1,3,32,256]{4,3,2,1,0:T(8,128)}, f32[2,1,3,32,256]{4,3,2,1,0:T(8,128)}, u32[]{:S(2)}, u32[]{:S(2)}) %collective-permute-start.3) | collective-permute-done | bytes 196640 | tf_op jit(solution)/shard_map/ppermute | solution.py:299
  80.3 1.8 %edge_terms.3 = (f32[8,3,64,256]{3,2,1,0:T(8,128)}, f32[8,3,64,256]{3,2,1,0:T(8,128)}) custom-call(f32[5,3,64,256]{3,2,1,0:T(8,128)S(1)} %get-tuple-element.29.refs_0_, f32[5,3,64,256]{3,2,1,0:T(8,128)S(1)} %get-tuple-element.30.refs_1_, f32[2,1,3,32,256]{4,3,2,1,0:T(8,128)} %collective-permute-done.2.refs_2_, ...), custom_call_target="tpu_custom_call", output_to_operand_aliasing={{0}: (4, {}), {1}: (5, {})} | custom-call | flops 1000 | bytes 1000 | tf_op jit(solution)/shard_map/edge_terms/pallas_call | solution.py:463
  (21 shorter events, 0.1 us)
Async XLA Ops:
  0.6 4.2 %copy-start.6 = (s32[1024]{0:T(1024)S(1)}, s32[1024]{0:T(1024)}, u32[]{:S(2)}) copy-start(s32[1024]{0:T(1024)} %param.18) | copy-start | bytes 12292
  0.6 4.2 %copy-start.4 = (s32[1024]{0:T(1024)S(1)}, s32[1024]{0:T(1024)}, u32[]{:S(2)}) copy-start(s32[1024]{0:T(1024)} %param.17) | copy-start | bytes 12292
  1.8 19.6 %collective-permute-start.1 = (f32[2,3,3,32,256]{4,3,2,1,0:T(8,128)S(1)}, f32[2,3,3,32,256]{4,3,2,1,0:T(8,128)S(1)}, u32[]{:S(2)}, u32[]{:S(2)}) collective-permute-start(f32[2,3,3,32,256]{4,3,2,1,0:T(8,128)S(1)} %pad_maximum_fusion), channel_id=1, source_target_pairs={{0,4},{4,8},{8,12},{12,16},{16,20},{20,24},{24,28},{28,0},{1,5},{5... | collective-permute-start | bytes 1769480 | tf_op jit(solution)/shard_map/ppermute | solution.py:298
  11.5 13.4 %all-to-all-start = ((f32[8,6,8,128]{3,2,1,0:T(8,128)}), f32[8,6,8,128]{3,2,1,0:T(8,128)}, u32[]{:S(2)}, u32[]{:S(2)}) async-start(f32[8,6,8,128]{3,2,1,0:T(8,128)} %get-tuple-element.28), calls=%async_computation | async-start | bytes 393216 | tf_op jit(solution)/shard_map/all_to_all | solution.py:362
  16.4 29.3 %collective-permute-start = (f32[2,5,3,32,256]{4,3,2,1,0:T(8,128)}, f32[2,5,3,32,256]{4,3,2,1,0:T(8,128)}, u32[]{:S(2)}, u32[]{:S(2)}) collective-permute-start(f32[2,5,3,32,256]{4,3,2,1,0:T(8,128)} %get-tuple-element.27), channel_id=1, source_target_pairs={{4,0},{8,4},{12,8},{16,12},{20,16},{24,20},{28,24},{0,28},{5,1},{9... | collective-permute-start | bytes 2949128 | tf_op jit(solution)/shard_map/ppermute | solution.py:299
  21.4 0.8 copy-start
  22.3 2.6 %copy-start.8 = (s32[16,256]{1,0:T(8,128)S(1)}, s32[16,256]{1,0:T(8,128)}, u32[]{:S(2)}) copy-start(s32[16,256]{1,0:T(8,128)} %status_ref.1) | copy-start | bytes 49156
  22.3 2.6 %copy-start.9 = (s32[2,256]{1,0:T(2,128)S(1)}, s32[2,256]{1,0:T(2,128)}, u32[]{:S(2)}) copy-start(s32[2,256]{1,0:T(2,128)} %pairs_ref.3) | copy-start | bytes 6148
  22.3 9.9 %copy-start.10 = (f32[256]{0:T(256)S(1)}, f32[256]{0:T(256)}, u32[]{:S(2)}) copy-start(f32[256]{0:T(256)} %param.21) | copy-start | bytes 3076
  22.3 9.9 %copy-start.11 = (f32[64,32]{1,0:T(8,128)S(1)}, f32[64,32]{1,0:T(8,128)}, u32[]{:S(2)}) copy-start(f32[64,32]{1,0:T(8,128)} %constant.8.clone.table_ref) | copy-start | bytes 24580
  22.3 9.9 %copy-start.12 = (f32[4,8,64]{2,1,0:T(8,128)S(1)}, f32[4,8,64]{2,1,0:T(8,128)}, u32[]{:S(2)}) copy-start(f32[4,8,64]{2,1,0:T(8,128)} %constant.9.clone.back_ref) | copy-start | bytes 24580
  34.9 15.7 %all-to-all-start.1 = ((f32[8,6,8,128]{3,2,1,0:T(8,128)}), f32[8,6,8,128]{3,2,1,0:T(8,128)}, u32[]{:S(2)}, u32[]{:S(2)}) async-start(f32[8,6,8,128]{3,2,1,0:T(8,128)} %pair_force.1), calls=%async_computation.1 | async-start | bytes 393216 | tf_op jit(solution)/shard_map/all_to_all | solution.py:362
  39.0 37.2 %collective-permute-start.5 = (f32[2,2,3,32,256]{4,3,2,1,0:T(8,128)}, f32[2,2,3,32,256]{4,3,2,1,0:T(8,128)}, u32[]{:S(2)}, u32[]{:S(2)}) collective-permute-start(f32[2,2,3,32,256]{4,3,2,1,0:T(8,128)} %get-tuple-element.41), channel_id=1, source_target_pairs={{4,0},{8,4},{12,8},{16,12},{20,16},{24,20},{28,24},{0,28},{5,1},{9... | collective-permute-start | bytes 1179656 | tf_op jit(solution)/shard_map/ppermute | solution.py:299
  43.6 32.6 %collective-permute-start.4 = (f32[2,4,3,32,256]{4,3,2,1,0:T(8,128)}, f32[2,4,3,32,256]{4,3,2,1,0:T(8,128)}, u32[]{:S(2)}, u32[]{:S(2)}) collective-permute-start(f32[2,4,3,32,256]{4,3,2,1,0:T(8,128)} %get-tuple-element.40), channel_id=1, source_target_pairs={{0,4},{4,8},{8,12},{12,16},{16,20},{20,24},{24,28},{28,0},{1,5},{5... | collective-permute-start | bytes 2359304 | tf_op jit(solution)/shard_map/ppermute | solution.py:298
  45.6 5.0 %copy-start.1 = (f32[2,3,3,32,256]{4,3,2,1,0:T(8,128)S(1)}, f32[2,3,3,32,256]{4,3,2,1,0:T(8,128)}, u32[]{:S(2)}) copy-start(f32[2,3,3,32,256]{4,3,2,1,0:T(8,128)} %copy-done) | copy-start | bytes 1769476
  45.6 5.0 %copy-start.2 = (f32[2,32,256]{2,1,0:T(8,128)S(1)}, f32[2,32,256]{2,1,0:T(8,128)}, u32[]{:S(2)}) copy-start(f32[2,32,256]{2,1,0:T(8,128)} %param.15) | copy-start | bytes 196612
  45.6 5.0 %copy-start.3 = (f32[2,32,256]{2,1,0:T(8,128)S(1)}, f32[2,32,256]{2,1,0:T(8,128)}, u32[]{:S(2)}) copy-start(f32[2,32,256]{2,1,0:T(8,128)} %param.16) | copy-start | bytes 196612
  45.6 5.0 %copy-start.5 = (s32[1024]{0:T(1024)S(1)}, s32[1024]{0:T(1024)}, u32[]{:S(2)}) copy-start(s32[1024]{0:T(1024)} %param.17) | copy-start | bytes 12292
  45.7 5.0 %copy-start.7 = (s32[1024]{0:T(1024)S(1)}, s32[1024]{0:T(1024)}, u32[]{:S(2)}) copy-start(s32[1024]{0:T(1024)} %param.18) | copy-start | bytes 12292
  58.8 19.9 %collective-permute-start.2 = (f32[2,1,3,32,256]{4,3,2,1,0:T(8,128)}, f32[2,1,3,32,256]{4,3,2,1,0:T(8,128)}, u32[]{:S(2)}, u32[]{:S(2)}) collective-permute-start(f32[2,1,3,32,256]{4,3,2,1,0:T(8,128)} %get-tuple-element.38), channel_id=1, source_target_pairs={{0,4},{4,8},{8,12},{12,16},{16,20},{20,24},{24,28},{28,0},{1,5},{5... | collective-permute-start | bytes 589832 | tf_op jit(solution)/shard_map/ppermute | solution.py:298
  59.8 20.5 %collective-permute-start.3 = (f32[2,1,3,32,256]{4,3,2,1,0:T(8,128)}, f32[2,1,3,32,256]{4,3,2,1,0:T(8,128)}, u32[]{:S(2)}, u32[]{:S(2)}) collective-permute-start(f32[2,1,3,32,256]{4,3,2,1,0:T(8,128)} %get-tuple-element.39), channel_id=1, source_target_pairs={{4,0},{8,4},{12,8},{16,12},{20,16},{24,20},{28,24},{0,28},{5,1},{9... | collective-permute-start | bytes 589832 | tf_op jit(solution)/shard_map/ppermute | solution.py:299
